TPU v7x, 512 devices: a whole 4x4x16 slice. The times are simulated.
512 devices in a mesh: dom: 128 (over y, z, core), sub: 4 (over x).
Axes of the slice: x: 4, y: 4, z: 16, core: 2. Of those that a mesh axis runs over, the one named last changes fastest.
Arguments:
- segments: float32 [1024, 9, 128], P(('dom', 'sub')), may hold values from -6 to 6
- stress: float32 [3, 3], replicated, may hold values from -3 to 3
- drag_coef: float32 [1024, 128], P(('dom', 'sub')), may hold values from 0.5 to 4
- send_ids: int32 [512, 128, 1], P(('dom', 'sub')), may hold values from -1 to 1, as said below
- partner_ids: int32 [512, 128, 1], P(('dom', 'sub')), may hold values from 0 to 1
Outputs:
- positions: float32 [1024, 3, 128], P(('dom', 'sub'))
- velocity: float32 [1024, 3, 128], P(('dom', 'sub'))
Inputs may be any that keep to these rules, and one draw needn't show every extreme that they name: `send_ids`: entry [d, p, s] names a block of device d, which goes in slot s to the device with dom index p and d's sub index; -1 marks an empty slot. Some device receives a block in every slot from every sender.
All inputs are finite; a program needn't handle non-finite values.
Results may differ from a plain program's by a relative error of at most 0.0003.
Values sent between devices are 32-bit elements; how exact they have to be, the bound alone decides.
No kernel may reach another device: no remote copies, remote signals or barrier semaphores. Data moves between devices by JAX's collectives and lax.ppermute only.
A program may use at most 64 MiB of HBM per device.

v0:
```python
import math

import jax
import jax.numpy as jnp
from jax import lax
from jax.sharding import Mesh
from jax.sharding import PartitionSpec as P

STEPS = 2
DOM = ("dom_0", "dom_1", "dom_2")
DOM_SUB = ("dom_0", "dom_1", "dom_2", "sub")


COUPLE = 0.0625
CORE_SQUARE = 0.5
TENSION = 0.25
STEP_LENGTH = 1.0
EPSILON = 1e-06


def one_axis_at_a_time(array, axes):
    for axis in axes:
        array = lax.pmax(array, axis)
    return array


def pair_terms(target, source):
    offsets = [
        target[..., component, :][..., :, None] - source[..., component, :][..., None, :]
        for component in range(3)
    ]
    distance_sq = (
        CORE_SQUARE + offsets[0] * offsets[0] + offsets[1] * offsets[1] + offsets[2] * offsets[2]
    )
    inverse = lax.rsqrt(distance_sq)
    burgers_dot = target[..., 6, :][..., :, None] * source[..., 6, :][..., None, :]
    burgers_dot = burgers_dot + target[..., 7, :][..., :, None] * source[..., 7, :][..., None, :]
    burgers_dot = burgers_dot + target[..., 8, :][..., :, None] * source[..., 8, :][..., None, :]
    lines_dot = target[..., 3, :][..., :, None] * source[..., 3, :][..., None, :]
    lines_dot = lines_dot + target[..., 4, :][..., :, None] * source[..., 4, :][..., None, :]
    lines_dot = lines_dot + target[..., 5, :][..., :, None] * source[..., 5, :][..., None, :]
    weights = burgers_dot * lines_dot * inverse * inverse * inverse
    return (weights, offsets)


def force_on_target(weights, offsets):
    return jnp.stack([jnp.sum(weights * offset_c, axis=-1) for offset_c in offsets], axis=-2)


def force_on_source(weights, offsets):
    return jnp.stack([-jnp.sum(weights * offset_c, axis=-2) for offset_c in offsets], axis=-2)


def external_force(stress, line_vec, burgers):
    pulled = [
        stress[component, 0] * burgers[:, 0]
        + stress[component, 1] * burgers[:, 1]
        + stress[component, 2] * burgers[:, 2]
        for component in range(3)
    ]
    first = pulled[1] * line_vec[:, 2] - pulled[2] * line_vec[:, 1]
    second = pulled[2] * line_vec[:, 0] - pulled[0] * line_vec[:, 2]
    third = pulled[0] * line_vec[:, 1] - pulled[1] * line_vec[:, 0]
    return jnp.stack([first, second, third], axis=1)


def chain_term(position):
    left_side = jnp.concatenate([position[..., :1], position[..., :-1]], axis=-1)
    right_side = jnp.concatenate([position[..., 1:], position[..., -1:]], axis=-1)
    return left_side + right_side - 2.0 * position


def group_forces(seg_state):
    block_count = seg_state.shape[0]
    seg_width = seg_state.shape[2]
    target = seg_state.transpose(1, 0, 2).reshape(9, block_count * seg_width)
    start_force = jnp.zeros((3, block_count * seg_width), jnp.float32)

    def add_block(accum_force, source):
        weights, offsets = pair_terms(target, source)
        return (accum_force + force_on_target(weights, offsets), None)

    running = lax.scan(
        add_block, start_force, lax.all_gather(seg_state, "sub", axis=0, tiled=True)
    )[0]
    return running.reshape(3, block_count, seg_width).transpose(1, 0, 2)


def both_sides(pieces):
    weights, offsets = pair_terms(pieces[0], pieces[1])
    return (force_on_target(weights, offsets), force_on_source(weights, offsets))


def cross_forces(
    seg_state,
    send_list,
    is_valid,
    partner_list,
    send_table,
    peer_count,
    slot_count,
    full_send,
    kept_rows,
):
    block_count = seg_state.shape[0]
    seg_width = seg_state.shape[2]
    payload = jnp.where(is_valid[:, None, None], seg_state[jnp.maximum(send_list, 0)], 0.0)
    payload = payload.reshape(peer_count, slot_count, 9, seg_width)
    outgoing = payload if full_send else payload[:, :, 0:3]
    arrived, arrived_partner = (
        lax.all_to_all(outgoing, DOM, split_axis=0, concat_axis=0, tiled=True),
        lax.all_to_all(partner_list, DOM, split_axis=0, concat_axis=0, tiled=True),
    )
    if not full_send:
        arrived = jnp.concatenate([arrived, kept_rows[0]], axis=2)
    remote = arrived.reshape(-1, 9, seg_width)
    local_ids = arrived_partner.reshape(-1)
    local_blocks = seg_state[local_ids]
    item_count = remote.shape[0]
    batch_size = math.gcd(item_count, 16)
    local_batched = local_blocks.reshape(-1, batch_size, 9, seg_width)
    remote_batched = remote.reshape(-1, batch_size, 9, seg_width)
    back_kept = kept_rows[1]
    on_local, on_remote = lax.map(both_sides, (local_batched, remote_batched))
    returned = lax.all_to_all(
        on_remote.reshape(peer_count, slot_count, 3, seg_width),
        DOM,
        split_axis=0,
        concat_axis=0,
        tiled=True,
    )
    block_range = jnp.arange(block_count, dtype=jnp.int32)
    local_table = (block_range[:, None] == local_ids[None, :]).astype(jnp.float32)
    add_local = jnp.einsum(
        "ni,icm->ncm",
        local_table,
        on_local.reshape(-1, 3, seg_width),
        precision=lax.Precision.HIGHEST,
    )
    add_sent = jnp.einsum(
        "ni,icm->ncm",
        send_table,
        returned.reshape(-1, 3, seg_width),
        precision=lax.Precision.HIGHEST,
    )
    return (add_local + add_sent, (arrived[:, :, 3:9], back_kept))


def local(segments, stress, drag_coef, send_ids, partner_ids):
    block_count = segments.shape[0]
    peer_count = send_ids.shape[1]
    slot_count = send_ids.shape[2]
    position = segments[:, 0:3]
    line_vec = segments[:, 3:6]
    burgers = segments[:, 6:9]
    applied = external_force(stress, line_vec, burgers)
    send_list = send_ids[0].reshape(-1)
    is_valid = send_list >= 0
    partner_list = partner_ids[0]
    block_range = jnp.arange(block_count, dtype=jnp.int32)
    send_table = (block_range[:, None] == send_list[None, :]).astype(jnp.float32)
    velocity = jnp.zeros_like(position)
    kept_rows = (None, None)
    for step_index in range(STEPS):
        full_send = step_index == 0
        seg_state = jnp.concatenate([position, line_vec, burgers], axis=1)
        grouped = group_forces(seg_state)
        crossed, kept_rows = cross_forces(
            seg_state,
            send_list,
            is_valid,
            partner_list,
            send_table,
            peer_count,
            slot_count,
            full_send,
            kept_rows,
        )
        force = COUPLE * (grouped + crossed) + applied + TENSION * chain_term(position)
        velocity = force / drag_coef[:, None, :]
        speed_sq = jnp.sum(velocity * velocity, axis=1)
        top_sq = one_axis_at_a_time(jnp.max(speed_sq), DOM_SUB)
        time_step = STEP_LENGTH / (jnp.sqrt(top_sq) + EPSILON)
        position = position + time_step * velocity
    return (position, velocity)


def solution(mesh):
    split = Mesh(
        mesh.devices.reshape(4, 16, 2, mesh.shape["sub"]), ("dom_0", "dom_1", "dom_2", "sub")
    )
    return jax.shard_map(
        local,
        mesh=split,
        in_specs=(
            P(DOM_SUB, None, None),
            P(),
            P(DOM_SUB, None),
            P(DOM_SUB, None, None),
            P(DOM_SUB, None, None),
        ),
        out_specs=(P(DOM_SUB, None, None), P(DOM_SUB, None, None)),
        check_vma=False,
    )
```

profile of v0, /device:TPU:1, one launch (start us, length us, event | category | flops | bytes accessed | tf_op | source)
XLA Modules:
  0.0 355.2 jit_solution(2715512862066963601)
XLA Ops:
  2.0 20.7 %all-to-all-start = ((s32[128,1,1]{2,1,0:T(1,128)}), s32[128,1,1]{2,1,0:T(1,128)S(1)}, u32[]{:S(2)}, u32[]{:S(2)}) async-start(s32[128,1,1]{2,1,0:T(1,128)} %copy.121), calls=%async_computation | async-start | bytes 131072 | tf_op jit(solution)/shard_map/all_to_all | solution.py:112
  24.5 10.2 %all_gather.6 = f32[8,9,128]{2,1,0:T(8,128)S(1)} all-gather(f32[2,9,128]{2,1,0:T(8,128)S(1)} %copy.120), channel_id=1, replica_groups=mesh['dom_0'=4,'dom_1'=16,'dom_2'=2,'sub'=4] {'sub'}, dimensions={0}, use_global_device_ids=true | all-gather | bytes 46080 | tf_op jit(solution)/shard_map/all_gather | solution.py:84
  37.7 16.6 %all-to-all-start.1 = ((f32[128,1,9,128]{3,1,2,0:T(1,128)}), f32[128,1,9,128]{3,1,2,0:T(1,128)S(1)}, u32[]{:S(2)}, u32[]{:S(2)}) async-start(f32[128,1,9,128]{3,1,2,0:T(1,128)} %copy.122), calls=%async_computation.1 | async-start | bytes 1179648 | tf_op jit(solution)/shard_map/all_to_all | solution.py:111
  54.4 5.1 %while.48 = (s32[]{:T(128)}, f32[3,256]{1,0:T(4,128)S(1)}, f32[9,256]{1,0:T(8,128)S(1)}, f32[8,9,128]{2,1,0:T(8,128)S(1)}, s32[]{:T(128)}, /*index=5*/s32[]{:T(1...) while((s32[]{:T(128)}, f32[3,256]{1,0:T(4,128)S(1)}, f32[9,256]{1,0:T(8,128)S(1)}, ...), condition=%wide.region_4.5_spmd.clone, body=%wide.region_0.4_spmd.clone.sunk | while | flops 952587 | bytes 54035 | solution.py:83
  69.7 20.3 %all-to-all-done.1 = f32[128,1,9,128]{3,1,2,0:T(1,128)S(1)} async-done(((f32[128,1,9,128]{3,1,2,0:T(1,128)}), f32[128,1,9,128]{3,1,2,0:T(1,128)S(1)}, u32[]{:S(2)}, u32[]{:S(2)}) %all-to-all-start.1) | async-done | bytes 589856 | tf_op jit(solution)/shard_map/all_to_all | solution.py:111
  90.1 35.9 %while.46 = (s32[]{:T(128)}, f32[8,16,3,128]{3,1,0,2:T(8,128)S(1)}, f32[8,16,3,128]{3,1,0,2:T(8,128)S(1)}, f32[8,16,9,128]{3,1,0,2:T(8,128)S(1)}, f32[8,16,9,128]{3,1,0,2:T(8,128)S(1)}, /*index=5*/s32[]{:T(128)}) while((s32[]{:T(128)}, f32[8,16,3,128]{3,1,0,2:T(8,128)S(1)}, f32[8,16,3,128]{3,1,0,2:T(8,128)S(1)}, ...), condition=%wide.region_12.13_spmd, body=%wide.region_5.12_spmd.sunk | while | flops 8407042 | bytes 933969 | solution.py:124
  90.2 4.3 %fusion.106 = (f32[16,128]{1,0:T(8,128)S(1)}, f32[16,128]{1,0:T(8,128)S(1)}, f32[16,128]{1,0:T(8,128)S(1)}, f32[16,128]{1,0:T(8,128)S(1)}, f32[16,128]{1,0:T(8,128)S(1)}, /*index=5*/f32[16,128]{1,0:T(8,128)S(1)}) fusion(f32[16,128]{1,0:T(8,128)S(1)} %get-tuple-element.555, f32[16,128]{1,0:T(8,128)S(1)} %get-tuple-element.557, ...), kind=kLoop, calls=%fused_computation.15.clone.1 | loop fusion | flops 8376320 | bytes 196608 | tf_op jit(solution)/shard_map/while/body/eval_jaxpr/reduce_sum | solution.py:51
  126.9 7.6 %all-to-all-start.2 = ((f32[128,1,3,128]{3,1,2,0:T(1,128)}), f32[128,1,3,128]{3,1,2,0:T(1,128)S(1)}, u32[]{:S(2)}, u32[]{:S(2)}) async-start(f32[128,1,3,128]{3,1,2,0:T(1,128)} %copy.128), calls=%async_computation.2 | async-start | bytes 393216 | tf_op jit(solution)/shard_map/all_to_all | solution.py:125
  134.8 19.6 %all-to-all-done.2 = f32[128,1,3,128]{3,1,2,0:T(1,128)S(1)} async-done(((f32[128,1,3,128]{3,1,2,0:T(1,128)}), f32[128,1,3,128]{3,1,2,0:T(1,128)S(1)}, u32[]{:S(2)}, u32[]{:S(2)}) %all-to-all-start.2) | async-done | bytes 196640 | tf_op jit(solution)/shard_map/all_to_all | solution.py:125
  155.9 7.4 %pmax.56 = f32[]{:T(128)} all-reduce(f32[]{:T(128)} %reduce_max.18), channel_id=1, replica_groups=mesh['dom_0'=4,'dom_1'=16,'dom_2'=2,'sub'=4] {'dom_0'}, use_global_device_ids=true, to_apply=%region_15.16 | all-reduce | flops 1 | bytes 8 | tf_op jit(solution)/shard_map/pmax | solution.py:23
  163.3 22.0 %pmax.57 = f32[]{:T(128)} all-reduce(f32[]{:T(128)} %pmax.56), channel_id=1, replica_groups=mesh['dom_0'=4,'dom_1'=16,'dom_2'=2,'sub'=4] {'dom_1'}, use_global_device_ids=true, to_apply=%region_16.17 | all-reduce | flops 1 | bytes 8 | tf_op jit(solution)/shard_map/pmax | solution.py:23
  185.3 12.5 %pmax.58 = f32[]{:T(128)} all-reduce(f32[]{:T(128)} %pmax.57), channel_id=1, replica_groups=mesh['dom_0'=4,'dom_1'=16,'dom_2'=2,'sub'=4] {'dom_2'}, use_global_device_ids=true, to_apply=%region_17.18 | all-reduce | flops 1 | bytes 8 | tf_op jit(solution)/shard_map/pmax | solution.py:23
  197.8 8.7 %pmax.59 = f32[]{:T(128)} all-reduce(f32[]{:T(128)} %pmax.58), channel_id=1, replica_groups=mesh['dom_0'=4,'dom_1'=16,'dom_2'=2,'sub'=4] {'sub'}, use_global_device_ids=true, to_apply=%region_18.19 | all-reduce | flops 1 | bytes 8 | tf_op jit(solution)/shard_map/pmax | solution.py:23
  209.2 9.2 %all-to-all-start.3 = ((f32[128,1,3,128]{3,1,2,0:T(1,128)}), f32[128,1,3,128]{3,1,2,0:T(1,128)S(1)}, u32[]{:S(2)}, u32[]{:S(2)}) async-start(f32[128,1,3,128]{3,1,2,0:T(1,128)} %copy.134), calls=%async_computation.3 | async-start | bytes 393216 | tf_op jit(solution)/shard_map/all_to_all | solution.py:111
  219.5 9.9 %all_gather.7 = f32[8,9,128]{2,1,0:T(8,128)S(1)} all-gather(f32[2,9,128]{2,1,0:T(8,128)S(1)} %get-tuple-element.339), channel_id=1, replica_groups=mesh['dom_0'=4,'dom_1'=16,'dom_2'=2,'sub'=4] {'sub'}, dimensions={0}, use_global_device_ids=true | all-gather | bytes 46080 | tf_op jit(solution)/shard_map/all_gather | solution.py:84
  229.4 9.1 %all-to-all-done.3 = f32[128,1,3,128]{3,1,2,0:T(1,128)S(1)} async-done(((f32[128,1,3,128]{3,1,2,0:T(1,128)}), f32[128,1,3,128]{3,1,2,0:T(1,128)S(1)}, u32[]{:S(2)}, u32[]{:S(2)}) %all-to-all-start.3) | async-done | bytes 196640 | tf_op jit(solution)/shard_map/all_to_all | solution.py:111
  238.5 35.9 %while.47 = (s32[]{:T(128)}, f32[8,16,3,128]{3,1,0,2:T(8,128)S(1)}, f32[8,16,3,128]{3,1,0,2:T(8,128)S(1)}, f32[8,16,9,128]{3,1,2,0:T(8,128)S(1)}, f32[8,16,9,128]{3,1,0,2:T(8,128)S(1)}, /*index=5*/s32[]{:T(128)}) while((s32[]{:T(128)}, f32[8,16,3,128]{3,1,0,2:T(8,128)S(1)}, f32[8,16,3,128]{3,1,0,2:T(8,128)S(1)}, ...), condition=%wide.region_31.32_spmd, body=%wide.region_24.31_spmd.sunk | while | flops 8407042 | bytes 933969 | solution.py:124
  275.3 9.1 %all-to-all-start.4 = ((f32[128,1,3,128]{3,1,2,0:T(1,128)}), f32[128,1,3,128]{3,1,2,0:T(1,128)S(1)}, u32[]{:S(2)}, u32[]{:S(2)}) async-start(f32[128,1,3,128]{3,1,2,0:T(1,128)} %copy.141), calls=%async_computation.4 | async-start | bytes 393216 | tf_op jit(solution)/shard_map/all_to_all | solution.py:125
  284.5 5.1 %while.49 = (s32[]{:T(128)}, f32[3,256]{1,0:T(4,128)S(1)}, f32[9,256]{1,0:T(8,128)S(1)}, f32[8,9,128]{2,1,0:T(8,128)S(1)}, s32[]{:T(128)}, /*index=5*/s32[]{:T(1...) while((s32[]{:T(128)}, f32[3,256]{1,0:T(4,128)S(1)}, f32[9,256]{1,0:T(8,128)S(1)}, ...), condition=%wide.region_23.24_spmd.clone, body=%wide.region_19.23_spmd.clone.sunk | while | flops 952587 | bytes 54035 | solution.py:83
  289.9 14.5 %all-to-all-done.4 = f32[128,1,3,128]{3,1,2,0:T(1,128)S(1)} async-done(((f32[128,1,3,128]{3,1,2,0:T(1,128)}), f32[128,1,3,128]{3,1,2,0:T(1,128)S(1)}, u32[]{:S(2)}, u32[]{:S(2)}) %all-to-all-start.4) | async-done | bytes 196640 | tf_op jit(solution)/shard_map/all_to_all | solution.py:125
  305.3 7.4 %pmax.60 = f32[]{:T(128)} all-reduce(f32[]{:T(128)} %reduce_max.19), channel_id=1, replica_groups=mesh['dom_0'=4,'dom_1'=16,'dom_2'=2,'sub'=4] {'dom_0'}, use_global_device_ids=true, to_apply=%region_34.35 | all-reduce | flops 1 | bytes 8 | tf_op jit(solution)/shard_map/pmax | solution.py:23
  312.7 22.0 %pmax.61 = f32[]{:T(128)} all-reduce(f32[]{:T(128)} %pmax.60), channel_id=1, replica_groups=mesh['dom_0'=4,'dom_1'=16,'dom_2'=2,'sub'=4] {'dom_1'}, use_global_device_ids=true, to_apply=%region_35.36 | all-reduce | flops 1 | bytes 8 | tf_op jit(solution)/shard_map/pmax | solution.py:23
  334.6 12.5 %pmax.62 = f32[]{:T(128)} all-reduce(f32[]{:T(128)} %pmax.61), channel_id=1, replica_groups=mesh['dom_0'=4,'dom_1'=16,'dom_2'=2,'sub'=4] {'dom_2'}, use_global_device_ids=true, to_apply=%region_36.37 | all-reduce | flops 1 | bytes 8 | tf_op jit(solution)/shard_map/pmax | solution.py:23
  347.2 6.7 %pmax.63 = f32[]{:T(128)} all-reduce(f32[]{:T(128)} %pmax.62), channel_id=1, replica_groups=mesh['dom_0'=4,'dom_1'=16,'dom_2'=2,'sub'=4] {'sub'}, use_global_device_ids=true, to_apply=%region_37.38 | all-reduce | flops 1 | bytes 8 | tf_op jit(solution)/shard_map/pmax | solution.py:23
  (276 shorter events, 100.5 us)
Async XLA Ops:
  0.6 0.7 copy-start.5
  2.0 20.7 %copy-start.4 = (s32[1,128,1]{1,2,0:T(1,128)S(1)}, s32[1,128,1]{1,2,0:T(1,128)}, u32[]{:S(2)}) copy-start(s32[1,128,1]{1,2,0:T(1,128)} %param.16) | copy-start | bytes 1540
  2.0 20.8 %copy-start = (f32[2,9,128]{2,0,1:T(2,128)S(1)}, f32[2,9,128]{2,0,1:T(2,128)}, u32[]{:S(2)}) copy-start(f32[2,9,128]{2,0,1:T(2,128)} %param.13) | copy-start | bytes 27652
  2.0 35.7 %all-to-all-start = ((s32[128,1,1]{2,1,0:T(1,128)}), s32[128,1,1]{2,1,0:T(1,128)S(1)}, u32[]{:S(2)}, u32[]{:S(2)}) async-start(s32[128,1,1]{2,1,0:T(1,128)} %copy.121), calls=%async_computation | async-start | bytes 131072 | tf_op jit(solution)/shard_map/all_to_all | solution.py:112
  37.7 52.3 %all-to-all-start.1 = ((f32[128,1,9,128]{3,1,2,0:T(1,128)}), f32[128,1,9,128]{3,1,2,0:T(1,128)S(1)}, u32[]{:S(2)}, u32[]{:S(2)}) async-start(f32[128,1,9,128]{3,1,2,0:T(1,128)} %copy.122), calls=%async_computation.1 | async-start | bytes 1179648 | tf_op jit(solution)/shard_map/all_to_all | solution.py:111
  54.3 5.1 %copy-start.2 = (f32[3,3]{1,0:T(4,128)S(1)}, f32[3,3]{1,0:T(4,128)}, u32[]{:S(2)}) copy-start(f32[3,3]{1,0:T(4,128)} %param.14) | copy-start | bytes 112
  126.9 27.5 %all-to-all-start.2 = ((f32[128,1,3,128]{3,1,2,0:T(1,128)}), f32[128,1,3,128]{3,1,2,0:T(1,128)S(1)}, u32[]{:S(2)}, u32[]{:S(2)}) async-start(f32[128,1,3,128]{3,1,2,0:T(1,128)} %copy.128), calls=%async_computation.2 | async-start | bytes 393216 | tf_op jit(solution)/shard_map/all_to_all | solution.py:125
  154.4 0.7 copy-start.3
  209.2 29.2 %all-to-all-start.3 = ((f32[128,1,3,128]{3,1,2,0:T(1,128)}), f32[128,1,3,128]{3,1,2,0:T(1,128)S(1)}, u32[]{:S(2)}, u32[]{:S(2)}) async-start(f32[128,1,3,128]{3,1,2,0:T(1,128)} %copy.134), calls=%async_computation.3 | async-start | bytes 393216 | tf_op jit(solution)/shard_map/all_to_all | solution.py:111
  275.3 29.1 %all-to-all-start.4 = ((f32[128,1,3,128]{3,1,2,0:T(1,128)}), f32[128,1,3,128]{3,1,2,0:T(1,128)S(1)}, u32[]{:S(2)}, u32[]{:S(2)}) async-start(f32[128,1,3,128]{3,1,2,0:T(1,128)} %copy.141), calls=%async_computation.4 | async-start | bytes 393216 | tf_op jit(solution)/shard_map/all_to_all | solution.py:125
  304.7 49.9 %copy-start.1 = (f32[2,3,128]{2,0,1:T(2,128)}, f32[2,3,128]{2,0,1:T(2,128)S(1)}, u32[]{:S(2)}) copy-start(f32[2,3,128]{2,0,1:T(2,128)S(1)} %get-tuple-element.360) | copy-start | bytes 9220
where the time goes:
time: 357 us; the launch traced here: 355 us
  blocking collectives  119 us (33%)
  other arithmetic  88.8 us (25%)
  waiting for transfers between devices  65 us (18%)
  starting transfers between devices  63.3 us (18%)
  local copies, waits for them, and re-layouts  13.6 us (4%)
    pmax x8, blocking collectives, one_axis_at_a_time(): array = lax.pmax(array, axis)  99.2 us
    reduce_sum x16, other arithmetic, force_on_source(): jnp.sum(weights * offset_c, axis=-2)  69.4 us
    all_to_all x2, waiting for transfers between devices, cross_forces(): lax.all_to_all(on_remote.reshape(peer_count, slot_count, 3, seg_width), D...  34.1 us
    all_to_all x2, waiting for transfers between devices, cross_forces(): lax.all_to_all(outgoing, DOM, split_axis=0, concat_axis=0, tiled=True)  29.3 us
    all_to_all x2, starting transfers between devices, cross_forces(): lax.all_to_all(outgoing, DOM, split_axis=0, concat_axis=0, tiled=True)  25.9 us
    all_to_all x1, starting transfers between devices, cross_forces(): lax.all_to_all(partner_list, DOM, split_axis=0, concat_axis=0, tiled=True)  20.7 us
    all_gather x2, blocking collectives, group_forces(): lax.all_gather(seg_state, 'sub', axis=0, tiled=True)  20.1 us
    all_to_all x2, starting transfers between devices, cross_forces(): lax.all_to_all(on_remote.reshape(peer_count, slot_count, 3, seg_width), D...  16.7 us
  transfers between devices with their start and end apart: 5, of which 5 were waited for; matrix products, arithmetic and copies ran while one was open for 7% of the time, Pallas kernels for 0%

commit v1 on v0

v1 whole, which is shorter than its diff:
```python
import functools

import jax
import jax.numpy as jnp
from jax import lax
from jax.experimental import pallas as pl
from jax.experimental.pallas import tpu as pltpu
from jax.sharding import Mesh
from jax.sharding import PartitionSpec as P

NY, NZ, NC = 4, 16, 2
DOM = ("y", "z", "c")
DOM_SUB = ("y", "z", "c", "x")

COUPLE = 0.0625
CORE_SQUARE = 0.5
TENSION = 0.25
STEP_LENGTH = 1.0
EPSILON = 1e-06

SEG = 128
NDEV = NY * NZ
BATCH = 8
LIST = 192
F32 = jnp.float32
BF16 = jnp.bfloat16


def sublane(shape=(8, SEG)):
    return lax.broadcasted_iota(jnp.int32, shape, len(shape) - 2)


def up(value, count):
    return jnp.concatenate([value[count:], value[:count]], axis=0)


def split2(value):
    high = value.astype(BF16).astype(F32)
    return high, value - high


def split3(value):
    high, rest = split2(value)
    mid, low = split2(rest)
    return high, mid, low


def source_operands(x_tile, l_tile, b_tile):
    row = sublane()
    x_tile = jnp.where(row < 6, x_tile, 0.0)
    square = x_tile * x_tile
    norm0 = square[0:1] + square[1:2] + square[2:3] + CORE_SQUARE
    norm1 = square[3:4] + square[4:5] + square[5:6] + CORE_SQUARE
    full = jnp.where(row == 6, norm0, jnp.where(row == 7, norm1, x_tile))
    high, mid, low = split3(full)
    one = jnp.ones_like(high)
    zero = jnp.zeros_like(high)
    dist = [high, mid, high, mid, low, high, one, zero]
    prod = [jnp.where(row < 3, b_tile[a : a + 1], b_tile[3 + a : 4 + a]) * l_tile for a in range(3)]
    parts = [split2(p) for p in prod]
    highs = [p[0] for p in parts]
    mids = [p[1] for p in parts]
    weight = highs + highs + mids + [zero]
    flag = jnp.where(row == 6, 1.0, 0.0)
    first = jnp.where(row < 6, high, flag)
    second = jnp.where(row < 6, mid, 0.0)
    first_up = jnp.where(row < 3, up(high, 3), flag)
    second_up = jnp.where(row < 3, up(mid, 3), 0.0)
    return dist, weight, (first, second), (first_up, second_up)


def store_rows(ref, index, tiles):
    for at in range(0, len(tiles), 2):
        pair = jnp.concatenate([tiles[at], tiles[at + 1]], axis=0).astype(BF16)
        ref[index, 8 * at : 8 * at + 16, :] = pair


def target_rows(x_tile, l_tile, b_tile, block):
    row = sublane()

    def both(tile):
        if block == 0:
            return jnp.where(row < 3, tile, jnp.where(row < 6, up(tile, 5), 0.0))
        return jnp.where(row < 3, up(tile, 3), jnp.where(row < 6, tile, 0.0))

    x_both = both(x_tile)
    high, mid, low = split3(x_both)
    square = x_both * x_both
    norm = square[0:1] + square[1:2] + square[2:3]
    norm_h, norm_m, norm_l = split3(norm)
    unit = jnp.where(row >= 6, 1.0, 0.0)
    norms = jnp.where(
        row == 0, norm_h, jnp.where(row == 1, norm_m, jnp.where(row == 2, norm_l, 0.0))
    )
    zero = jnp.zeros_like(high)
    dist = [
        -2.0 * high + unit,
        -2.0 * high + unit,
        -2.0 * mid,
        -2.0 * mid,
        -2.0 * high + unit,
        -2.0 * low,
        norms,
    ]
    l_both = both(l_tile)
    base = 3 * block
    prod = [b_tile[base + a : base + a + 1] * l_both for a in range(3)]
    parts = [split2(p) for p in prod]
    highs = [p[0] for p in parts]
    mids = [p[1] for p in parts]
    weight = highs + mids + highs
    dist = dist + [zero] * (16 - len(dist))
    weight = weight + [zero] * (16 - len(weight))
    return jnp.concatenate(dist, axis=0), jnp.concatenate(weight, axis=0)


def build_lists(ints_ref, list_ref, count_ref):
    core = ints_ref[6, 0]
    dummy = 2 * (NDEV + 4)
    for side in range(NC):

        def add(k, counts, side=side):
            c0, c1 = counts
            sent = ints_ref[side, 2 * k]
            part = ints_ref[side, 2 * k + 1]
            source = 2 * k + sent
            list_ref[2 * side, c0] = source
            list_ref[2 * side + 1, c1] = source
            valid = (sent >= 0).astype(jnp.int32)
            to1 = valid * part
            c1 = c1 + to1
            c0 = c0 + valid - to1
            mine = ints_ref[2 + 2 * side, 2 * k + core]
            other = ints_ref[3 + 2 * side, 2 * k + core]
            source = 2 * k + other
            list_ref[2 * side, c0] = source
            list_ref[2 * side + 1, c1] = source
            c0 = c0 + (mine == 0).astype(jnp.int32)
            c1 = c1 + (mine == 1).astype(jnp.int32)
            return c0, c1

        c0, c1 = lax.fori_loop(0, NDEV, add, (jnp.int32(0), jnp.int32(0)), unroll=8)
        own = (core == side).astype(jnp.int32)
        for place, count in ((2 * side, c0), (2 * side + 1, c1)):
            for j in range(8):
                list_ref[place, count + j] = 2 * NDEV + j
            count = count + 8 * own
            for j in range(BATCH):
                list_ref[place, count + j] = dummy
            count_ref[0, place] = lax.div(count + (BATCH - 1), BATCH)


def pair_body(
    list_ref, count_ref, get_source, get_target, force_ref, dist_s, prod_s, mom_s, dist_t, prod_t
):
    def prepare(k):
        x_tile, l_tile, b_tile = get_source(k)
        dist, weight, first, second = source_operands(x_tile, l_tile, b_tile)
        store_rows(dist_s, k, dist)
        store_rows(prod_s, k, weight)
        mom_s[2 * k] = jnp.concatenate(first, axis=0).astype(BF16)
        mom_s[2 * k + 1] = jnp.concatenate(second, axis=0).astype(BF16)

    tail = jnp.zeros((64, SEG), BF16)
    tail_p = jnp.zeros((48, SEG), BF16)

    def clear(k, carry):
        dist_s[k, 64:128, :] = tail
        prod_s[k, 80:128, :] = tail_p
        return carry

    lax.fori_loop(0, NDEV + 5, clear, 0, unroll=3)

    def prepare_loop(k, carry):
        prepare(k)
        return carry

    lax.fori_loop(0, NDEV, prepare_loop, 0, unroll=4)
    for k in range(NDEV, NDEV + 5):
        prepare(k)

    lane = lax.broadcasted_iota(jnp.int32, (SEG, SEG), 1)
    group = lax.shift_right_logical(lane, 3)
    place = lax.bitwise_and(lane, 7)
    for side in range(NC):
        x_tile, l_tile, b_tile = get_target(side)
        for block in range(2):
            dist, weight = target_rows(x_tile, l_tile, b_tile, block)
            dist = dist.T
            weight = weight.T
            for j in range(2):
                mine = (place >= 3 * j) & (place < 3 * j + 3)
                keep = mine | (place == 6 + j) | (group == 6)
                at = 2 * (2 * side + block) + j
                dist_t[at] = jnp.where(keep, dist, 0.0).astype(BF16)
                prod_t[at] = jnp.where(mine, weight, 0.0).astype(BF16)

    for side in range(NC):
        x_tile = get_target(side)[0]
        rows = []
        for block in range(2):
            n = 2 * side + block

            def items(step, total, n=n):
                lows, highs, moments = [], [], []
                for b in range(BATCH):
                    m = list_ref[n, step * BATCH + b]
                    k = lax.shift_right_logical(m, 1)
                    at = 2 * n + lax.bitwise_and(m, 1)
                    sq = jnp.dot(dist_t[at], dist_s[k], preferred_element_type=F32)
                    pr = jnp.dot(prod_t[at], prod_s[k], preferred_element_type=F32)
                    inverse = lax.rsqrt(sq)
                    w = pr * (inverse * inverse * inverse)
                    high = w.astype(BF16)
                    low = (w - high.astype(F32)).astype(BF16)
                    highs.append(high)
                    lows.append(low)
                    moments.append(mom_s[m])
                lhs = jnp.concatenate(highs + lows, axis=1)
                rhs = jnp.concatenate(moments + moments, axis=1)
                return total + lax.dot_general(
                    lhs, rhs, (((1,), (1,)), ((), ())), preferred_element_type=F32
                )

            total = lax.fori_loop(0, count_ref[0, n], items, jnp.zeros((SEG, 16), F32))
            total = jnp.concatenate([total, jnp.zeros((SEG, SEG - 16), F32)], axis=1).T
            x_block = x_tile[3 * block : 3 * block + 3]
            rows.append(x_block * total[6:7] - (total[0:3] + total[8:11]))
        rows.append(jnp.zeros((2, SEG), F32))
        force_ref[side] = jnp.concatenate(rows, axis=0)


SCRATCH = [
    pltpu.VMEM((NDEV + 5, SEG, SEG), BF16),
    pltpu.VMEM((NDEV + 5, SEG, SEG), BF16),
    pltpu.VMEM((2 * (NDEV + 5), 16, SEG), BF16),
    pltpu.VMEM((8, SEG, SEG), BF16),
    pltpu.VMEM((8, SEG, SEG), BF16),
]


def first_kernel(
    ints_ref, all_ref, group_ref, chip_ref, force_ref, list_ref, count_ref, *scratch
):
    build_lists(ints_ref, list_ref, count_ref)

    def get_source(k):
        if isinstance(k, int) and k == NDEV + 4:
            zero = jnp.zeros((8, SEG), F32)
            return zero, zero, zero
        if isinstance(k, int):
            tile = group_ref[k - NDEV]
        else:
            tile = all_ref[k]
        return tile[0:8], tile[8:16], tile[16:24]

    def get_target(side):
        return chip_ref[side, 0:8], chip_ref[side, 8:16], chip_ref[side, 16:24]

    pair_body(list_ref, count_ref, get_source, get_target, force_ref, *scratch)


def second_kernel(
    ints_ref,
    list_ref,
    count_ref,
    all_ref,
    group_ref,
    chip_ref,
    vel_ref,
    top_ref,
    chip_vel_ref,
    force_ref,
    chip_x_ref,
    *scratch,
):
    y_index = ints_ref[6, 1]
    top = jnp.max(jnp.max(top_ref[...], axis=0)[6:7], axis=1, keepdims=True)
    step = STEP_LENGTH / (jnp.sqrt(top) + EPSILON)
    row = sublane()

    def get_source(k):
        if isinstance(k, int) and k == NDEV + 4:
            zero = jnp.zeros((8, SEG), F32)
            return zero, zero, zero
        if isinstance(k, int):
            tile = group_ref[k - NDEV]
            moved = top_ref[4 * y_index + (k - NDEV)]
        else:
            tile = all_ref[k]
            moved = vel_ref[k]
        return tile[0:8] + step * moved, tile[8:16], tile[16:24]

    for side in range(NC):
        moved = jnp.where(row < 6, chip_vel_ref[side], 0.0)
        chip_x_ref[side] = chip_ref[side, 0:8] + step * moved

    def get_target(side):
        return chip_x_ref[side], chip_ref[side, 8:16], chip_ref[side, 16:24]

    pair_body(list_ref, count_ref, get_source, get_target, force_ref, *scratch)


def finish_kernel(ints_ref, stress_ref, parts_ref, chip_ref, x_ref, vel_ref, mine_ref):
    core = ints_ref[6, 0]
    row = sublane()
    lane = lax.broadcasted_iota(jnp.int32, (8, SEG), 1)
    tops = []
    tiles = []
    for side in range(NC):
        x_tile = x_ref[side, 0:8]
        l_tile = chip_ref[side, 8:16]
        b_tile = chip_ref[side, 16:24]
        rows = []
        for block in range(2):
            b = [b_tile[3 * block + a : 3 * block + a + 1] for a in range(3)]
            line = [l_tile[3 * block + a : 3 * block + a + 1] for a in range(3)]
            pulled = [
                stress_ref[a, 0] * b[0] + stress_ref[a, 1] * b[1] + stress_ref[a, 2] * b[2]
                for a in range(3)
            ]
            rows.append(pulled[1] * line[2] - pulled[2] * line[1])
            rows.append(pulled[2] * line[0] - pulled[0] * line[2])
            rows.append(pulled[0] * line[1] - pulled[1] * line[0])
        rows.append(jnp.zeros((2, SEG), F32))
        applied = jnp.concatenate(rows, axis=0)
        left = jnp.where(lane == 0, x_tile, pltpu.roll(x_tile, 1, 1))
        right = jnp.where(lane == SEG - 1, x_tile, pltpu.roll(x_tile, SEG - 1, 1))
        chain = left + right - 2.0 * x_tile
        pair = parts_ref[0, side] + parts_ref[1, side]
        drag = jnp.where(row < 3, b_tile[6:7], b_tile[7:8])
        velocity = (COUPLE * pair + applied + TENSION * chain) / drag
        speed = velocity * velocity
        tops.append(
            jnp.maximum(
                speed[0:1] + speed[1:2] + speed[2:3], speed[3:4] + speed[4:5] + speed[5:6]
            )
        )
        tiles.append(velocity)
    top = jnp.maximum(tops[0], tops[1])
    for side in range(NC):
        vel_ref[side] = jnp.where(row < 6, tiles[side], jnp.where(row == 6, top, 0.0))
    mine_ref[...] = vel_ref[core]


def last_kernel(ints_ref, top_ref, x_ref, vel_ref, pos_out, vel_out):
    core = ints_ref[6, 0]
    top = jnp.max(jnp.max(top_ref[...], axis=0)[6:7], axis=1, keepdims=True)
    step = STEP_LENGTH / (jnp.sqrt(top) + EPSILON)
    velocity = vel_ref[core]
    moved = x_ref[core] + step * velocity
    for block in range(2):
        pos_out[block] = moved[3 * block : 3 * block + 3]
        vel_out[block] = velocity[3 * block : 3 * block + 3]


SMEM = pl.BlockSpec(memory_space=pltpu.SMEM)
VMEM = pl.BlockSpec(memory_space=pltpu.VMEM)


def shape(*dims, dtype=F32):
    return jax.ShapeDtypeStruct(dims, dtype)


def spread(value, axes, count):
    return lax.all_to_all(
        jnp.broadcast_to(value[None], (count,) + value.shape), axes, 0, 0, tiled=True
    )


def local(segments, stress, drag_coef, send_ids, partner_ids):
    core = lax.axis_index("c")
    y_index = lax.axis_index("y")
    chip_index = y_index * NZ + lax.axis_index("z")
    send = send_ids.reshape(1, SEG).astype(F32)
    part = partner_ids.reshape(1, SEG).astype(F32)
    raw = jnp.concatenate(
        [
            segments[:, 0:3].reshape(6, SEG),
            jnp.zeros((2, SEG), F32),
            segments[:, 3:6].reshape(6, SEG),
            send,
            part,
            segments[:, 6:9].reshape(6, SEG),
            drag_coef,
        ],
        axis=0,
    )
    chip = lax.all_gather(raw, "c", axis=0)
    along_z = spread(raw, "z", NZ)
    group = spread(raw, "x", 4)
    everyone = spread(along_z.reshape(NZ * 24, SEG), "y", NY).reshape(NDEV, 24, SEG)

    lists = everyone[:, 14:16].reshape(2 * NDEV, SEG)
    lane = lax.broadcasted_iota(jnp.int32, (NC, SEG), 1)
    wanted = 2 * chip_index + lax.broadcasted_iota(jnp.int32, (NC, SEG), 0)
    pick = (lane == wanted).astype(F32)
    incoming = lax.dot_general(
        pick, lists, (((1,), (1,)), ((), ())), precision=lax.Precision.HIGHEST
    )
    where = jnp.where(lane[0:1] == 0, core, y_index)
    ints = jnp.concatenate(
        [
            incoming.astype(jnp.int32),
            chip[:, 14:16].reshape(4, SEG).astype(jnp.int32),
            where,
            jnp.zeros((1, SEG), jnp.int32),
        ],
        axis=0,
    )

    force, lists, counts = pl.pallas_call(
        first_kernel,
        name="first_pairs",
        in_specs=[SMEM, VMEM, VMEM, VMEM],
        out_specs=[VMEM, SMEM, SMEM],
        out_shape=[
            shape(NC, 8, SEG),
            shape(4, LIST, dtype=jnp.int32),
            shape(1, 4, dtype=jnp.int32),
        ],
        scratch_shapes=SCRATCH,
    )(ints, everyone, group, chip)

    def finish(parts, position):
        return pl.pallas_call(
            finish_kernel,
            name="finish",
            in_specs=[SMEM, SMEM, VMEM, VMEM, VMEM],
            out_specs=[VMEM, VMEM],
            out_shape=[shape(NC, 8, SEG), shape(8, SEG)],
        )(ints, stress, parts, chip, position)

    chip_vel, mine = finish(lax.all_gather(force, "c", axis=0), chip[:, 0:8])
    vel_z = spread(mine, "z", NZ)
    vel_all = spread(vel_z.reshape(NZ * 8, SEG), "y", NY).reshape(NDEV, 8, SEG)
    row = lax.broadcasted_iota(jnp.int32, (8, SEG), 0)
    with_top = jnp.where(row == 6, jnp.max(vel_z[:, 6:7], axis=0), mine)
    tops = spread(with_top, ("y", "x"), 16)

    force, position = pl.pallas_call(
        second_kernel,
        name="second_pairs",
        in_specs=[SMEM, SMEM, SMEM] + [VMEM] * 6,
        out_specs=[VMEM, VMEM],
        out_shape=[shape(NC, 8, SEG), shape(NC, 8, SEG)],
        scratch_shapes=SCRATCH,
    )(ints, lists, counts, everyone, group, chip, vel_all, tops, chip_vel)

    chip_vel, mine = finish(lax.all_gather(force, "c", axis=0), position)
    top_z = jnp.max(spread(mine, "z", NZ), axis=0)
    tops = spread(top_z, ("y", "x"), 16)
    return pl.pallas_call(
        last_kernel,
        name="last",
        in_specs=[SMEM, VMEM, VMEM, VMEM],
        out_specs=[VMEM, VMEM],
        out_shape=[shape(2, 3, SEG), shape(2, 3, SEG)],
    )(ints, tops, position, chip_vel)


def solution(mesh):
    split = Mesh(
        mesh.devices.reshape(NY, NZ, NC, mesh.shape["sub"]), ("y", "z", "c", "x")
    )
    return jax.shard_map(
        local,
        mesh=split,
        in_specs=(
            P(DOM_SUB, None, None),
            P(),
            P(DOM_SUB, None),
            P(DOM_SUB, None, None),
            P(DOM_SUB, None, None),
        ),
        out_specs=(P(DOM_SUB, None, None), P(DOM_SUB, None, None)),
        check_vma=False,
    )
```

time: 357 us -> 170 us (0.48)
  other arithmetic: 88.8 us -> 0.82 us
  waiting for transfers between devices: 65 us -> 16.2 us
  starting transfers between devices: 63.3 us -> 17.7 us
  Pallas kernels: 0 us -> 26.7 us
  blocking collectives: 119 us -> 96.9 us
  local copies, waits for them, and re-layouts: 13.6 us -> 8.92 us
    pmax x8 -> x0, blocking collectives: 99.2 us -> none  [one_axis_at_a_time(): array = lax.pmax(array, axis)]
    reduce_sum x32 -> x0, other arithmetic: 78 us -> none  [the longest x16 69.4 us: force_on_source(): jnp.sum(weights * offset_c, axis=-2)]
    all_to_all x0 -> x5, blocking collectives: none -> 72.4 us  [spread(): lax.all_to_all(jnp.broadcast_to(value[None], (count,) + value.shape), axe...]
    all_to_all x5 -> x3, waiting for transfers between devices: 65 us -> 16.2 us  [spread(): lax.all_to_all(jnp.broadcast_to(value[None], (count,) + value.shape), axe...]
    all_to_all x5 -> x3, starting transfers between devices: 63.3 us -> 17.7 us  [spread(): lax.all_to_all(jnp.broadcast_to(value[None], (count,) + value.shape), axe...]
    pallas_call x0 -> x5, Pallas kernels: none -> 26.7 us  [the longest x1 12 us: local(): pl.pallas_call(first_kernel, name='first_pairs', in_specs=[SMEM, VMEM, VM...]
    sub x3 -> x0, other arithmetic: 5.67 us -> none  [the longest x1 3.8 us: external_force(): first = pulled[1] * line_vec[:, 2] - pulled[2] * line_vec[:, 1]]
    gather x5 -> x0, local copies, waits for them, and re-layouts: 4.84 us -> none  [the longest x3 2.52 us: cross_forces(): seg_state[jnp.maximum(send_list, 0)]]
  transfers between devices with their start and end apart: 5 -> 3, of which waited for: 5 -> 3; matrix products, arithmetic and copies ran while one was open for 7% -> 1% of each run, Pallas kernels for 0% -> 0%
where the time goes in v1:
time: 170 us; the launch traced here: 168 us
  blocking collectives  96.9 us (57%)
  Pallas kernels  26.7 us (16%)
  starting transfers between devices  17.7 us (10%)
  waiting for transfers between devices  16.2 us (10%)
  local copies, waits for them, and re-layouts  8.92 us (5%)
    all_to_all x5, blocking collectives, spread(): lax.all_to_all(jnp.broadcast_to(value[None], (count,) + value.shape), axe...  72.4 us
    all_to_all x3, starting transfers between devices, spread(): lax.all_to_all(jnp.broadcast_to(value[None], (count,) + value.shape), axe...  17.7 us
    all_to_all x3, waiting for transfers between devices, spread(): lax.all_to_all(jnp.broadcast_to(value[None], (count,) + value.shape), axe...  16.2 us
    pallas_call x1, Pallas kernels, local(): pl.pallas_call(first_kernel, name='first_pairs', in_specs=[SMEM, VMEM, VM...  12 us
    all_gather x1, blocking collectives, local(): chip_vel, mine = finish(lax.all_gather(force, 'c', axis=0), chip[:, 0:8])  10.6 us
    pallas_call x1, Pallas kernels, local(): pl.pallas_call(second_kernel, name='second_pairs', in_specs=[SMEM, SMEM,...  9.92 us
    all_gather x1, blocking collectives, local(): chip_vel, mine = finish(lax.all_gather(force, 'c', axis=0), position)  7.2 us
    all_gather x1, blocking collectives, local(): chip = lax.all_gather(raw, 'c', axis=0)  6.59 us
  transfers between devices with their start and end apart: 3, of which 3 were waited for; matrix products, arithmetic and copies ran while one was open for 1% of the time, Pallas kernels for 0%

profile of v1, /device:TPU:1, one launch (start us, length us, event | category | flops | bytes accessed | tf_op | source)
XLA Modules:
  0.0 168.1 jit_solution(16115340735077593584)
XLA Ops:
  0.6 0.7 fusion.3
  2.8 28.1 %all_to_all.40 = f32[16,24,128]{2,1,0:T(8,128)S(1)} all-to-all(f32[16,24,128]{2,1,0:T(8,128)S(1)} %broadcast_in_dim.72), channel_id=1, replica_groups=mesh['y'=4,'z'=16,'c'=2,'x'=4] {'z'}, dimensions={0} | all-to-all | bytes 393216 | tf_op jit(solution)/shard_map/all_to_all | solution.py:366
  30.9 1.0 broadcast_in_dim.74
  31.9 4.2 %all-to-all-start.1 = ((f32[4,384,128]{2,1,0:T(8,128)}), f32[4,384,128]{2,1,0:T(8,128)S(1)}, u32[]{:S(2)}, u32[]{:S(2)}) async-start(f32[4,384,128]{2,1,0:T(8,128)} %broadcast_in_dim.74), calls=%async_computation.1 | async-start | bytes 1572864 | tf_op jit(solution)/shard_map/all_to_all | solution.py:366
  36.1 6.6 %all-gather = f32[48,128]{1,0:T(8,128)S(1)} all-gather(f32[24,128]{1,0:T(8,128)S(1)} %concatenate.6), channel_id=2, replica_groups=mesh['y'=4,'z'=16,'c'=2,'x'=4] {'c'}, dimensions={0}, use_global_device_ids=true | all-gather | bytes 36864 | tf_op jit(solution)/shard_map/all_gather | solution.py:389
  43.3 1.1 all-to-all-done.1
  45.1 4.0 %all-to-all-start.2 = ((f32[4,24,128]{2,1,0:T(8,128)}), f32[4,24,128]{2,1,0:T(8,128)S(1)}, u32[]{:S(2)}, u32[]{:S(2)}) async-start(f32[4,24,128]{2,1,0:T(8,128)} %broadcast_in_dim.78), calls=%async_computation.2 | async-start | bytes 98304 | tf_op jit(solution)/shard_map/all_to_all | solution.py:366
  50.0 3.5 %all-to-all-done.2.group_ref = f32[4,24,128]{2,1,0:T(8,128)S(1)} async-done(((f32[4,24,128]{2,1,0:T(8,128)}), f32[4,24,128]{2,1,0:T(8,128)S(1)}, u32[]{:S(2)}, u32[]{:S(2)}) %all-to-all-start.2) | async-done | bytes 49184 | tf_op jit(solution)/shard_map/all_to_all | solution.py:366
  54.1 12.0 %first_pairs.1 = (f32[2,8,128]{2,1,0:T(8,128)}, s32[4,192]{1,0:T(4,128)}, s32[1,4]{1,0:T(1,128)}) custom-call(s32[8,128]{1,0:T(8,128)} %pad_add_fusion.ints_ref, f32[64,24,128]{2,1,0:T(8,128)} %bitcast.15, f32[4,24,128]{2,1,0:T(8,128)} %copy-done.2, f32[2,24,128]{2,1,0:T(8,128)} %bitcast.21), custom_call_target="tpu_custom_call" | custom-call | tf_op jit(solution)/shard_map/first_pairs/pallas_call | solution.py:412
  66.1 10.6 %all-gather.1 = f32[4,8,128]{2,1,0:T(8,128)} all-gather(f32[2,8,128]{2,1,0:T(8,128)} %get-tuple-element.13), channel_id=3, replica_groups=mesh['y'=4,'z'=16,'c'=2,'x'=4] {'c'}, dimensions={0}, use_global_device_ids=true | all-gather | bytes 24576 | tf_op jit(solution)/shard_map/all_gather | solution.py:434
  76.8 1.6 finish.2
  78.4 1.3 broadcast_in_dim.79
  79.7 9.5 %all-to-all-start.3 = ((f32[16,8,128]{2,1,0:T(8,128)}), f32[16,8,128]{2,1,0:T(8,128)S(1)}, u32[]{:S(2)}, u32[]{:S(2)}) async-start(f32[16,8,128]{2,1,0:T(8,128)} %broadcast_in_dim.79), calls=%async_computation.3 | async-start | bytes 131072 | tf_op jit(solution)/shard_map/all_to_all | solution.py:366
  89.2 11.6 %all-to-all-done.3 = f32[16,8,128]{2,1,0:T(8,128)S(1)} async-done(((f32[16,8,128]{2,1,0:T(8,128)}), f32[16,8,128]{2,1,0:T(8,128)S(1)}, u32[]{:S(2)}, u32[]{:S(2)}) %all-to-all-start.3) | async-done | bytes 65568 | tf_op jit(solution)/shard_map/all_to_all | solution.py:366
  100.9 9.7 %all_to_all.41.top_ref = f32[16,8,128]{2,1,0:T(8,128)} all-to-all(f32[16,8,128]{2,1,0:T(8,128)S(1)} %broadcast_in_dim.83), channel_id=1, replica_groups=mesh['y'=4,'z'=16,'c'=2,'x'=4] {'y','x'}, dimensions={0} | all-to-all | bytes 131072 | tf_op jit(solution)/shard_map/all_to_all | solution.py:366
  110.6 8.6 %all_to_all.42 = f32[4,128,128]{2,1,0:T(8,128)} all-to-all(f32[4,128,128]{2,1,0:T(8,128)S(1)} %broadcast_in_dim.81), channel_id=1, replica_groups=mesh['y'=4,'z'=16,'c'=2,'x'=4] {'y'}, dimensions={0} | all-to-all | bytes 524288 | tf_op jit(solution)/shard_map/all_to_all | solution.py:366
  119.2 9.9 %second_pairs.1 = (f32[2,8,128]{2,1,0:T(8,128)}, f32[2,8,128]{2,1,0:T(8,128)}) custom-call(s32[8,128]{1,0:T(8,128)} %pad_add_fusion.ints_ref, s32[4,192]{1,0:T(4,128)} %get-tuple-element.11.list_ref, s32[1,4]{1,0:T(1,128)} %get-tuple-element.12.count_ref, f32[64,24,128]{2,1,0:T(8,128)} %bitcast.16, f32[4,24,128]{2,1,0:T(8,128)} %copy-done.2, ...), custom_call_target="tpu_custom_call" | custom-call | tf_op jit(solution)/shard_map/second_pairs/pallas_call | solution.py:441
  129.2 7.2 %all-gather.2 = f32[4,8,128]{2,1,0:T(8,128)} all-gather(f32[2,8,128]{2,1,0:T(8,128)} %get-tuple-element.16), channel_id=4, replica_groups=mesh['y'=4,'z'=16,'c'=2,'x'=4] {'c'}, dimensions={0}, use_global_device_ids=true | all-gather | bytes 24576 | tf_op jit(solution)/shard_map/all_gather | solution.py:450
  136.4 1.6 finish.3
  137.9 0.7 broadcast_in_dim.84
  138.6 16.3 %all_to_all.43 = f32[16,8,128]{2,1,0:T(8,128)S(1)} all-to-all(f32[16,8,128]{2,1,0:T(8,128)S(1)} %broadcast_in_dim.84), channel_id=1, replica_groups=mesh['y'=4,'z'=16,'c'=2,'x'=4] {'z'}, dimensions={0} | all-to-all | bytes 131072 | tf_op jit(solution)/shard_map/all_to_all | solution.py:366
  154.9 9.8 %all_to_all.44.top_ref = f32[16,8,128]{2,1,0:T(8,128)} all-to-all(f32[16,8,128]{2,1,0:T(8,128)S(1)} %broadcast_in_dim.85), channel_id=1, replica_groups=mesh['y'=4,'z'=16,'c'=2,'x'=4] {'y','x'}, dimensions={0} | all-to-all | bytes 131072 | tf_op jit(solution)/shard_map/all_to_all | solution.py:366
  164.7 1.6 last.1
  166.2 1.3 copy.22
  (44 shorter events, 5.0 us)
Async XLA Ops:
  1.4 0.7 copy-start.6
  1.4 0.7 copy-start.7
  2.1 0.7 copy-start.5
  31.9 12.5 %all-to-all-start.1 = ((f32[4,384,128]{2,1,0:T(8,128)}), f32[4,384,128]{2,1,0:T(8,128)S(1)}, u32[]{:S(2)}, u32[]{:S(2)}) async-start(f32[4,384,128]{2,1,0:T(8,128)} %broadcast_in_dim.74), calls=%async_computation.1 | async-start | bytes 1572864 | tf_op jit(solution)/shard_map/all_to_all | solution.py:366
  42.7 2.4 %copy-start.1 = (f32[48,128]{1,0:T(8,128)}, f32[48,128]{1,0:T(8,128)S(1)}, u32[]{:S(2)}) copy-start(f32[48,128]{1,0:T(8,128)S(1)} %all-gather) | copy-start | bytes 73732
  44.4 9.1 %copy-start = (f32[4,384,128]{2,1,0:T(8,128)}, f32[4,384,128]{2,1,0:T(8,128)S(1)}, u32[]{:S(2)}) copy-start(f32[4,384,128]{2,1,0:T(8,128)S(1)} %all-to-all-done.1) | copy-start | bytes 2359300
  45.1 8.4 %all-to-all-start.2 = ((f32[4,24,128]{2,1,0:T(8,128)}), f32[4,24,128]{2,1,0:T(8,128)S(1)}, u32[]{:S(2)}, u32[]{:S(2)}) async-start(f32[4,24,128]{2,1,0:T(8,128)} %broadcast_in_dim.78), calls=%async_computation.2 | async-start | bytes 98304 | tf_op jit(solution)/shard_map/all_to_all | solution.py:366
  53.5 0.6 copy-start.2
  79.7 21.1 %all-to-all-start.3 = ((f32[16,8,128]{2,1,0:T(8,128)}), f32[16,8,128]{2,1,0:T(8,128)S(1)}, u32[]{:S(2)}, u32[]{:S(2)}) async-start(f32[16,8,128]{2,1,0:T(8,128)} %broadcast_in_dim.79), calls=%async_computation.3 | async-start | bytes 131072 | tf_op jit(solution)/shard_map/all_to_all | solution.py:366
  89.2 11.6 %copy-start.3 = (f32[8,128]{1,0:T(8,128)S(1)}, f32[8,128]{1,0:T(8,128)}, u32[]{:S(2)}) copy-start(f32[8,128]{1,0:T(8,128)} %get-tuple-element.14) | copy-start | bytes 12292
  166.2 1.3 copy-start.4

commit v2 on v1

v2 whole, which is shorter than its diff:
```python
import functools

import jax
import jax.numpy as jnp
from jax import lax
from jax.experimental import pallas as pl
from jax.experimental.pallas import tpu as pltpu
from jax.sharding import Mesh
from jax.sharding import PartitionSpec as P

NY, NZ, NC = 4, 16, 2
DOM = ("y", "z", "c")
DOM_SUB = ("y", "z", "c", "x")

COUPLE = 0.0625
CORE_SQUARE = 0.5
TENSION = 0.25
STEP_LENGTH = 1.0
EPSILON = 1e-06

SEG = 128
NDEV = NY * NZ
NX = 4
BATCH = 16
LIST = 320
DUMMY = 2 * (NDEV + NX)
F32 = jnp.float32
BF16 = jnp.bfloat16


def sublane(shape=(8, SEG)):
    return lax.broadcasted_iota(jnp.int32, shape, len(shape) - 2)


def up(value, count):
    return jnp.concatenate([value[count:], value[:count]], axis=0)


def split2(value):
    high = value.astype(BF16).astype(F32)
    return high, value - high


def split3(value):
    high, rest = split2(value)
    mid, low = split2(rest)
    return high, mid, low


def source_operands(x_tile, l_tile, b_tile):
    row = sublane()
    x_tile = jnp.where(row < 6, x_tile, 0.0)
    square = x_tile * x_tile
    norm0 = square[0:1] + square[1:2] + square[2:3] + CORE_SQUARE
    norm1 = square[3:4] + square[4:5] + square[5:6] + CORE_SQUARE
    full = jnp.where(row == 6, norm0, jnp.where(row == 7, norm1, x_tile))
    high, mid, low = split3(full)
    dist = [high, mid, high, mid, low, high, jnp.ones_like(high)]
    prod = [jnp.where(row < 3, b_tile[a : a + 1], b_tile[3 + a : 4 + a]) * l_tile for a in range(3)]
    parts = [split2(p) for p in prod]
    highs = [p[0] for p in parts]
    mids = [p[1] for p in parts]
    weight = highs + highs + mids
    flag = jnp.where(row == 6, 1.0, 0.0)
    first = (jnp.where(row < 6, high, flag), jnp.where(row < 6, mid, 0.0))
    second = (jnp.where(row < 3, up(high, 3), flag), jnp.where(row < 3, up(mid, 3), 0.0))
    return dist + weight, first, second


def store_rows(ref, index, tiles):
    for at in range(0, len(tiles), 2):
        pair = jnp.concatenate([tiles[at], tiles[at + 1]], axis=0).astype(BF16)
        ref[index, 8 * at : 8 * at + 16, :] = pair


def target_rows(x_tile, l_tile, b_tile, block):
    row = sublane()

    def both(tile):
        if block == 0:
            return jnp.where(row < 3, tile, jnp.where(row < 6, up(tile, 5), 0.0))
        return jnp.where(row < 3, up(tile, 3), jnp.where(row < 6, tile, 0.0))

    x_both = both(x_tile)
    high, mid, low = split3(x_both)
    square = x_both * x_both
    norm = square[0:1] + square[1:2] + square[2:3]
    norm_h, norm_m, norm_l = split3(norm)
    unit = jnp.where(row >= 6, 1.0, 0.0)
    norms = jnp.where(
        row == 0, norm_h, jnp.where(row == 1, norm_m, jnp.where(row == 2, norm_l, 0.0))
    )
    zero = jnp.zeros_like(high)
    dist = [
        -2.0 * high + unit,
        -2.0 * high + unit,
        -2.0 * mid,
        -2.0 * mid,
        -2.0 * high + unit,
        -2.0 * low,
        norms,
    ]
    l_both = both(l_tile)
    base = 3 * block
    prod = [b_tile[base + a : base + a + 1] * l_both for a in range(3)]
    parts = [split2(p) for p in prod]
    highs = [p[0] for p in parts]
    mids = [p[1] for p in parts]
    weight = highs + mids + highs
    return jnp.concatenate(dist + [zero] * 9, axis=0), jnp.concatenate([zero] * 7 + weight, axis=0)


def build_list(codes_ref, list_ref, count_ref):
    core = codes_ref[6, 0]

    def add(k, count):
        for line in range(2 * NC):
            code = codes_ref[line, 2 * k + core if line >= NC else 2 * k]
            list_ref[0, count] = code
            count = count + (code >= 0).astype(jnp.int32)
        return count

    count = lax.fori_loop(0, NDEV, add, jnp.int32(0), unroll=8)
    for block in range(2):
        for j in range(2 * NX):
            list_ref[0, count + 2 * NX * block + j] = 256 * (2 * core + block) + 2 * NDEV + j
    count = count + 4 * NX
    for j in range(BATCH):
        list_ref[0, count + j] = DUMMY
    count_ref[0, 0] = lax.div(count + (BATCH - 1), BATCH)


def pair_body(list_ref, count_ref, get_source, get_target, force_ref, source_s, moment_s, target_s):
    def prepare(k):
        tiles, first, second = source_operands(*get_source(k))
        store_rows(source_s, k, tiles)
        moment_s[2 * k] = jnp.concatenate(first, axis=0).astype(BF16)
        moment_s[2 * k + 1] = jnp.concatenate(second, axis=0).astype(BF16)

    def prepare_loop(k, carry):
        prepare(k)
        return carry

    lax.fori_loop(0, NDEV, prepare_loop, 0, unroll=4)
    for k in range(NDEV, NDEV + NX + 1):
        prepare(k)

    lane = lax.broadcasted_iota(jnp.int32, (SEG, SEG), 1)
    place = lax.bitwise_and(lane, 7)
    for side in range(NC):
        x_tile, l_tile, b_tile = get_target(side)
        for block in range(2):
            dist, weight = target_rows(x_tile, l_tile, b_tile, block)
            dist = dist.T
            weight = weight.T
            for j in range(2):
                mine = (place >= 3 * j) & (place < 3 * j + 3)
                keep = mine | (place == 6 + j) | (lane >= 48)
                at = 2 * (2 * side + block) + j
                target_s[at, 0:SEG] = jnp.where(keep, dist, 0.0).astype(BF16)
                target_s[at, SEG : 2 * SEG] = jnp.where(mine, weight, 0.0).astype(BF16)

    def items(step, total):
        lows, highs, moments = [], [], []
        for b in range(BATCH):
            code = list_ref[0, step * BATCH + b]
            n = lax.shift_right_logical(code, 8)
            m = lax.bitwise_and(code, 255)
            at = 2 * n + lax.bitwise_and(m, 1)
            both = jnp.dot(
                target_s[at], source_s[lax.shift_right_logical(m, 1)], preferred_element_type=F32
            )
            inverse = lax.rsqrt(both[0:SEG])
            w = both[SEG : 2 * SEG] * (inverse * inverse * inverse)
            high = w.astype(BF16)
            highs.append(high)
            lows.append((w - high.astype(F32)).astype(BF16))
            moment = moment_s[m]
            zero = jnp.zeros_like(moment)
            moments.append(
                jnp.concatenate([jnp.where(n == t, moment, zero) for t in range(4)], axis=0)
            )
        lhs = jnp.concatenate(moments + moments, axis=1)
        rhs = jnp.concatenate(highs + lows, axis=1)
        return total + lax.dot_general(
            lhs, rhs, (((1,), (1,)), ((), ())), preferred_element_type=F32
        )

    total = lax.fori_loop(0, count_ref[0, 0], items, jnp.zeros((64, SEG), F32))
    for side in range(NC):
        x_tile = get_target(side)[0]
        rows = []
        for block in range(2):
            at = 16 * (2 * side + block)
            x_block = x_tile[3 * block : 3 * block + 3]
            rows.append(
                x_block * total[at + 6 : at + 7] - (total[at : at + 3] + total[at + 8 : at + 11])
            )
        rows.append(jnp.zeros((2, SEG), F32))
        force_ref[side] = jnp.concatenate(rows, axis=0)


SCRATCH = [
    pltpu.VMEM((NDEV + NX + 1, SEG, SEG), BF16),
    pltpu.VMEM((2 * (NDEV + NX + 1), 16, SEG), BF16),
    pltpu.VMEM((8, 2 * SEG, SEG), BF16),
]


def tiles_of(tile):
    return tile[0:8], tile[8:16], tile[16:24]


def no_source():
    zero = jnp.zeros((8, SEG), F32)
    return zero, zero, zero


def first_kernel(codes_ref, all_ref, g0, g1, g2, g3, chip_ref, force_ref, list_ref, count_ref, *scratch):
    build_list(codes_ref, list_ref, count_ref)
    group = (g0, g1, g2, g3)

    def get_source(k):
        if isinstance(k, int):
            return no_source() if k == NDEV + NX else tiles_of(group[k - NDEV])
        return tiles_of(all_ref.at[k])

    def get_target(side):
        return tiles_of(chip_ref.at[side])

    pair_body(list_ref, count_ref, get_source, get_target, force_ref, *scratch)


def second_kernel(
    codes_ref,
    list_ref,
    count_ref,
    all_ref,
    g0,
    g1,
    g2,
    g3,
    chip_ref,
    vel_ref,
    near_ref,
    chip_vel_ref,
    force_ref,
    chip_x_ref,
    *scratch,
):
    y_index = codes_ref[6, 1]
    x_index = codes_ref[6, 2]
    top = vel_ref[0, 0]
    for z in range(1, NZ):
        top = jnp.maximum(top, vel_ref[z, 0])
    top = jnp.max(top[6:7], axis=1, keepdims=True)
    step = STEP_LENGTH / (jnp.sqrt(top) + EPSILON)
    row = sublane()
    group = (g0, g1, g2, g3)

    def get_source(k):
        if isinstance(k, int):
            if k == NDEV + NX:
                return no_source()
            shift = k - NDEV
            x_tile, l_tile, b_tile = tiles_of(group[shift])
            moved = near_ref[y_index, lax.bitwise_and(x_index - shift, NX - 1)]
        else:
            x_tile, l_tile, b_tile = tiles_of(all_ref.at[k])
            moved = vel_ref[lax.bitwise_and(k, NZ - 1), lax.shift_right_logical(k, 4)]
        return x_tile + step * moved, l_tile, b_tile

    for side in range(NC):
        moved = jnp.where(row < 6, chip_vel_ref[side], 0.0)
        chip_x_ref[side] = chip_ref[side, 0:8] + step * moved

    def get_target(side):
        return chip_x_ref[side], chip_ref[side, 8:16], chip_ref[side, 16:24]

    pair_body(list_ref, count_ref, get_source, get_target, force_ref, *scratch)


def finish_kernel(last, codes_ref, stress_ref, parts_ref, chip_ref, x_ref, vel_ref, out_ref):
    core = codes_ref[6, 0]
    row = sublane()
    lane = lax.broadcasted_iota(jnp.int32, (8, SEG), 1)
    tops = []
    tiles = []
    for side in range(NC):
        x_tile = x_ref[side, 0:8]
        l_tile = chip_ref[side, 8:16]
        b_tile = chip_ref[side, 16:24]
        rows = []
        for block in range(2):
            b = [b_tile[3 * block + a : 3 * block + a + 1] for a in range(3)]
            line = [l_tile[3 * block + a : 3 * block + a + 1] for a in range(3)]
            pulled = [
                stress_ref[a, 0] * b[0] + stress_ref[a, 1] * b[1] + stress_ref[a, 2] * b[2]
                for a in range(3)
            ]
            rows.append(pulled[1] * line[2] - pulled[2] * line[1])
            rows.append(pulled[2] * line[0] - pulled[0] * line[2])
            rows.append(pulled[0] * line[1] - pulled[1] * line[0])
        rows.append(jnp.zeros((2, SEG), F32))
        applied = jnp.concatenate(rows, axis=0)
        left = jnp.where(lane == 0, x_tile, pltpu.roll(x_tile, 1, 1))
        right = jnp.where(lane == SEG - 1, x_tile, pltpu.roll(x_tile, SEG - 1, 1))
        chain = left + right - 2.0 * x_tile
        pair = parts_ref[0, side] + parts_ref[1, side]
        drag = jnp.where(row < 3, b_tile[6:7], b_tile[7:8])
        velocity = (COUPLE * pair + applied + TENSION * chain) / drag
        speed = velocity * velocity
        tops.append(
            jnp.maximum(
                speed[0:1] + speed[1:2] + speed[2:3], speed[3:4] + speed[4:5] + speed[5:6]
            )
        )
        tiles.append(velocity)
    top = jnp.maximum(tops[0], tops[1])
    for side in range(NC):
        vel_ref[side] = jnp.where(row < 6, tiles[side], jnp.where(row == 6, top, 0.0))
    if last:
        for peer in range(NZ):
            out_ref[peer] = top
    else:
        mine = vel_ref[core]
        for peer in range(NY * NX):
            out_ref[peer] = mine


def pack_kernel(seg_ref, drag_ref, send_ref, part_ref, raw_ref, out_ref):
    raw_ref[...] = jnp.zeros((24, SEG), F32)
    for block in range(2):
        for comp in range(3):
            for tile in range(3):
                raw_ref[8 * tile + 3 * block + comp, :] = seg_ref[3 * tile + comp, block, :]
        raw_ref[22 + block, :] = drag_ref[block, :]
    raw_ref[14, :] = send_ref[0, :].astype(F32)
    raw_ref[15, :] = part_ref[0, :].astype(F32)
    raw = raw_ref[...]
    for peer in range(NZ):
        out_ref[peer] = raw


def relay_kernel(codes_ref, near_ref, out_ref):
    x_index = codes_ref[6, 2]
    top = near_ref[0, 0]
    for at in range(1, NY * NX):
        top = jnp.maximum(top, near_ref[at // NX, at % NX])
    row = sublane()
    for y in range(NY):
        tile = jnp.where(row == 6, top, near_ref[y, x_index])
        for peer in range(NZ):
            out_ref[peer, y] = tile


def last_kernel(codes_ref, top_ref, x_ref, vel_ref, pos_out, vel_out):
    core = codes_ref[6, 0]
    top = jnp.max(jnp.max(top_ref[...], axis=0), axis=1, keepdims=True)
    step = STEP_LENGTH / (jnp.sqrt(top) + EPSILON)
    velocity = vel_ref[core]
    moved = x_ref[core] + step * velocity
    for block in range(2):
        for comp in range(3):
            pos_out[comp, block, :] = moved[3 * block + comp]
            vel_out[comp, block, :] = velocity[3 * block + comp]


SMEM = pl.BlockSpec(memory_space=pltpu.SMEM)
VMEM = pl.BlockSpec(memory_space=pltpu.VMEM)


def shape(*dims, dtype=F32):
    return jax.ShapeDtypeStruct(dims, dtype)


def call(kernel, name, operands, outs, smem_in=0, smem_out=0, scratch=(), mib=4):
    return pl.pallas_call(
        kernel,
        name=name,
        in_specs=[SMEM] * smem_in + [VMEM] * (len(operands) - smem_in),
        out_specs=[VMEM] * (len(outs) - smem_out) + [SMEM] * smem_out,
        out_shape=outs,
        scratch_shapes=scratch,
        compiler_params=pltpu.CompilerParams(vmem_limit_bytes=mib << 20),
    )(*operands)


def exchange(value, axes):
    return lax.all_to_all(value, axes, 0, 0, tiled=True)


def local(segments, stress, drag_coef, send_ids, partner_ids):
    core = lax.axis_index("c")
    y_index = lax.axis_index("y")
    x_index = lax.axis_index("x")
    chip_index = y_index * NZ + lax.axis_index("z")
    raw, to_z = call(
        pack_kernel,
        "pack",
        (
            segments.transpose(1, 0, 2),
            drag_coef,
            send_ids.reshape(1, SEG),
            partner_ids.reshape(1, SEG),
        ),
        [shape(24, SEG), shape(NZ, 24, SEG)],
    )
    along_z = exchange(to_z, "z")
    group = [raw] + [
        lax.ppermute(raw, "x", [(i, (i + shift) % NX) for i in range(NX)])
        for shift in range(1, NX)
    ]
    chip = lax.all_gather(raw, "c", axis=0)
    everyone = exchange(
        jnp.broadcast_to(along_z.reshape(1, NZ * 24, SEG), (NY, NZ * 24, SEG)), "y"
    ).reshape(NDEV, 24, SEG)

    lists = everyone[:, 14:16].reshape(2 * NDEV, SEG)
    lane = lax.broadcasted_iota(jnp.int32, (NC, SEG), 1)
    side = lax.broadcasted_iota(jnp.int32, (NC, SEG), 0)
    even = lax.bitwise_and(lane, SEG - 2)
    pick = (lane == 2 * chip_index + side).astype(F32)
    incoming = lax.dot_general(
        pick, lists, (((1,), (1,)), ((), ())), precision=lax.Precision.HIGHEST
    ).astype(jnp.int32)
    partner = jnp.concatenate([incoming[:, 1:], incoming[:, :1]], axis=1)
    into = jnp.where(incoming >= 0, even + incoming + 256 * (2 * side + partner), -1)
    sent = chip[:, 14].astype(jnp.int32)
    other = chip[:, 15].astype(jnp.int32)
    out = jnp.where(sent >= 0, even + other + 256 * (2 * side + sent), -1)
    first = lane[0:1]
    where = jnp.where(first == 0, core, jnp.where(first == 1, y_index, x_index))
    zero = jnp.zeros((1, SEG), jnp.int32)
    codes = jnp.concatenate([into, out, zero, zero, where, zero], axis=0)

    force, items, count = call(
        first_kernel,
        "first_pairs",
        (codes, everyone, *group, chip),
        [
            shape(NC, 8, SEG),
            shape(1, LIST, dtype=jnp.int32),
            shape(1, 1, dtype=jnp.int32),
        ],
        smem_in=1,
        smem_out=2,
        scratch=SCRATCH,
        mib=16,
    )
    chip_vel, to_near = call(
        functools.partial(finish_kernel, False),
        "finish",
        (codes, stress, lax.all_gather(force, "c", axis=0), chip, chip),
        [shape(NC, 8, SEG), shape(NY * NX, 8, SEG)],
        smem_in=2,
    )
    near = exchange(to_near, ("y", "x")).reshape(NY, NX, 8, SEG)
    (to_z,) = call(relay_kernel, "relay", (codes, near), [shape(NZ, NY, 8, SEG)], smem_in=1)
    vel_all = exchange(to_z.reshape(NZ, NY * 8, SEG), "z").reshape(NZ, NY, 8, SEG)

    force, position = call(
        second_kernel,
        "second_pairs",
        (codes, items, count, everyone, *group, chip, vel_all, near, chip_vel),
        [shape(NC, 8, SEG), shape(NC, 8, SEG)],
        smem_in=3,
        scratch=SCRATCH,
        mib=16,
    )
    chip_vel, to_z = call(
        functools.partial(finish_kernel, True),
        "finish_last",
        (codes, stress, lax.all_gather(force, "c", axis=0), chip, position),
        [shape(NC, 8, SEG), shape(NZ, 1, SEG)],
        smem_in=2,
    )
    top_z = jnp.max(exchange(to_z, "z"), axis=0)
    tops = exchange(jnp.broadcast_to(top_z[None], (NY * NX, 1, SEG)), ("y", "x"))
    positions, velocity = call(
        last_kernel,
        "last",
        (codes, tops, position, chip_vel),
        [shape(3, 2, SEG), shape(3, 2, SEG)],
        smem_in=1,
    )
    return positions.transpose(1, 0, 2), velocity.transpose(1, 0, 2)


def solution(mesh):
    split = Mesh(
        mesh.devices.reshape(NY, NZ, NC, mesh.shape["sub"]), ("y", "z", "c", "x")
    )
    return jax.shard_map(
        local,
        mesh=split,
        in_specs=(
            P(DOM_SUB, None, None),
            P(),
            P(DOM_SUB, None),
            P(DOM_SUB, None, None),
            P(DOM_SUB, None, None),
        ),
        out_specs=(P(DOM_SUB, None, None), P(DOM_SUB, None, None)),
        check_vma=False,
    )
```

time: 170 us -> 140 us (0.82)
  blocking collectives: 96.9 us -> 81.2 us
  starting transfers between devices: 17.7 us -> 30.5 us
  waiting for transfers between devices: 16.2 us -> 3.72 us
  Pallas kernels: 26.7 us -> 19.9 us
  local copies, waits for them, and re-layouts: 8.92 us -> 2.52 us
    all_to_all x3 -> x2, waiting for transfers between devices: 16.2 us -> 3.71 us  [exchange(): return lax.all_to_all(value, axes, 0, 0, tiled=True)]
    all_to_all x5 -> x4, blocking collectives: 72.4 us -> 60.1 us  [exchange(): return lax.all_to_all(value, axes, 0, 0, tiled=True)]
    ppermute x0 -> x3, starting transfers between devices: none -> 10.5 us  [local(): lax.ppermute(raw, 'x', [(i, (i + shift) % NX) for i in range(NX)])]
    pallas_call x5 -> x7, Pallas kernels: 26.7 us -> 19.9 us  [call(): pl.pallas_call(kernel, name=name, in_specs=[SMEM] * smem_in + [VMEM] * (l...]
    all_gather x2, blocking collectives: 17.8 us -> 14.5 us  [local(): lax.all_gather(force, 'c', axis=0)]
    broadcast_in_dim x9 -> x2, local copies, waits for them, and re-layouts: 3.67 us -> 0.96 us  [the longest x1 0.95 us: local(): jnp.broadcast_to(along_z.reshape(1, NZ * 24, SEG), (NY, NZ * 24, SEG))]
    all_to_all x3 -> x2, starting transfers between devices: 17.7 us -> 19.9 us  [exchange(): return lax.all_to_all(value, axes, 0, 0, tiled=True)]
    pallas_call x2 -> x0, local copies, waits for them, and re-layouts: 1.84 us -> none  [local(): pl.pallas_call(last_kernel, name='last', in_specs=[SMEM, VMEM, VMEM, VMEM...]
  transfers between devices with their start and end apart: 3 -> 5, of which waited for: 3 -> 2; matrix products, arithmetic and copies ran while one was open for 1% -> 1% of each run, Pallas kernels for 0% -> 0%
where the time goes in v2:
time: 140 us; the launch traced here: 139 us
  blocking collectives  81.2 us (58%)
  starting transfers between devices  30.5 us (22%)
  Pallas kernels  19.9 us (14%)
  waiting for transfers between devices  3.72 us (3%)
  local copies, waits for them, and re-layouts  2.52 us (2%)
    all_to_all x4, blocking collectives, exchange(): return lax.all_to_all(value, axes, 0, 0, tiled=True)  60.1 us
    all_to_all x2, starting transfers between devices, exchange(): return lax.all_to_all(value, axes, 0, 0, tiled=True)  19.9 us
    pallas_call x7, Pallas kernels, call(): pl.pallas_call(kernel, name=name, in_specs=[SMEM] * smem_in + [VMEM] * (l...  19.9 us
    all_gather x2, blocking collectives, local(): lax.all_gather(force, 'c', axis=0)  14.5 us
    ppermute x3, starting transfers between devices, local(): lax.ppermute(raw, 'x', [(i, (i + shift) % NX) for i in range(NX)])  10.5 us
    all_gather x1, blocking collectives, local(): chip = lax.all_gather(raw, 'c', axis=0)  6.59 us
    all_to_all x2, waiting for transfers between devices, exchange(): return lax.all_to_all(value, axes, 0, 0, tiled=True)  3.71 us
  transfers between devices with their start and end apart: 5, of which 2 were waited for; matrix products, arithmetic and copies ran while one was open for 1% of the time, Pallas kernels for 0%

profile of v2, /device:TPU:1, one launch (start us, length us, event | category | flops | bytes accessed | tf_op | source)
XLA Modules:
  0.0 138.9 jit_solution(17468564582510984265)
XLA Ops:
  0.7 0.6 copy-done.4
  1.3 0.7 copy-done
  2.0 0.7 pack.1
  2.7 15.7 %all-to-all-start = ((f32[16,24,128]{2,1,0:T(8,128)}), f32[16,24,128]{2,1,0:T(8,128)S(1)}, u32[]{:S(2)}, u32[]{:S(2)}) async-start(f32[16,24,128]{2,1,0:T(8,128)} %get-tuple-element.15), calls=%async_computation | async-start | bytes 393216 | tf_op jit(solution)/shard_map/all_to_all | solution.py:390
  18.5 3.1 %collective-permute-start = (f32[24,128]{1,0:T(8,128)S(1)}, f32[24,128]{1,0:T(8,128)S(1)}, u32[]{:S(2)}, u32[]{:S(2)}) collective-permute-start(f32[24,128]{1,0:T(8,128)S(1)} %get-tuple-element.16.g0), channel_id=1, source_target_pairs={{0,1},{1,2},{2,3},{3,0},{4,5},{5,6},{6,7},{7,4},{8,9},{9,10},{10,1... | collective-permute-start | bytes 36872 | tf_op jit(solution)/shard_map/ppermute | solution.py:411
  21.6 4.4 %collective-permute-start.1 = (f32[24,128]{1,0:T(8,128)S(1)}, f32[24,128]{1,0:T(8,128)S(1)}, u32[]{:S(2)}, u32[]{:S(2)}) collective-permute-start(f32[24,128]{1,0:T(8,128)S(1)} %get-tuple-element.16.g0), channel_id=1, source_target_pairs={{0,2},{1,3},{2,0},{3,1},{4,6},{5,7},{6,4},{7,5},{8,10},{9,11},{10,... | collective-permute-start | bytes 36872 | tf_op jit(solution)/shard_map/ppermute | solution.py:411
  26.0 3.1 %collective-permute-start.2 = (f32[24,128]{1,0:T(8,128)S(1)}, f32[24,128]{1,0:T(8,128)S(1)}, u32[]{:S(2)}, u32[]{:S(2)}) collective-permute-start(f32[24,128]{1,0:T(8,128)S(1)} %get-tuple-element.16.g0), channel_id=1, source_target_pairs={{0,3},{1,0},{2,1},{3,2},{4,7},{5,4},{6,5},{7,6},{8,11},{9,8},{10,9... | collective-permute-start | bytes 36872 | tf_op jit(solution)/shard_map/ppermute | solution.py:411
  29.0 2.0 %all-to-all-done = f32[16,24,128]{2,1,0:T(8,128)S(1)} async-done(((f32[16,24,128]{2,1,0:T(8,128)}), f32[16,24,128]{2,1,0:T(8,128)S(1)}, u32[]{:S(2)}, u32[]{:S(2)}) %all-to-all-start) | async-done | bytes 196640 | tf_op jit(solution)/shard_map/all_to_all | solution.py:390
  31.0 0.9 broadcast_in_dim.31
  32.0 4.2 %all-to-all-start.1 = ((f32[4,384,128]{2,1,0:T(8,128)}), f32[4,384,128]{2,1,0:T(8,128)S(1)}, u32[]{:S(2)}, u32[]{:S(2)}) async-start(f32[4,384,128]{2,1,0:T(8,128)} %broadcast_in_dim.31), calls=%async_computation.1 | async-start | bytes 1572864 | tf_op jit(solution)/shard_map/all_to_all | solution.py:390
  36.2 6.6 %all-gather = f32[48,128]{1,0:T(8,128)S(1)} all-gather(f32[24,128]{1,0:T(8,128)S(1)} %get-tuple-element.16.g0), channel_id=2, replica_groups=mesh['y'=4,'z'=16,'c'=2,'x'=4] {'c'}, dimensions={0}, use_global_device_ids=true | all-gather | bytes 36864 | tf_op jit(solution)/shard_map/all_gather | solution.py:414
  42.8 1.7 %all-to-all-done.1 = f32[4,384,128]{2,1,0:T(8,128)S(1)} async-done(((f32[4,384,128]{2,1,0:T(8,128)}), f32[4,384,128]{2,1,0:T(8,128)S(1)}, u32[]{:S(2)}, u32[]{:S(2)}) %all-to-all-start.1) | async-done | bytes 786464 | tf_op jit(solution)/shard_map/all_to_all | solution.py:390
  45.0 8.2 %first_pairs.1 = (f32[2,8,128]{2,1,0:T(8,128)S(1)}, s32[1,320]{1,0:T(1,128)S(1)}, s32[1,1]{1,0:T(1,128)}) custom-call(s32[8,128]{1,0:T(8,128)S(1)} %concatenate.7.codes_ref, f32[64,24,128]{2,1,0:T(8,128)S(1)} %bitcast.32, f32[24,128]{1,0:T(8,128)S(1)} %get-tuple-element.16.g0, f32[24,128]{1,0:T(8,128)S(1)} %collective-permute-done.g1, ...), custom_call_target="tpu_custom_call" | custom-call | tf_op jit(solution)/shard_map/first_pairs/pallas_call | solution.py:378
  53.2 7.0 %all-gather.1 = f32[4,8,128]{2,1,0:T(8,128)S(1)} all-gather(f32[2,8,128]{2,1,0:T(8,128)S(1)} %get-tuple-element.19), channel_id=3, replica_groups=mesh['y'=4,'z'=16,'c'=2,'x'=4] {'c'}, dimensions={0}, use_global_device_ids=true | all-gather | bytes 24576 | tf_op jit(solution)/shard_map/all_gather | solution.py:454
  60.2 0.7 finish.1
  60.9 12.4 %all_to_all.30 = f32[16,8,128]{2,1,0:T(8,128)S(1)} all-to-all(f32[16,8,128]{2,1,0:T(8,128)S(1)} %get-tuple-element.20), channel_id=1, replica_groups=mesh['y'=4,'z'=16,'c'=2,'x'=4] {'y','x'}, dimensions={0} | all-to-all | bytes 131072 | tf_op jit(solution)/shard_map/all_to_all | solution.py:390
  73.3 0.6 relay.1
  73.9 19.7 %all_to_all.31 = f32[16,32,128]{2,1,0:T(8,128)S(1)} all-to-all(f32[16,32,128]{2,1,0:T(8,128)S(1)} %bitcast.34), channel_id=1, replica_groups=mesh['y'=4,'z'=16,'c'=2,'x'=4] {'z'}, dimensions={0} | all-to-all | bytes 524288 | tf_op jit(solution)/shard_map/all_to_all | solution.py:390
  93.6 7.6 %second_pairs.1 = (f32[2,8,128]{2,1,0:T(8,128)S(1)}, f32[2,8,128]{2,1,0:T(8,128)S(1)}) custom-call(s32[8,128]{1,0:T(8,128)S(1)} %concatenate.7.codes_ref, s32[1,320]{1,0:T(1,128)S(1)} %get-tuple-element.17.list_ref, s32[1,1]{1,0:T(1,128)} %get-tuple-element.18.count_ref, f32[64,24,128]{2,1,0:T(8,128)S(1)} %bitcast.33, f32[24,128]{1,0:T(8,128)S(1)} %get-tuple-element.16.g0, ...), custom_call_target="tpu_custom_call" | custom-call | tf_op jit(solution)/shard_map/second_pairs/pallas_call | solution.py:378
  101.3 7.6 %all-gather.2 = f32[4,8,128]{2,1,0:T(8,128)S(1)} all-gather(f32[2,8,128]{2,1,0:T(8,128)S(1)} %get-tuple-element.22), channel_id=4, replica_groups=mesh['y'=4,'z'=16,'c'=2,'x'=4] {'c'}, dimensions={0}, use_global_device_ids=true | all-gather | bytes 24576 | tf_op jit(solution)/shard_map/all_gather | solution.py:474
  108.8 0.7 finish_last.1
  109.5 17.9 %all_to_all.32 = f32[16,1,128]{2,1,0:T(1,128)S(1)} all-to-all(f32[16,1,128]{2,1,0:T(1,128)S(1)} %get-tuple-element.24), channel_id=1, replica_groups=mesh['y'=4,'z'=16,'c'=2,'x'=4] {'z'}, dimensions={0} | all-to-all | bytes 16384 | tf_op jit(solution)/shard_map/all_to_all | solution.py:390
  127.4 10.2 %all_to_all.33.top_ref = f32[16,1,128]{2,1,0:T(1,128)S(1)} all-to-all(f32[16,1,128]{2,1,0:T(1,128)S(1)} %broadcast_in_dim.36), channel_id=1, replica_groups=mesh['y'=4,'z'=16,'c'=2,'x'=4] {'y','x'}, dimensions={0} | all-to-all | bytes 16384 | tf_op jit(solution)/shard_map/all_to_all | solution.py:390
  137.6 1.3 last.1
  (25 shorter events, 0.5 us)
Async XLA Ops:
  0.6 0.7 copy-start.4
  0.6 0.7 copy-start.2
  0.7 0.7 copy-start.3
  1.3 0.7 copy-start
  2.7 28.3 %all-to-all-start = ((f32[16,24,128]{2,1,0:T(8,128)}), f32[16,24,128]{2,1,0:T(8,128)S(1)}, u32[]{:S(2)}, u32[]{:S(2)}) async-start(f32[16,24,128]{2,1,0:T(8,128)} %get-tuple-element.15), calls=%async_computation | async-start | bytes 393216 | tf_op jit(solution)/shard_map/all_to_all | solution.py:390
  18.5 26.5 %collective-permute-start = (f32[24,128]{1,0:T(8,128)S(1)}, f32[24,128]{1,0:T(8,128)S(1)}, u32[]{:S(2)}, u32[]{:S(2)}) collective-permute-start(f32[24,128]{1,0:T(8,128)S(1)} %get-tuple-element.16.g0), channel_id=1, source_target_pairs={{0,1},{1,2},{2,3},{3,0},{4,5},{5,6},{6,7},{7,4},{8,9},{9,10},{10,1... | collective-permute-start | bytes 36872 | tf_op jit(solution)/shard_map/ppermute | solution.py:411
  21.6 23.3 %collective-permute-start.1 = (f32[24,128]{1,0:T(8,128)S(1)}, f32[24,128]{1,0:T(8,128)S(1)}, u32[]{:S(2)}, u32[]{:S(2)}) collective-permute-start(f32[24,128]{1,0:T(8,128)S(1)} %get-tuple-element.16.g0), channel_id=1, source_target_pairs={{0,2},{1,3},{2,0},{3,1},{4,6},{5,7},{6,4},{7,5},{8,10},{9,11},{10,... | collective-permute-start | bytes 36872 | tf_op jit(solution)/shard_map/ppermute | solution.py:411
  26.0 19.0 %collective-permute-start.2 = (f32[24,128]{1,0:T(8,128)S(1)}, f32[24,128]{1,0:T(8,128)S(1)}, u32[]{:S(2)}, u32[]{:S(2)}) collective-permute-start(f32[24,128]{1,0:T(8,128)S(1)} %get-tuple-element.16.g0), channel_id=1, source_target_pairs={{0,3},{1,0},{2,1},{3,2},{4,7},{5,4},{6,5},{7,6},{8,11},{9,8},{10,9... | collective-permute-start | bytes 36872 | tf_op jit(solution)/shard_map/ppermute | solution.py:411
  32.0 12.5 %all-to-all-start.1 = ((f32[4,384,128]{2,1,0:T(8,128)}), f32[4,384,128]{2,1,0:T(8,128)S(1)}, u32[]{:S(2)}, u32[]{:S(2)}) async-start(f32[4,384,128]{2,1,0:T(8,128)} %broadcast_in_dim.31), calls=%async_computation.1 | async-start | bytes 1572864 | tf_op jit(solution)/shard_map/all_to_all | solution.py:390
  45.0 15.2 %copy-start.1 = (f32[3,3]{1,0:T(4,128)S(1)}, f32[3,3]{1,0:T(4,128)}, u32[]{:S(2)}) copy-start(f32[3,3]{1,0:T(4,128)} %stress_ref.3) | copy-start | bytes 112

commit v3 on v2

--- a/solution.py
+++ b/solution.py
@@ -248,11 +248,10 @@
     chip_x_ref,
     *scratch,
 ):
-    y_index = codes_ref[6, 1]
     x_index = codes_ref[6, 2]
-    top = vel_ref[0, 0]
-    for z in range(1, NZ):
-        top = jnp.maximum(top, vel_ref[z, 0])
+    top = vel_ref[0]
+    for k in range(1, NDEV):
+        top = jnp.maximum(top, vel_ref[k])
     top = jnp.max(top[6:7], axis=1, keepdims=True)
     step = STEP_LENGTH / (jnp.sqrt(top) + EPSILON)
     row = sublane()
@@ -264,10 +263,10 @@
                 return no_source()
             shift = k - NDEV
             x_tile, l_tile, b_tile = tiles_of(group[shift])
-            moved = near_ref[y_index, lax.bitwise_and(x_index - shift, NX - 1)]
+            moved = near_ref[lax.bitwise_and(x_index - shift, NX - 1)]
         else:
             x_tile, l_tile, b_tile = tiles_of(all_ref.at[k])
-            moved = vel_ref[lax.bitwise_and(k, NZ - 1), lax.shift_right_logical(k, 4)]
+            moved = vel_ref[k]
         return x_tile + step * moved, l_tile, b_tile
 
     for side in range(NC):
@@ -320,11 +319,10 @@
     for side in range(NC):
         vel_ref[side] = jnp.where(row < 6, tiles[side], jnp.where(row == 6, top, 0.0))
     if last:
-        for peer in range(NZ):
-            out_ref[peer] = top
+        out_ref[...] = jnp.broadcast_to(top[None], out_ref.shape)
     else:
         mine = vel_ref[core]
-        for peer in range(NY * NX):
+        for peer in range(NX):
             out_ref[peer] = mine
 
 
@@ -344,14 +342,12 @@
 
 def relay_kernel(codes_ref, near_ref, out_ref):
     x_index = codes_ref[6, 2]
-    top = near_ref[0, 0]
-    for at in range(1, NY * NX):
-        top = jnp.maximum(top, near_ref[at // NX, at % NX])
-    row = sublane()
-    for y in range(NY):
-        tile = jnp.where(row == 6, top, near_ref[y, x_index])
-        for peer in range(NZ):
-            out_ref[peer, y] = tile
+    top = near_ref[0]
+    for x in range(1, NX):
+        top = jnp.maximum(top, near_ref[x])
+    tile = jnp.where(sublane() == 6, top, near_ref[x_index])
+    for peer in range(NZ):
+        out_ref[peer] = tile
 
 
 def last_kernel(codes_ref, top_ref, x_ref, vel_ref, pos_out, vel_out):
@@ -384,6 +380,10 @@
         scratch_shapes=scratch,
         compiler_params=pltpu.CompilerParams(vmem_limit_bytes=mib << 20),
     )(*operands)
+
+
+def pass_x(value, shift):
+    return lax.ppermute(value, "x", [(i, (i + shift) % NX) for i in range(NX)])
 
 
 def exchange(value, axes):
@@ -405,13 +405,13 @@
             partner_ids.reshape(1, SEG),
         ),
         [shape(24, SEG), shape(NZ, 24, SEG)],
+        mib=56,
     )
     along_z = exchange(to_z, "z")
-    group = [raw] + [
-        lax.ppermute(raw, "x", [(i, (i + shift) % NX) for i in range(NX)])
-        for shift in range(1, NX)
-    ]
     chip = lax.all_gather(raw, "c", axis=0)
+    near1 = pass_x(raw, 1)
+    along_z, chip, near1, raw = lax.optimization_barrier((along_z, chip, near1, raw))
+    group = [raw, near1, pass_x(raw, 2), pass_x(raw, 3)]
     everyone = exchange(
         jnp.broadcast_to(along_z.reshape(1, NZ * 24, SEG), (NY, NZ * 24, SEG)), "y"
     ).reshape(NDEV, 24, SEG)
@@ -452,12 +452,13 @@
         functools.partial(finish_kernel, False),
         "finish",
         (codes, stress, lax.all_gather(force, "c", axis=0), chip, chip),
-        [shape(NC, 8, SEG), shape(NY * NX, 8, SEG)],
+        [shape(NC, 8, SEG), shape(NX, 8, SEG)],
         smem_in=2,
     )
-    near = exchange(to_near, ("y", "x")).reshape(NY, NX, 8, SEG)
-    (to_z,) = call(relay_kernel, "relay", (codes, near), [shape(NZ, NY, 8, SEG)], smem_in=1)
-    vel_all = exchange(to_z.reshape(NZ, NY * 8, SEG), "z").reshape(NZ, NY, 8, SEG)
+    near = exchange(to_near, "x")
+    (to_z,) = call(relay_kernel, "relay", (codes, near), [shape(NZ, 8, SEG)], smem_in=1)
+    along_z = exchange(to_z, "z").reshape(1, NZ * 8, SEG)
+    vel_all = exchange(jnp.broadcast_to(along_z, (NY, NZ * 8, SEG)), "y").reshape(NDEV, 8, SEG)
 
     force, position = call(
         second_kernel,
@@ -468,15 +469,14 @@
         scratch=SCRATCH,
         mib=16,
     )
-    chip_vel, to_z = call(
+    chip_vel, to_all = call(
         functools.partial(finish_kernel, True),
         "finish_last",
         (codes, stress, lax.all_gather(force, "c", axis=0), chip, position),
-        [shape(NC, 8, SEG), shape(NZ, 1, SEG)],
+        [shape(NC, 8, SEG), shape(NDEV * NX, 1, SEG)],
         smem_in=2,
     )
-    top_z = jnp.max(exchange(to_z, "z"), axis=0)
-    tops = exchange(jnp.broadcast_to(top_z[None], (NY * NX, 1, SEG)), ("y", "x"))
+    tops = exchange(to_all, ("y", "z", "x"))
     positions, velocity = call(
         last_kernel,
         "last",

time: 140 us -> 142 us (1.014)
  waiting for transfers between devices: 3.72 us -> 8.18 us
  blocking collectives: 81.2 us -> 79.3 us
    all_gather x1, blocking collectives: 6.59 us -> 2.73 us  [local(): chip = lax.all_gather(raw, 'c', axis=0)]
    all_to_all x2, waiting for transfers between devices: 3.71 us -> 7.54 us  [exchange(): return lax.all_to_all(value, axes, 0, 0, tiled=True)]
    all_to_all x4, blocking collectives: 60.1 us -> 62.6 us  [exchange(): return lax.all_to_all(value, axes, 0, 0, tiled=True)]
  transfers between devices with their start and end apart: 5 -> 5, of which waited for: 2 -> 3; matrix products, arithmetic and copies ran while one was open for 1% -> 0% of each run, Pallas kernels for 0% -> 0%
where the time goes in v3:
time: 142 us; the launch traced here: 141 us
  blocking collectives  79.3 us (56%)
  starting transfers between devices  30.6 us (22%)
  Pallas kernels  20.8 us (15%)
  waiting for transfers between devices  8.18 us (6%)
    all_to_all x4, blocking collectives, exchange(): return lax.all_to_all(value, axes, 0, 0, tiled=True)  62.6 us
    pallas_call x7, Pallas kernels, call(): pl.pallas_call(kernel, name=name, in_specs=[SMEM] * smem_in + [VMEM] * (l...  20.8 us
    all_to_all x2, starting transfers between devices, exchange(): return lax.all_to_all(value, axes, 0, 0, tiled=True)  20.1 us
    all_gather x2, blocking collectives, local(): lax.all_gather(force, 'c', axis=0)  13.9 us
    ppermute x3, starting transfers between devices, pass_x(): return lax.ppermute(value, 'x', [(i, (i + shift) % NX) for i in range(NX)])  10.5 us
    all_to_all x2, waiting for transfers between devices, exchange(): return lax.all_to_all(value, axes, 0, 0, tiled=True)  7.54 us
  transfers between devices with their start and end apart: 5, of which 3 were waited for; matrix products, arithmetic and copies ran while one was open for 0% of the time, Pallas kernels for 0%

profile of v3, /device:TPU:1, one launch (start us, length us, event | category | flops | bytes accessed | tf_op | source)
XLA Modules:
  0.0 141.1 jit_solution(10570462083754836138)
XLA Ops:
  0.6 1.4 %pack.1 = (f32[24,128]{1,0:T(8,128)}, f32[16,24,128]{2,1,0:T(8,128)}) custom-call(f32[9,2,128]{2,1,0:T(2,128)} %bitcast.43, f32[2,128]{1,0:T(2,128)} %drag_ref.1, s32[1,128]{1,0:T(1,128)} %bitcast.44, s32[1,128]{1,0:T(1,128)} %bitcast.45), custom_call_target="tpu_custom_call" | custom-call | tf_op jit(solution)/shard_map/pack/pallas_call | solution.py:374
  2.1 15.9 %all-to-all-start = ((f32[16,24,128]{2,1,0:T(8,128)}), f32[16,24,128]{2,1,0:T(8,128)S(1)}, u32[]{:S(2)}, u32[]{:S(2)}) async-start(f32[16,24,128]{2,1,0:T(8,128)} %get-tuple-element.19), calls=%async_computation | async-start | bytes 393216 | tf_op jit(solution)/shard_map/all_to_all | solution.py:390
  18.0 3.1 %collective-permute-start = (f32[24,128]{1,0:T(8,128)S(1)}, f32[24,128]{1,0:T(8,128)S(1)}, u32[]{:S(2)}, u32[]{:S(2)}) collective-permute-start(f32[24,128]{1,0:T(8,128)S(1)} %copy-done), channel_id=1, source_target_pairs={{0,1},{1,2},{2,3},{3,0},{4,5},{5,6},{6,7},{7,4},{8,9},{9,10},{10,1... | collective-permute-start | bytes 36872 | tf_op jit(solution)/shard_map/ppermute | solution.py:386
  21.1 2.7 %all-gather = f32[48,128]{1,0:T(8,128)S(1)} all-gather(f32[24,128]{1,0:T(8,128)S(1)} %copy-done), channel_id=2, replica_groups=mesh['y'=4,'z'=16,'c'=2,'x'=4] {'c'}, dimensions={0}, use_global_device_ids=true | all-gather | bytes 36864 | tf_op jit(solution)/shard_map/all_gather | solution.py:411
  23.8 6.7 %all-to-all-done = f32[16,24,128]{2,1,0:T(8,128)S(1)} async-done(((f32[16,24,128]{2,1,0:T(8,128)}), f32[16,24,128]{2,1,0:T(8,128)S(1)}, u32[]{:S(2)}, u32[]{:S(2)}) %all-to-all-start) | async-done | bytes 196640 | tf_op jit(solution)/shard_map/all_to_all | solution.py:390
  30.5 1.0 broadcast_in_dim.32
  31.5 4.2 %all-to-all-start.1 = ((f32[4,384,128]{2,1,0:T(8,128)}), f32[4,384,128]{2,1,0:T(8,128)S(1)}, u32[]{:S(2)}, u32[]{:S(2)}) async-start(f32[4,384,128]{2,1,0:T(8,128)} %broadcast_in_dim.32), calls=%async_computation.1 | async-start | bytes 1572864 | tf_op jit(solution)/shard_map/all_to_all | solution.py:390
  35.7 4.7 %collective-permute-start.1 = (f32[24,128]{1,0:T(8,128)S(1)}, f32[24,128]{1,0:T(8,128)S(1)}, u32[]{:S(2)}, u32[]{:S(2)}) collective-permute-start(f32[24,128]{1,0:T(8,128)S(1)} %copy-done), channel_id=1, source_target_pairs={{0,2},{1,3},{2,0},{3,1},{4,6},{5,7},{6,4},{7,5},{8,10},{9,11},{10,... | collective-permute-start | bytes 36872 | tf_op jit(solution)/shard_map/ppermute | solution.py:386
  40.3 2.8 %collective-permute-start.2 = (f32[24,128]{1,0:T(8,128)S(1)}, f32[24,128]{1,0:T(8,128)S(1)}, u32[]{:S(2)}, u32[]{:S(2)}) collective-permute-start(f32[24,128]{1,0:T(8,128)S(1)} %copy-done), channel_id=1, source_target_pairs={{0,3},{1,0},{2,1},{3,2},{4,7},{5,4},{6,5},{7,6},{8,11},{9,8},{10,9... | collective-permute-start | bytes 36872 | tf_op jit(solution)/shard_map/ppermute | solution.py:386
  43.1 0.8 all-to-all-done.1
  44.0 0.2 convolution_convert_fusion
  44.4 0.6 collective-permute-done.2.g3
  45.1 8.2 %first_pairs.1 = (f32[2,8,128]{2,1,0:T(8,128)S(1)}, s32[1,320]{1,0:T(1,128)S(1)}, s32[1,1]{1,0:T(1,128)}) custom-call(s32[8,128]{1,0:T(8,128)S(1)} %concatenate.7.codes_ref, f32[64,24,128]{2,1,0:T(8,128)S(1)} %bitcast.28, f32[24,128]{1,0:T(8,128)S(1)} %copy-done, f32[24,128]{1,0:T(8,128)S(1)} %collective-permute-done.g1, ...), custom_call_target="tpu_custom_call" | custom-call | tf_op jit(solution)/shard_map/first_pairs/pallas_call | solution.py:374
  53.3 7.7 %all-gather.1 = f32[4,8,128]{2,1,0:T(8,128)S(1)} all-gather(f32[2,8,128]{2,1,0:T(8,128)S(1)} %get-tuple-element.27), channel_id=3, replica_groups=mesh['y'=4,'z'=16,'c'=2,'x'=4] {'c'}, dimensions={0}, use_global_device_ids=true | all-gather | bytes 24576 | tf_op jit(solution)/shard_map/all_gather | solution.py:454
  61.0 0.7 finish.1
  61.8 7.4 %all_to_all.30.near_ref = f32[4,8,128]{2,1,0:T(8,128)S(1)} all-to-all(f32[4,8,128]{2,1,0:T(8,128)S(1)} %get-tuple-element.28), channel_id=1, replica_groups=mesh['y'=4,'z'=16,'c'=2,'x'=4] {'x'}, dimensions={0} | all-to-all | bytes 32768 | tf_op jit(solution)/shard_map/all_to_all | solution.py:390
  69.2 0.6 relay.1
  69.8 18.8 %all_to_all.31 = f32[16,8,128]{2,1,0:T(8,128)S(1)} all-to-all(f32[16,8,128]{2,1,0:T(8,128)S(1)} %relay.1), channel_id=1, replica_groups=mesh['y'=4,'z'=16,'c'=2,'x'=4] {'z'}, dimensions={0} | all-to-all | bytes 131072 | tf_op jit(solution)/shard_map/all_to_all | solution.py:390
  88.6 9.1 %all_to_all.32 = f32[4,128,128]{2,1,0:T(8,128)S(1)} all-to-all(f32[4,128,128]{2,1,0:T(8,128)S(1)} %broadcast_in_dim.38), channel_id=1, replica_groups=mesh['y'=4,'z'=16,'c'=2,'x'=4] {'y'}, dimensions={0} | all-to-all | bytes 524288 | tf_op jit(solution)/shard_map/all_to_all | solution.py:390
  97.7 7.7 %second_pairs.1 = (f32[2,8,128]{2,1,0:T(8,128)S(1)}, f32[2,8,128]{2,1,0:T(8,128)S(1)}) custom-call(s32[8,128]{1,0:T(8,128)S(1)} %concatenate.7.codes_ref, s32[1,320]{1,0:T(1,128)S(1)} %get-tuple-element.25.list_ref, s32[1,1]{1,0:T(1,128)} %get-tuple-element.26.count_ref, f32[64,24,128]{2,1,0:T(8,128)S(1)} %bitcast.29, f32[24,128]{1,0:T(8,128)S(1)} %copy-done, ...), custom_call_target="tpu_custom_call" | custom-call | tf_op jit(solution)/shard_map/second_pairs/pallas_call | solution.py:374
  105.4 6.2 %all-gather.2 = f32[4,8,128]{2,1,0:T(8,128)S(1)} all-gather(f32[2,8,128]{2,1,0:T(8,128)S(1)} %get-tuple-element.30), channel_id=4, replica_groups=mesh['y'=4,'z'=16,'c'=2,'x'=4] {'c'}, dimensions={0}, use_global_device_ids=true | all-gather | bytes 24576 | tf_op jit(solution)/shard_map/all_gather | solution.py:475
  111.6 0.8 finish_last.1
  112.4 27.3 %all_to_all.33.top_ref = f32[256,1,128]{2,1,0:T(1,128)S(1)} all-to-all(f32[256,1,128]{2,1,0:T(1,128)S(1)} %get-tuple-element.32), channel_id=1, replica_groups=mesh['y'=4,'z'=16,'c'=2,'x'=4] {'y','z','x'}, dimensions={0} | all-to-all | bytes 262144 | tf_op jit(solution)/shard_map/all_to_all | solution.py:390
  139.7 1.3 last.1
  (18 shorter events, 0.3 us)
Async XLA Ops:
  2.1 15.9 %copy-start = (f32[24,128]{1,0:T(8,128)S(1)}, f32[24,128]{1,0:T(8,128)}, u32[]{:S(2)}) copy-start(f32[24,128]{1,0:T(8,128)} %get-tuple-element.23.g0) | copy-start | bytes 36868
  2.1 28.4 %all-to-all-start = ((f32[16,24,128]{2,1,0:T(8,128)}), f32[16,24,128]{2,1,0:T(8,128)S(1)}, u32[]{:S(2)}, u32[]{:S(2)}) async-start(f32[16,24,128]{2,1,0:T(8,128)} %get-tuple-element.19), calls=%async_computation | async-start | bytes 393216 | tf_op jit(solution)/shard_map/all_to_all | solution.py:390
  18.0 5.9 %collective-permute-start = (f32[24,128]{1,0:T(8,128)S(1)}, f32[24,128]{1,0:T(8,128)S(1)}, u32[]{:S(2)}, u32[]{:S(2)}) collective-permute-start(f32[24,128]{1,0:T(8,128)S(1)} %copy-done), channel_id=1, source_target_pairs={{0,1},{1,2},{2,3},{3,0},{4,5},{5,6},{6,7},{7,4},{8,9},{9,10},{10,1... | collective-permute-start | bytes 36872 | tf_op jit(solution)/shard_map/ppermute | solution.py:386
  31.5 12.5 %all-to-all-start.1 = ((f32[4,384,128]{2,1,0:T(8,128)}), f32[4,384,128]{2,1,0:T(8,128)S(1)}, u32[]{:S(2)}, u32[]{:S(2)}) async-start(f32[4,384,128]{2,1,0:T(8,128)} %broadcast_in_dim.32), calls=%async_computation.1 | async-start | bytes 1572864 | tf_op jit(solution)/shard_map/all_to_all | solution.py:390
  35.7 8.7 %collective-permute-start.1 = (f32[24,128]{1,0:T(8,128)S(1)}, f32[24,128]{1,0:T(8,128)S(1)}, u32[]{:S(2)}, u32[]{:S(2)}) collective-permute-start(f32[24,128]{1,0:T(8,128)S(1)} %copy-done), channel_id=1, source_target_pairs={{0,2},{1,3},{2,0},{3,1},{4,6},{5,7},{6,4},{7,5},{8,10},{9,11},{10,... | collective-permute-start | bytes 36872 | tf_op jit(solution)/shard_map/ppermute | solution.py:386
  40.3 4.7 %collective-permute-start.2 = (f32[24,128]{1,0:T(8,128)S(1)}, f32[24,128]{1,0:T(8,128)S(1)}, u32[]{:S(2)}, u32[]{:S(2)}) collective-permute-start(f32[24,128]{1,0:T(8,128)S(1)} %copy-done), channel_id=1, source_target_pairs={{0,3},{1,0},{2,1},{3,2},{4,7},{5,4},{6,5},{7,6},{8,11},{9,8},{10,9... | collective-permute-start | bytes 36872 | tf_op jit(solution)/shard_map/ppermute | solution.py:386
  45.1 16.0 %copy-start.1 = (f32[3,3]{1,0:T(4,128)S(1)}, f32[3,3]{1,0:T(4,128)}, u32[]{:S(2)}) copy-start(f32[3,3]{1,0:T(4,128)} %stress_ref.3) | copy-start | bytes 112

commit v4 on v3

v4 whole, which is shorter than its diff:
```python
import functools

import jax
import jax.numpy as jnp
from jax import lax
from jax.experimental import pallas as pl
from jax.experimental.pallas import tpu as pltpu
from jax.sharding import Mesh
from jax.sharding import PartitionSpec as P

NY, NZ, NC = 4, 16, 2
DOM = ("y", "z", "c")
DOM_SUB = ("y", "z", "c", "x")

COUPLE = 0.0625
CORE_SQUARE = 0.5
TENSION = 0.25
STEP_LENGTH = 1.0
EPSILON = 1e-06

SEG = 128
NT = NY * NC
NX = 4
BATCH = 16
LIST = 320
NONE = NZ + NX
F32 = jnp.float32
BF16 = jnp.bfloat16


def sublane(shape=(8, SEG)):
    return lax.broadcasted_iota(jnp.int32, shape, len(shape) - 2)


def up(value, count):
    return jnp.concatenate([value[count:], value[:count]], axis=0)


def split2(value):
    high = value.astype(BF16).astype(F32)
    return high, value - high


def split3(value):
    high, rest = split2(value)
    mid, low = split2(rest)
    return high, mid, low


def source_operands(x_tile, l_tile, b_tile):
    row = sublane()
    x_tile = jnp.where(row < 6, x_tile, 0.0)
    square = x_tile * x_tile
    norm0 = square[0:1] + square[1:2] + square[2:3] + CORE_SQUARE
    norm1 = square[3:4] + square[4:5] + square[5:6] + CORE_SQUARE
    full = jnp.where(row == 6, norm0, jnp.where(row == 7, norm1, x_tile))
    high, mid, low = split3(full)
    dist = [high, mid, high, mid, low, high, jnp.ones_like(high)]
    prod = [jnp.where(row < 3, b_tile[a : a + 1], b_tile[3 + a : 4 + a]) * l_tile for a in range(3)]
    parts = [split2(p) for p in prod]
    highs = [p[0] for p in parts]
    mids = [p[1] for p in parts]
    weight = highs + highs + mids
    flag = jnp.where(row == 6, 1.0, 0.0)
    first = (jnp.where(row < 6, high, flag), jnp.where(row < 6, mid, 0.0))
    second = (jnp.where(row < 3, up(high, 3), flag), jnp.where(row < 3, up(mid, 3), 0.0))
    return dist + weight, first, second


def store_rows(ref, index, tiles):
    for at in range(0, len(tiles), 2):
        pair = jnp.concatenate([tiles[at], tiles[at + 1]], axis=0).astype(BF16)
        ref[index, 8 * at : 8 * at + 16, :] = pair


def target_rows(x_tile, l_tile, b_tile, block):
    row = sublane()

    def both(tile):
        if block == 0:
            return jnp.where(row < 3, tile, jnp.where(row < 6, up(tile, 5), 0.0))
        return jnp.where(row < 3, up(tile, 3), jnp.where(row < 6, tile, 0.0))

    x_both = both(x_tile)
    high, mid, low = split3(x_both)
    square = x_both * x_both
    norm = square[0:1] + square[1:2] + square[2:3]
    norm_h, norm_m, norm_l = split3(norm)
    unit = jnp.where(row >= 6, 1.0, 0.0)
    norms = jnp.where(
        row == 0, norm_h, jnp.where(row == 1, norm_m, jnp.where(row == 2, norm_l, 0.0))
    )
    zero = jnp.zeros_like(high)
    dist = [
        -2.0 * high + unit,
        -2.0 * high + unit,
        -2.0 * mid,
        -2.0 * mid,
        -2.0 * high + unit,
        -2.0 * low,
        norms,
    ]
    l_both = both(l_tile)
    base = 3 * block
    prod = [b_tile[base + a : base + a + 1] * l_both for a in range(3)]
    parts = [split2(p) for p in prod]
    highs = [p[0] for p in parts]
    mids = [p[1] for p in parts]
    weight = highs + mids + highs
    return jnp.concatenate(dist + [zero] * 9, axis=0), jnp.concatenate([zero] * 7 + weight, axis=0)


def build_list(codes_ref, info_ref, list_ref, count_ref):
    core, y_index, z_index = info_ref[8, 0], info_ref[8, 1], info_ref[8, 2]
    from_here = 32 * y_index + core

    def add(z, count):
        for t in range(NT):
            for code in (
                codes_ref[z, 2 * z_index + (32 * (t // NC) + t % NC)],
                info_ref[t, 2 * z + from_here],
            ):
                list_ref[0, count] = code
                count = count + (code >= 0).astype(jnp.int32)
        return count

    count = lax.fori_loop(0, NZ, add, jnp.int32(0))
    mine = 2 * (NC * y_index + core)
    for block in range(2):
        for j in range(2 * NX):
            list_ref[0, count + 2 * NX * block + j] = 256 * (mine + block) + 2 * NZ + j
    count = count + 4 * NX
    for j in range(BATCH):
        list_ref[0, count + j] = 2 * NONE
    count_ref[0, 0] = lax.div(count + (BATCH - 1), BATCH)


def pair_body(
    list_ref, count_ref, get_source, get_target, force_ref, source_s, moment_s, target_s, total_s
):
    def prepare(k):
        tiles, first, second = source_operands(*get_source(k))
        store_rows(source_s, k, tiles)
        moment_s[2 * k] = jnp.concatenate(first, axis=0).astype(BF16)
        moment_s[2 * k + 1] = jnp.concatenate(second, axis=0).astype(BF16)

    def prepare_loop(k, carry):
        prepare(k)
        return carry

    lax.fori_loop(0, NZ, prepare_loop, 0, unroll=4)
    for k in range(NZ, NONE + 1):
        prepare(k)

    lane = lax.broadcasted_iota(jnp.int32, (SEG, SEG), 1)
    place = lax.bitwise_and(lane, 7)

    def target_loop(t, carry):
        x_tile, l_tile, b_tile = get_target(t)
        for block in range(2):
            dist, weight = target_rows(x_tile, l_tile, b_tile, block)
            dist = dist.T
            weight = weight.T
            for j in range(2):
                mine = (place >= 3 * j) & (place < 3 * j + 3)
                keep = mine | (place == 6 + j) | (lane >= 48)
                at = 4 * t + 2 * block + j
                target_s[at, 0:SEG] = jnp.where(keep, dist, 0.0).astype(BF16)
                target_s[at, SEG : 2 * SEG] = jnp.where(mine, weight, 0.0).astype(BF16)
        return carry

    lax.fori_loop(0, NT, target_loop, 0, unroll=2)
    total_s[...] = jnp.zeros_like(total_s)

    def items(step, carry):
        sums = []
        for b in range(BATCH):
            code = list_ref[0, step * BATCH + b]
            n = lax.shift_right_logical(code, 8)
            m = lax.bitwise_and(code, 255)
            at = 2 * n + lax.bitwise_and(m, 1)
            both = jnp.dot(
                target_s[at], source_s[lax.shift_right_logical(m, 1)], preferred_element_type=F32
            )
            inverse = lax.rsqrt(both[0:SEG])
            w = both[SEG : 2 * SEG] * (inverse * inverse * inverse)
            high = w.astype(BF16)
            low = (w - high.astype(F32)).astype(BF16)
            moment = moment_s[m]
            total = lax.dot_general(
                jnp.concatenate([moment, moment], axis=1),
                jnp.concatenate([high, low], axis=1),
                (((1,), (1,)), ((), ())),
                preferred_element_type=F32,
            )
            sums.append((n, total))
        for n, total in sums:
            total_s[n] += total
        return carry

    lax.fori_loop(0, count_ref[0, 0], items, 0)
    for t in range(NT):
        x_tile = get_target(t)[0]
        rows = []
        for block in range(2):
            total = total_s[2 * t + block]
            x_block = x_tile[3 * block : 3 * block + 3]
            rows.append(x_block * total[6:7] - (total[0:3] + total[8:11]))
        rows.append(jnp.zeros((2, SEG), F32))
        force = jnp.concatenate(rows, axis=0)
        for core in range(NC):
            force_ref[NC * (t // NC) + core, t % NC] = force


SCRATCH = [
    pltpu.VMEM((NONE + 1, SEG, SEG), BF16),
    pltpu.VMEM((2 * (NONE + 1), 16, SEG), BF16),
    pltpu.VMEM((4 * NT, 2 * SEG, SEG), BF16),
    pltpu.VMEM((2 * NT, 16, SEG), F32),
]


def tiles_of(tile):
    return tile[0:8], tile[8:16], tile[16:24]


def no_source():
    zero = jnp.zeros((8, SEG), F32)
    return zero, zero, zero


def first_kernel(
    codes_ref, info_ref, line_ref, group_ref, near_ref, force_ref, list_ref, count_ref, *scratch
):
    build_list(codes_ref, info_ref, list_ref, count_ref)

    def get_source(k):
        if isinstance(k, int):
            return no_source() if k == NONE else tiles_of(group_ref.at[k - NZ])
        return tiles_of(line_ref.at[k])

    def get_target(t):
        return tiles_of(near_ref.at[t])

    pair_body(list_ref, count_ref, get_source, get_target, force_ref, *scratch)


def second_kernel(
    info_ref,
    list_ref,
    count_ref,
    line_ref,
    group_ref,
    near_ref,
    vel_ref,
    near_vel_ref,
    force_ref,
    position_ref,
    *scratch,
):
    mine = NC * info_ref[8, 1] + info_ref[8, 0]
    x_index = info_ref[8, 3]
    top = vel_ref[0]
    for z in range(1, NZ):
        top = jnp.maximum(top, vel_ref[z])
    top = jnp.max(top[6:7], axis=1, keepdims=True)
    step = STEP_LENGTH / (jnp.sqrt(top) + EPSILON)

    def get_source(k):
        if isinstance(k, int):
            if k == NONE:
                return no_source()
            x_tile, l_tile, b_tile = tiles_of(group_ref.at[k - NZ])
            moved = near_vel_ref[mine, k - NZ]
        else:
            x_tile, l_tile, b_tile = tiles_of(line_ref.at[k])
            moved = vel_ref[k]
        return x_tile + step * moved, l_tile, b_tile

    def get_target(t):
        x_tile, l_tile, b_tile = tiles_of(near_ref.at[t])
        return x_tile + step * near_vel_ref[t, x_index], l_tile, b_tile

    for side in range(NC):
        at = NC * info_ref[8, 1] + side
        moved = jnp.where(sublane() < 6, near_vel_ref[at, x_index], 0.0)
        position_ref[side] = near_ref[at, 0:8] + step * moved
    pair_body(list_ref, count_ref, get_source, get_target, force_ref, *scratch)


def finish_kernel(info_ref, stress_ref, parts_ref, near_ref, x_ref, vel_ref, out_ref):
    core, y_index = info_ref[8, 0], info_ref[8, 1]
    row = sublane()
    lane = lax.broadcasted_iota(jnp.int32, (8, SEG), 1)
    tops = []
    for side in range(NC):
        at = NC * y_index + side
        x_tile = x_ref[at, 0:8] if x_ref.shape[0] == NT else x_ref[side]
        l_tile = near_ref[at, 8:16]
        b_tile = near_ref[at, 16:24]
        rows = []
        for block in range(2):
            b = [b_tile[3 * block + a : 3 * block + a + 1] for a in range(3)]
            line = [l_tile[3 * block + a : 3 * block + a + 1] for a in range(3)]
            pulled = [
                stress_ref[a, 0] * b[0] + stress_ref[a, 1] * b[1] + stress_ref[a, 2] * b[2]
                for a in range(3)
            ]
            rows.append(pulled[1] * line[2] - pulled[2] * line[1])
            rows.append(pulled[2] * line[0] - pulled[0] * line[2])
            rows.append(pulled[0] * line[1] - pulled[1] * line[0])
        rows.append(jnp.zeros((2, SEG), F32))
        applied = jnp.concatenate(rows, axis=0)
        left = jnp.where(lane == 0, x_tile, pltpu.roll(x_tile, 1, 1))
        right = jnp.where(lane == SEG - 1, x_tile, pltpu.roll(x_tile, SEG - 1, 1))
        chain = left + right - 2.0 * x_tile
        pair = parts_ref[0, side]
        for part in range(1, NT):
            pair = pair + parts_ref[part, side]
        drag = jnp.where(row < 3, b_tile[6:7], b_tile[7:8])
        velocity = (COUPLE * pair + applied + TENSION * chain) / drag
        speed = velocity * velocity
        tops.append(
            jnp.maximum(
                speed[0:1] + speed[1:2] + speed[2:3], speed[3:4] + speed[4:5] + speed[5:6]
            )
        )

        @pl.when(core == side)
        def _(velocity=velocity):
            vel_ref[...] = velocity

    top = jnp.maximum(tops[0], tops[1])
    tile = jnp.where(row < 6, vel_ref[...], jnp.where(row == 6, top, 0.0))
    vel_ref[...] = tile
    send = top if out_ref.shape[1] == 1 else tile
    out_ref[...] = jnp.broadcast_to(send[None], out_ref.shape)


def pack_kernel(seg_ref, drag_ref, send_ref, part_ref, raw_ref, out_ref):
    raw_ref[...] = jnp.zeros((24, SEG), F32)
    for block in range(2):
        for comp in range(3):
            for tile in range(3):
                raw_ref[8 * tile + 3 * block + comp, :] = seg_ref[3 * tile + comp, block, :]
        raw_ref[22 + block, :] = drag_ref[block, :]
    raw_ref[14, :] = send_ref[0, :].astype(F32)
    raw_ref[15, :] = part_ref[0, :].astype(F32)
    raw = raw_ref[...]
    for peer in range(NZ):
        out_ref[peer] = raw


def relay_kernel(near_ref, vel_ref, out_ref):
    top = near_ref[0]
    for at in range(1, NT * NX):
        top = jnp.maximum(top, near_ref[at])
    tile = jnp.where(sublane() == 6, top, vel_ref[...])
    out_ref[...] = jnp.broadcast_to(tile[None], out_ref.shape)


def last_kernel(info_ref, top_ref, x_ref, vel_ref, pos_out, vel_out):
    top = jnp.max(jnp.max(top_ref[...], axis=0), axis=1, keepdims=True)
    step = STEP_LENGTH / (jnp.sqrt(top) + EPSILON)
    velocity = vel_ref[...]
    moved = x_ref[info_ref[8, 0]] + step * velocity
    for block in range(2):
        for comp in range(3):
            pos_out[comp, block, :] = moved[3 * block + comp]
            vel_out[comp, block, :] = velocity[3 * block + comp]


SMEM = pl.BlockSpec(memory_space=pltpu.SMEM)
VMEM = pl.BlockSpec(memory_space=pltpu.VMEM)


def shape(*dims, dtype=F32):
    return jax.ShapeDtypeStruct(dims, dtype)


def call(kernel, name, operands, outs, smem_in=0, smem_out=0, scratch=(), mib=4):
    return pl.pallas_call(
        kernel,
        name=name,
        in_specs=[SMEM] * smem_in + [VMEM] * (len(operands) - smem_in),
        out_specs=[VMEM] * (len(outs) - smem_out) + [SMEM] * smem_out,
        out_shape=outs,
        scratch_shapes=scratch,
        compiler_params=pltpu.CompilerParams(vmem_limit_bytes=mib << 20),
    )(*operands)


def exchange(value, axes):
    return lax.all_to_all(value, axes, 0, 0, tiled=True)


def local(segments, stress, drag_coef, send_ids, partner_ids):
    raw, to_z = call(
        pack_kernel,
        "pack",
        (
            segments.transpose(1, 0, 2),
            drag_coef,
            send_ids.reshape(1, SEG),
            partner_ids.reshape(1, SEG),
        ),
        [shape(24, SEG), shape(NZ, 24, SEG)],
        mib=56,
    )
    line = exchange(to_z, "z")
    near = lax.all_gather(raw, ("y", "c"), axis=0)
    group = lax.all_gather(raw, "x", axis=0)
    line, near, group = lax.optimization_barrier((line, near, group))

    sent = line[:, 14].astype(jnp.int32)
    part = line[:, 15].astype(jnp.int32)
    z_row = lax.broadcasted_iota(jnp.int32, (NZ, SEG), 0)
    peer = lax.broadcasted_iota(jnp.int32, (NZ, SEG), 1)
    target = 2 * lax.shift_right_logical(peer, 5) + lax.bitwise_and(peer, 1)
    codes = jnp.where(sent >= 0, 2 * z_row + sent + 256 * (2 * target + part), -1)
    mine = near[:, 14].astype(jnp.int32)
    other = near[:, 15].astype(jnp.int32)
    row = lax.broadcasted_iota(jnp.int32, (NT, SEG), 0)
    lane = lax.broadcasted_iota(jnp.int32, (NT, SEG), 1)
    z_lane = lax.bitwise_and(lax.shift_right_logical(lane, 1), NZ - 1)
    out = jnp.where(mine >= 0, 2 * z_lane + other + 256 * (2 * row + mine), -1)
    place = jnp.zeros((NT, SEG), jnp.int32)
    for at, axis in enumerate(("c", "y", "z", "x")):
        place = jnp.where(lane == at, lax.axis_index(axis), place)
    info = jnp.concatenate([out, place], axis=0)

    force, items, count = call(
        first_kernel,
        "first_pairs",
        (codes, info, line, group, near),
        [
            shape(NT, NC, 8, SEG),
            shape(1, LIST, dtype=jnp.int32),
            shape(1, 1, dtype=jnp.int32),
        ],
        smem_in=2,
        smem_out=2,
        scratch=SCRATCH,
        mib=16,
    )

    def finish(force, position, peers, name):
        return call(
            finish_kernel,
            name,
            (info, stress, exchange(force, ("y", "c")), near, position),
            [shape(8, SEG), shape(*peers, SEG)],
            smem_in=2,
        )

    velocity, to_near = finish(force, near, (NT * NX, 8), "finish")
    near_vel = exchange(to_near, ("y", "c", "x"))
    (to_z,) = call(relay_kernel, "relay", (near_vel, velocity), [shape(NZ, 8, SEG)])
    line_vel = exchange(to_z, "z")

    force, position = call(
        second_kernel,
        "second_pairs",
        (info, items, count, line, group, near, line_vel, near_vel.reshape(NT, NX, 8, SEG)),
        [shape(NT, NC, 8, SEG), shape(NC, 8, SEG)],
        smem_in=3,
        scratch=SCRATCH,
        mib=16,
    )
    velocity, to_all = finish(force, position, (NY * NZ * NX, 1), "finish_last")
    tops = exchange(to_all, ("y", "z", "x"))
    positions, velocity = call(
        last_kernel,
        "last",
        (info, tops, position, velocity),
        [shape(3, 2, SEG), shape(3, 2, SEG)],
        smem_in=1,
    )
    return positions.transpose(1, 0, 2), velocity.transpose(1, 0, 2)


def solution(mesh):
    split = Mesh(
        mesh.devices.reshape(NY, NZ, NC, mesh.shape["sub"]), ("y", "z", "c", "x")
    )
    return jax.shard_map(
        local,
        mesh=split,
        in_specs=(
            P(DOM_SUB, None, None),
            P(),
            P(DOM_SUB, None),
            P(DOM_SUB, None, None),
            P(DOM_SUB, None, None),
        ),
        out_specs=(P(DOM_SUB, None, None), P(DOM_SUB, None, None)),
        check_vma=False,
    )
```

time: 142 us -> 147 us (1.035)
  blocking collectives: 79.3 us -> 108 us
  starting transfers between devices: 30.6 us -> 15.7 us
  waiting for transfers between devices: 8.18 us -> 0.01 us
    all_to_all x4 -> x5, blocking collectives: 62.6 us -> 82 us  [exchange(): return lax.all_to_all(value, axes, 0, 0, tiled=True)]
    ppermute x3 -> x0, starting transfers between devices: 10.5 us -> none  [pass_x(): return lax.ppermute(value, 'x', [(i, (i + shift) % NX) for i in range(NX)])]
    all_gather x3 -> x2, blocking collectives: 16.6 us -> 26.3 us  [the longest x1 16.4 us: local(): near = lax.all_gather(raw, ('y', 'c'), axis=0)]
    all_to_all x2 -> x1, waiting for transfers between devices: 7.54 us -> 0.01 us  [exchange(): return lax.all_to_all(value, axes, 0, 0, tiled=True)]
    all_to_all x2 -> x1, starting transfers between devices: 20.1 us -> 15.7 us  [exchange(): return lax.all_to_all(value, axes, 0, 0, tiled=True)]
  transfers between devices with their start and end apart: 5 -> 1, of which waited for: 3 -> 0; matrix products, arithmetic and copies ran while one was open for 0% -> 0% of each run, Pallas kernels for 0% -> 0%
where the time goes in v4:
time: 147 us; the launch traced here: 146 us
  blocking collectives  108 us (73%)
  Pallas kernels  19.9 us (14%)
  starting transfers between devices  15.7 us (11%)
    all_to_all x5, blocking collectives, exchange(): return lax.all_to_all(value, axes, 0, 0, tiled=True)  82 us
    pallas_call x7, Pallas kernels, call(): pl.pallas_call(kernel, name=name, in_specs=[SMEM] * smem_in + [VMEM] * (l...  19.9 us
    all_gather x1, blocking collectives, local(): near = lax.all_gather(raw, ('y', 'c'), axis=0)  16.4 us
    all_to_all x1, starting transfers between devices, exchange(): return lax.all_to_all(value, axes, 0, 0, tiled=True)  15.7 us
    all_gather x1, blocking collectives, local(): group = lax.all_gather(raw, 'x', axis=0)  9.89 us
  transfers between devices with their start and end apart: 1, of which 0 were waited for; matrix products, arithmetic and copies ran while one was open for 0% of the time, Pallas kernels for 0%

profile of v4, /device:TPU:1, one launch (start us, length us, event | category | flops | bytes accessed | tf_op | source)
XLA Modules:
  0.0 145.7 jit_solution(1052864063849596036)
XLA Ops:
  0.6 1.4 pack.1
  2.1 15.7 %all-to-all-start = ((f32[16,24,128]{2,1,0:T(8,128)}), f32[16,24,128]{2,1,0:T(8,128)S(1)}, u32[]{:S(2)}, u32[]{:S(2)}) async-start(f32[16,24,128]{2,1,0:T(8,128)} %get-tuple-element.18), calls=%async_computation | async-start | bytes 393216 | tf_op jit(solution)/shard_map/all_to_all | solution.py:394
  17.8 0.0 copy-start.1
  17.9 0.7 copy-done.1
  18.5 9.9 %all-gather.1 = f32[96,128]{1,0:T(8,128)S(1)} all-gather(f32[24,128]{1,0:T(8,128)S(1)} %copy-done.1), channel_id=3, replica_groups=mesh['y'=4,'z'=16,'c'=2,'x'=4] {'x'}, dimensions={0}, use_global_device_ids=true | all-gather | bytes 61440 | tf_op jit(solution)/shard_map/all_gather | solution.py:412
  28.4 16.4 %all-gather = f32[192,128]{1,0:T(8,128)S(1)} all-gather(f32[24,128]{1,0:T(8,128)S(1)} %copy-done.1), channel_id=2, replica_groups=mesh['y'=4,'z'=16,'c'=2,'x'=4] {'y','c'}, dimensions={0}, use_global_device_ids=true | all-gather | bytes 110592 | tf_op jit(solution)/shard_map/all_gather | solution.py:411
  44.9 0.0 all-to-all-done.line_ref
  45.0 0.1 fusion.4
  45.1 0.1 add_select_fusion.codes_ref
  45.1 8.0 %first_pairs.1 = (f32[8,2,8,128]{3,2,1,0:T(8,128)S(1)}, s32[1,320]{1,0:T(1,128)S(1)}, s32[1,1]{1,0:T(1,128)}) custom-call(s32[16,128]{1,0:T(8,128)S(1)} %add_select_fusion.codes_ref, s32[16,128]{1,0:T(8,128)S(1)} %pad_add_fusion.info_ref, f32[16,24,128]{2,1,0:T(8,128)S(1)} %all-to-all-done.line_ref, f32[4,24,128]{2,1,0:T(8,128)S(1)} %bitcast.32, ...), custom_call_target="tpu_custom_call" | custom-call | tf_op jit(solution)/shard_map/first_pairs/pallas_call | solution.py:382
  53.1 0.0 copy-start
  53.2 9.4 %all_to_all.30.parts_ref = f32[8,2,8,128]{3,2,1,0:T(8,128)S(1)} all-to-all(f32[8,2,8,128]{3,2,1,0:T(8,128)S(1)} %get-tuple-element.25), channel_id=1, replica_groups=mesh['y'=4,'z'=16,'c'=2,'x'=4] {'y','c'}, dimensions={0} | all-to-all | bytes 131072 | tf_op jit(solution)/shard_map/all_to_all | solution.py:394
  62.6 0.0 copy-done
  62.6 0.9 finish.1
  63.5 12.6 %all_to_all.31.near_ref = f32[32,8,128]{2,1,0:T(8,128)S(1)} all-to-all(f32[32,8,128]{2,1,0:T(8,128)S(1)} %get-tuple-element.26), channel_id=1, replica_groups=mesh['y'=4,'z'=16,'c'=2,'x'=4] {'y','c','x'}, dimensions={0} | all-to-all | bytes 262144 | tf_op jit(solution)/shard_map/all_to_all | solution.py:394
  76.1 23.3 %all_to_all.32.vel_ref = f32[16,8,128]{2,1,0:T(8,128)S(1)} all-to-all(f32[16,8,128]{2,1,0:T(8,128)S(1)} %relay.1), channel_id=1, replica_groups=mesh['y'=4,'z'=16,'c'=2,'x'=4] {'z'}, dimensions={0} | all-to-all | bytes 131072 | tf_op jit(solution)/shard_map/all_to_all | solution.py:394
  99.4 7.2 %second_pairs.1 = (f32[8,2,8,128]{3,2,1,0:T(8,128)S(1)}, f32[2,8,128]{2,1,0:T(8,128)S(1)}) custom-call(s32[16,128]{1,0:T(8,128)S(1)} %pad_add_fusion.info_ref, s32[1,320]{1,0:T(1,128)S(1)} %get-tuple-element.23.list_ref, s32[1,1]{1,0:T(1,128)} %get-tuple-element.24.count_ref, f32[16,24,128]{2,1,0:T(8,128)S(1)} %all-to-all-done.line_ref, ...), custom_call_target="tpu_custom_call" | custom-call | tf_op jit(solution)/shard_map/second_pairs/pallas_call | solution.py:382
  106.6 9.9 %all_to_all.33.parts_ref = f32[8,2,8,128]{3,2,1,0:T(8,128)S(1)} all-to-all(f32[8,2,8,128]{3,2,1,0:T(8,128)S(1)} %get-tuple-element.28), channel_id=1, replica_groups=mesh['y'=4,'z'=16,'c'=2,'x'=4] {'y','c'}, dimensions={0} | all-to-all | bytes 131072 | tf_op jit(solution)/shard_map/all_to_all | solution.py:394
  116.6 0.9 finish_last.1
  117.5 26.7 %all_to_all.34.top_ref = f32[256,1,128]{2,1,0:T(1,128)S(1)} all-to-all(f32[256,1,128]{2,1,0:T(1,128)S(1)} %get-tuple-element.30), channel_id=1, replica_groups=mesh['y'=4,'z'=16,'c'=2,'x'=4] {'y','z','x'}, dimensions={0} | all-to-all | bytes 262144 | tf_op jit(solution)/shard_map/all_to_all | solution.py:394
  144.3 1.4 last.1
  (13 shorter events, 0.2 us)
Async XLA Ops:
  2.1 42.8 %all-to-all-start = ((f32[16,24,128]{2,1,0:T(8,128)}), f32[16,24,128]{2,1,0:T(8,128)S(1)}, u32[]{:S(2)}, u32[]{:S(2)}) async-start(f32[16,24,128]{2,1,0:T(8,128)} %get-tuple-element.18), calls=%async_computation | async-start | bytes 393216 | tf_op jit(solution)/shard_map/all_to_all | solution.py:394
  17.8 0.7 copy-start.1
  53.1 9.4 %copy-start = (f32[3,3]{1,0:T(4,128)S(1)}, f32[3,3]{1,0:T(4,128)}, u32[]{:S(2)}) copy-start(f32[3,3]{1,0:T(4,128)} %stress_ref.3) | copy-start | bytes 112

commit v5 on v3

--- a/solution.py
+++ b/solution.py
@@ -21,7 +21,7 @@
 SEG = 128
 NDEV = NY * NZ
 NX = 4
-BATCH = 16
+BATCH = 32
 LIST = 320
 DUMMY = 2 * (NDEV + NX)
 F32 = jnp.float32
@@ -49,22 +49,30 @@
 
 def source_operands(x_tile, l_tile, b_tile):
     row = sublane()
-    x_tile = jnp.where(row < 6, x_tile, 0.0)
+    x_tile = jnp.where(lax.bitwise_and(row, 3) < 3, x_tile, 0.0)
     square = x_tile * x_tile
     norm0 = square[0:1] + square[1:2] + square[2:3] + CORE_SQUARE
-    norm1 = square[3:4] + square[4:5] + square[5:6] + CORE_SQUARE
-    full = jnp.where(row == 6, norm0, jnp.where(row == 7, norm1, x_tile))
+    norm1 = square[4:5] + square[5:6] + square[6:7] + CORE_SQUARE
+    full = jnp.where(row == 3, norm0, jnp.where(row == 7, norm1, x_tile))
     high, mid, low = split3(full)
     dist = [high, mid, high, mid, low, high, jnp.ones_like(high)]
-    prod = [jnp.where(row < 3, b_tile[a : a + 1], b_tile[3 + a : 4 + a]) * l_tile for a in range(3)]
+    burgers = [burgers_rows(l_tile, b_tile, block) for block in range(2)]
+    prod = [jnp.where(row < 4, burgers[0][a], burgers[1][a]) * l_tile for a in range(3)]
     parts = [split2(p) for p in prod]
     highs = [p[0] for p in parts]
     mids = [p[1] for p in parts]
     weight = highs + highs + mids
-    flag = jnp.where(row == 6, 1.0, 0.0)
-    first = (jnp.where(row < 6, high, flag), jnp.where(row < 6, mid, 0.0))
-    second = (jnp.where(row < 3, up(high, 3), flag), jnp.where(row < 3, up(mid, 3), 0.0))
+    first = (jnp.where(row == 3, 1.0, high), jnp.where(row == 3, 0.0, mid))
+    second = (jnp.where(row == 3, 1.0, up(high, 4)), jnp.where(row == 3, 0.0, up(mid, 4)))
     return dist + weight, first, second
+
+
+def burgers_rows(l_tile, b_tile, block):
+    return [
+        l_tile[4 * block + 3 : 4 * block + 4],
+        b_tile[2 * block : 2 * block + 1],
+        b_tile[2 * block + 1 : 2 * block + 2],
+    ]
 
 
 def store_rows(ref, index, tiles):
@@ -77,16 +85,16 @@
     row = sublane()
 
     def both(tile):
-        if block == 0:
-            return jnp.where(row < 3, tile, jnp.where(row < 6, up(tile, 5), 0.0))
-        return jnp.where(row < 3, up(tile, 3), jnp.where(row < 6, tile, 0.0))
+        other = up(tile, 4)
+        own, far = (tile, other) if block == 0 else (other, tile)
+        return jnp.where(lax.bitwise_and(row, 3) == 3, 0.0, jnp.where(row < 4, own, far))
 
     x_both = both(x_tile)
     high, mid, low = split3(x_both)
     square = x_both * x_both
     norm = square[0:1] + square[1:2] + square[2:3]
     norm_h, norm_m, norm_l = split3(norm)
-    unit = jnp.where(row >= 6, 1.0, 0.0)
+    unit = jnp.where(lax.bitwise_and(row, 3) == 3, 1.0, 0.0)
     norms = jnp.where(
         row == 0, norm_h, jnp.where(row == 1, norm_m, jnp.where(row == 2, norm_l, 0.0))
     )
@@ -101,8 +109,7 @@
         norms,
     ]
     l_both = both(l_tile)
-    base = 3 * block
-    prod = [b_tile[base + a : base + a + 1] * l_both for a in range(3)]
+    prod = [b * l_both for b in burgers_rows(l_tile, b_tile, block)]
     parts = [split2(p) for p in prod]
     highs = [p[0] for p in parts]
     mids = [p[1] for p in parts]
@@ -154,8 +161,8 @@
             dist = dist.T
             weight = weight.T
             for j in range(2):
-                mine = (place >= 3 * j) & (place < 3 * j + 3)
-                keep = mine | (place == 6 + j) | (lane >= 48)
+                mine = (place >= 4 * j) & (place < 4 * j + 3)
+                keep = mine | (place == 4 * j + 3) | (lane >= 48)
                 at = 2 * (2 * side + block) + j
                 target_s[at, 0:SEG] = jnp.where(keep, dist, 0.0).astype(BF16)
                 target_s[at, SEG : 2 * SEG] = jnp.where(mine, weight, 0.0).astype(BF16)
@@ -183,20 +190,21 @@
         lhs = jnp.concatenate(moments + moments, axis=1)
         rhs = jnp.concatenate(highs + lows, axis=1)
         return total + lax.dot_general(
-            lhs, rhs, (((1,), (1,)), ((), ())), preferred_element_type=F32
+            rhs, lhs, (((1,), (1,)), ((), ())), preferred_element_type=F32
         )
 
-    total = lax.fori_loop(0, count_ref[0, 0], items, jnp.zeros((64, SEG), F32))
+    total = lax.fori_loop(0, count_ref[0, 0], items, jnp.zeros((SEG, 64), F32))
+    total = jnp.concatenate([total, jnp.zeros((SEG, SEG - 64), F32)], axis=1).T
     for side in range(NC):
         x_tile = get_target(side)[0]
         rows = []
         for block in range(2):
             at = 16 * (2 * side + block)
-            x_block = x_tile[3 * block : 3 * block + 3]
+            x_block = x_tile[4 * block : 4 * block + 3]
             rows.append(
-                x_block * total[at + 6 : at + 7] - (total[at : at + 3] + total[at + 8 : at + 11])
+                x_block * total[at + 3 : at + 4] - (total[at : at + 3] + total[at + 8 : at + 11])
             )
-        rows.append(jnp.zeros((2, SEG), F32))
+            rows.append(jnp.zeros((1, SEG), F32))
         force_ref[side] = jnp.concatenate(rows, axis=0)
 
 
@@ -211,6 +219,14 @@
     return tile[0:8], tile[8:16], tile[16:24]
 
 
+def tiles_of_rows(rows):
+    return (
+        jnp.concatenate([rows[0], rows[1]], axis=0),
+        jnp.concatenate([rows[2], rows[3]], axis=0),
+        rows[4],
+    )
+
+
 def no_source():
     zero = jnp.zeros((8, SEG), F32)
     return zero, zero, zero
@@ -223,7 +239,7 @@
     def get_source(k):
         if isinstance(k, int):
             return no_source() if k == NDEV + NX else tiles_of(group[k - NDEV])
-        return tiles_of(all_ref.at[k])
+        return tiles_of_rows(all_ref.at[k])
 
     def get_target(side):
         return tiles_of(chip_ref.at[side])
@@ -252,7 +268,7 @@
     top = vel_ref[0]
     for k in range(1, NDEV):
         top = jnp.maximum(top, vel_ref[k])
-    top = jnp.max(top[6:7], axis=1, keepdims=True)
+    top = jnp.max(top[3:4], axis=1, keepdims=True)
     step = STEP_LENGTH / (jnp.sqrt(top) + EPSILON)
     row = sublane()
     group = (g0, g1, g2, g3)
@@ -265,12 +281,12 @@
             x_tile, l_tile, b_tile = tiles_of(group[shift])
             moved = near_ref[lax.bitwise_and(x_index - shift, NX - 1)]
         else:
-            x_tile, l_tile, b_tile = tiles_of(all_ref.at[k])
+            x_tile, l_tile, b_tile = tiles_of_rows(all_ref.at[k])
             moved = vel_ref[k]
         return x_tile + step * moved, l_tile, b_tile
 
     for side in range(NC):
-        moved = jnp.where(row < 6, chip_vel_ref[side], 0.0)
+        moved = jnp.where(row == 3, 0.0, chip_vel_ref[side])
         chip_x_ref[side] = chip_ref[side, 0:8] + step * moved
 
     def get_target(side):
@@ -291,8 +307,8 @@
         b_tile = chip_ref[side, 16:24]
         rows = []
         for block in range(2):
-            b = [b_tile[3 * block + a : 3 * block + a + 1] for a in range(3)]
-            line = [l_tile[3 * block + a : 3 * block + a + 1] for a in range(3)]
+            b = burgers_rows(l_tile, b_tile, block)
+            line = [l_tile[4 * block + a : 4 * block + a + 1] for a in range(3)]
             pulled = [
                 stress_ref[a, 0] * b[0] + stress_ref[a, 1] * b[1] + stress_ref[a, 2] * b[2]
                 for a in range(3)
@@ -300,24 +316,24 @@
             rows.append(pulled[1] * line[2] - pulled[2] * line[1])
             rows.append(pulled[2] * line[0] - pulled[0] * line[2])
             rows.append(pulled[0] * line[1] - pulled[1] * line[0])
-        rows.append(jnp.zeros((2, SEG), F32))
+            rows.append(jnp.zeros((1, SEG), F32))
         applied = jnp.concatenate(rows, axis=0)
         left = jnp.where(lane == 0, x_tile, pltpu.roll(x_tile, 1, 1))
         right = jnp.where(lane == SEG - 1, x_tile, pltpu.roll(x_tile, SEG - 1, 1))
         chain = left + right - 2.0 * x_tile
         pair = parts_ref[0, side] + parts_ref[1, side]
-        drag = jnp.where(row < 3, b_tile[6:7], b_tile[7:8])
+        drag = jnp.where(row < 4, b_tile[4:5], b_tile[5:6])
         velocity = (COUPLE * pair + applied + TENSION * chain) / drag
         speed = velocity * velocity
         tops.append(
             jnp.maximum(
-                speed[0:1] + speed[1:2] + speed[2:3], speed[3:4] + speed[4:5] + speed[5:6]
+                speed[0:1] + speed[1:2] + speed[2:3], speed[4:5] + speed[5:6] + speed[6:7]
             )
         )
         tiles.append(velocity)
     top = jnp.maximum(tops[0], tops[1])
     for side in range(NC):
-        vel_ref[side] = jnp.where(row < 6, tiles[side], jnp.where(row == 6, top, 0.0))
+        vel_ref[side] = jnp.where(row == 3, top, jnp.where(row == 7, 0.0, tiles[side]))
     if last:
         out_ref[...] = jnp.broadcast_to(top[None], out_ref.shape)
     else:
@@ -330,14 +346,18 @@
     raw_ref[...] = jnp.zeros((24, SEG), F32)
     for block in range(2):
         for comp in range(3):
-            for tile in range(3):
-                raw_ref[8 * tile + 3 * block + comp, :] = seg_ref[3 * tile + comp, block, :]
-        raw_ref[22 + block, :] = drag_ref[block, :]
-    raw_ref[14, :] = send_ref[0, :].astype(F32)
-    raw_ref[15, :] = part_ref[0, :].astype(F32)
-    raw = raw_ref[...]
-    for peer in range(NZ):
-        out_ref[peer] = raw
+            raw_ref[4 * block + comp, :] = seg_ref[comp, block, :]
+            raw_ref[8 + 4 * block + comp, :] = seg_ref[3 + comp, block, :]
+        raw_ref[11 + 4 * block, :] = seg_ref[6, block, :]
+        raw_ref[16 + 2 * block, :] = seg_ref[7, block, :]
+        raw_ref[17 + 2 * block, :] = seg_ref[8, block, :]
+        raw_ref[20 + block, :] = drag_ref[block, :]
+    raw_ref[3, :] = send_ref[0, :].astype(F32)
+    raw_ref[7, :] = part_ref[0, :].astype(F32)
+    for at in range(5):
+        rows = raw_ref[4 * at : 4 * at + 4, :]
+        for peer in range(NZ):
+            out_ref[peer, at] = rows
 
 
 def relay_kernel(codes_ref, near_ref, out_ref):
@@ -345,7 +365,7 @@
     top = near_ref[0]
     for x in range(1, NX):
         top = jnp.maximum(top, near_ref[x])
-    tile = jnp.where(sublane() == 6, top, near_ref[x_index])
+    tile = jnp.where(sublane() == 3, top, near_ref[x_index])
     for peer in range(NZ):
         out_ref[peer] = tile
 
@@ -358,8 +378,8 @@
     moved = x_ref[core] + step * velocity
     for block in range(2):
         for comp in range(3):
-            pos_out[comp, block, :] = moved[3 * block + comp]
-            vel_out[comp, block, :] = velocity[3 * block + comp]
+            pos_out[comp, block, :] = moved[4 * block + comp]
+            vel_out[comp, block, :] = velocity[4 * block + comp]
 
 
 SMEM = pl.BlockSpec(memory_space=pltpu.SMEM)
@@ -404,35 +424,35 @@
             send_ids.reshape(1, SEG),
             partner_ids.reshape(1, SEG),
         ),
-        [shape(24, SEG), shape(NZ, 24, SEG)],
+        [shape(24, SEG), shape(NZ, 5, 4, SEG)],
         mib=56,
     )
     along_z = exchange(to_z, "z")
     chip = lax.all_gather(raw, "c", axis=0)
-    near1 = pass_x(raw, 1)
-    along_z, chip, near1, raw = lax.optimization_barrier((along_z, chip, near1, raw))
-    group = [raw, near1, pass_x(raw, 2), pass_x(raw, 3)]
-    everyone = exchange(
-        jnp.broadcast_to(along_z.reshape(1, NZ * 24, SEG), (NY, NZ * 24, SEG)), "y"
-    ).reshape(NDEV, 24, SEG)
-
-    lists = everyone[:, 14:16].reshape(2 * NDEV, SEG)
+    group = [raw] + [pass_x(raw, shift) for shift in range(1, NX)]
+
     lane = lax.broadcasted_iota(jnp.int32, (NC, SEG), 1)
     side = lax.broadcasted_iota(jnp.int32, (NC, SEG), 0)
     even = lax.bitwise_and(lane, SEG - 2)
+    sent = chip[:, 3].astype(jnp.int32)
+    other = chip[:, 7].astype(jnp.int32)
+    out = jnp.where(sent >= 0, even + other + 256 * (2 * side + sent), -1)
+    first = lane[0:1]
+    where = jnp.where(first == 0, core, jnp.where(first == 1, y_index, x_index))
+    zero = jnp.zeros((1, SEG), jnp.int32)
+    known = jnp.concatenate([out, zero, zero, where, zero], axis=0)
     pick = (lane == 2 * chip_index + side).astype(F32)
+
+    everyone = exchange(
+        jnp.broadcast_to(along_z.reshape(1, NZ * 5, 4, SEG), (NY, NZ * 5, 4, SEG)), "y"
+    ).reshape(NDEV, 5, 4, SEG)
+    lists = everyone[:, 0:2, 3].reshape(2 * NDEV, SEG)
     incoming = lax.dot_general(
         pick, lists, (((1,), (1,)), ((), ())), precision=lax.Precision.HIGHEST
     ).astype(jnp.int32)
     partner = jnp.concatenate([incoming[:, 1:], incoming[:, :1]], axis=1)
     into = jnp.where(incoming >= 0, even + incoming + 256 * (2 * side + partner), -1)
-    sent = chip[:, 14].astype(jnp.int32)
-    other = chip[:, 15].astype(jnp.int32)
-    out = jnp.where(sent >= 0, even + other + 256 * (2 * side + sent), -1)
-    first = lane[0:1]
-    where = jnp.where(first == 0, core, jnp.where(first == 1, y_index, x_index))
-    zero = jnp.zeros((1, SEG), jnp.int32)
-    codes = jnp.concatenate([into, out, zero, zero, where, zero], axis=0)
+    codes = jnp.concatenate([into, known], axis=0)
 
     force, items, count = call(
         first_kernel,

time: 142 us -> 137 us (0.965)
  waiting for transfers between devices: 8.18 us -> 3.13 us
  blocking collectives: 79.3 us -> 83.2 us
  Pallas kernels: 20.8 us -> 17.6 us
    all_to_all x2, waiting for transfers between devices: 7.54 us -> 3.12 us  [exchange(): return lax.all_to_all(value, axes, 0, 0, tiled=True)]
    all_gather x1, blocking collectives: 2.73 us -> 6.13 us  [local(): chip = lax.all_gather(raw, 'c', axis=0)]
    pallas_call x7, Pallas kernels: 20.8 us -> 17.6 us  [call(): pl.pallas_call(kernel, name=name, in_specs=[SMEM] * smem_in + [VMEM] * (l...]
  transfers between devices with their start and end apart: 5 -> 5, of which waited for: 3 -> 2; matrix products, arithmetic and copies ran while one was open for 0% -> 1% of each run, Pallas kernels for 0% -> 0%
where the time goes in v5:
time: 137 us
  blocking collectives  83.2 us (61%)
  starting transfers between devices  30.6 us (22%)
  Pallas kernels  17.6 us (13%)
  waiting for transfers between devices  3.13 us (2%)
    all_to_all x4, blocking collectives, exchange(): return lax.all_to_all(value, axes, 0, 0, tiled=True)  63.7 us
    all_to_all x2, starting transfers between devices, exchange(): return lax.all_to_all(value, axes, 0, 0, tiled=True)  20.1 us
    pallas_call x7, Pallas kernels, call(): pl.pallas_call(kernel, name=name, in_specs=[SMEM] * smem_in + [VMEM] * (l...  17.6 us
    all_gather x2, blocking collectives, local(): lax.all_gather(force, 'c', axis=0)  13.4 us
    ppermute x3, starting transfers between devices, pass_x(): return lax.ppermute(value, 'x', [(i, (i + shift) % NX) for i in range(NX)])  10.5 us
    all_gather x1, blocking collectives, local(): chip = lax.all_gather(raw, 'c', axis=0)  6.13 us
    all_to_all x2, waiting for transfers between devices, exchange(): return lax.all_to_all(value, axes, 0, 0, tiled=True)  3.12 us
  transfers between devices with their start and end apart: 5, of which 2 were waited for; matrix products, arithmetic and copies ran while one was open for 1% of the time, Pallas kernels for 0%

profile of v5, /device:TPU:1, one launch (start us, length us, event | category | flops | bytes accessed | tf_op | source)
XLA Modules:
  0.0 136.8 jit_solution(1757001682653845022)
XLA Ops:
  0.6 1.4 %pack.1 = (f32[24,128]{1,0:T(8,128)}, f32[16,5,4,128]{3,2,1,0:T(4,128)}) custom-call(f32[9,2,128]{2,1,0:T(2,128)} %bitcast.46, f32[2,128]{1,0:T(2,128)} %drag_ref.1, s32[1,128]{1,0:T(1,128)} %bitcast.49, s32[1,128]{1,0:T(1,128)} %bitcast.50), custom_call_target="tpu_custom_call" | custom-call | tf_op jit(solution)/shard_map/pack/pallas_call | solution.py:394
  2.1 15.9 %all-to-all-start = ((f32[16,5,4,128]{3,2,1,0:T(4,128)}), f32[16,5,4,128]{3,2,1,0:T(4,128)S(1)}, u32[]{:S(2)}, u32[]{:S(2)}) async-start(f32[16,5,4,128]{3,2,1,0:T(4,128)} %get-tuple-element.15), calls=%async_computation | async-start | bytes 327680 | tf_op jit(solution)/shard_map/all_to_all | solution.py:410
  18.0 3.1 %collective-permute-start = (f32[24,128]{1,0:T(8,128)S(1)}, f32[24,128]{1,0:T(8,128)S(1)}, u32[]{:S(2)}, u32[]{:S(2)}) collective-permute-start(f32[24,128]{1,0:T(8,128)S(1)} %copy-done), channel_id=1, source_target_pairs={{0,1},{1,2},{2,3},{3,0},{4,5},{5,6},{6,7},{7,4},{8,9},{9,10},{10,1... | collective-permute-start | bytes 36872 | tf_op jit(solution)/shard_map/ppermute | solution.py:406
  21.1 4.4 %collective-permute-start.1 = (f32[24,128]{1,0:T(8,128)S(1)}, f32[24,128]{1,0:T(8,128)S(1)}, u32[]{:S(2)}, u32[]{:S(2)}) collective-permute-start(f32[24,128]{1,0:T(8,128)S(1)} %copy-done), channel_id=1, source_target_pairs={{0,2},{1,3},{2,0},{3,1},{4,6},{5,7},{6,4},{7,5},{8,10},{9,11},{10,... | collective-permute-start | bytes 36872 | tf_op jit(solution)/shard_map/ppermute | solution.py:406
  25.4 3.1 %collective-permute-start.2 = (f32[24,128]{1,0:T(8,128)S(1)}, f32[24,128]{1,0:T(8,128)S(1)}, u32[]{:S(2)}, u32[]{:S(2)}) collective-permute-start(f32[24,128]{1,0:T(8,128)S(1)} %copy-done), channel_id=1, source_target_pairs={{0,3},{1,0},{2,1},{3,2},{4,7},{5,4},{6,5},{7,6},{8,11},{9,8},{10,9... | collective-permute-start | bytes 36872 | tf_op jit(solution)/shard_map/ppermute | solution.py:406
  28.5 1.6 %all-to-all-done = f32[16,5,4,128]{3,2,1,0:T(4,128)S(1)} async-done(((f32[16,5,4,128]{3,2,1,0:T(4,128)}), f32[16,5,4,128]{3,2,1,0:T(4,128)S(1)}, u32[]{:S(2)}, u32[]{:S(2)}) %all-to-all-start) | async-done | bytes 163872 | tf_op jit(solution)/shard_map/all_to_all | solution.py:410
  30.2 0.9 broadcast_in_dim.32
  31.1 4.2 %all-to-all-start.1 = ((f32[4,80,4,128]{3,2,1,0:T(4,128)}), f32[4,80,4,128]{3,2,1,0:T(4,128)S(1)}, u32[]{:S(2)}, u32[]{:S(2)}) async-start(f32[4,80,4,128]{3,2,1,0:T(4,128)} %broadcast_in_dim.32), calls=%async_computation.1 | async-start | bytes 1310720 | tf_op jit(solution)/shard_map/all_to_all | solution.py:410
  35.3 6.1 %all-gather = f32[48,128]{1,0:T(8,128)S(1)} all-gather(f32[24,128]{1,0:T(8,128)S(1)} %copy-done), channel_id=2, replica_groups=mesh['y'=4,'z'=16,'c'=2,'x'=4] {'c'}, dimensions={0}, use_global_device_ids=true | all-gather | bytes 36864 | tf_op jit(solution)/shard_map/all_gather | solution.py:431
  41.4 1.5 %all-to-all-done.1 = f32[4,80,4,128]{3,2,1,0:T(4,128)S(1)} async-done(((f32[4,80,4,128]{3,2,1,0:T(4,128)}), f32[4,80,4,128]{3,2,1,0:T(4,128)S(1)}, u32[]{:S(2)}, u32[]{:S(2)}) %all-to-all-start.1) | async-done | bytes 655392 | tf_op jit(solution)/shard_map/all_to_all | solution.py:410
  43.0 0.2 convolution_convert_fusion
  43.2 0.1 compare_select_fusion.2
  43.4 6.6 %first_pairs.1 = (f32[2,8,128]{2,1,0:T(8,128)S(1)}, s32[1,320]{1,0:T(1,128)S(1)}, s32[1,1]{1,0:T(1,128)}) custom-call(s32[8,128]{1,0:T(8,128)S(1)} %concatenate.7.codes_ref, f32[64,5,4,128]{3,2,1,0:T(4,128)S(1)} %bitcast.31, f32[24,128]{1,0:T(8,128)S(1)} %copy-done, f32[24,128]{1,0:T(8,128)S(1)} %collective-permute-done.g1, ...), custom_call_target="tpu_custom_call" | custom-call | tf_op jit(solution)/shard_map/first_pairs/pallas_call | solution.py:394
  50.1 7.3 %all-gather.1 = f32[4,8,128]{2,1,0:T(8,128)S(1)} all-gather(f32[2,8,128]{2,1,0:T(8,128)S(1)} %get-tuple-element.19), channel_id=3, replica_groups=mesh['y'=4,'z'=16,'c'=2,'x'=4] {'c'}, dimensions={0}, use_global_device_ids=true | all-gather | bytes 24576 | tf_op jit(solution)/shard_map/all_gather | solution.py:474
  57.4 0.7 finish.1
  58.1 9.0 %all_to_all.30.near_ref = f32[4,8,128]{2,1,0:T(8,128)S(1)} all-to-all(f32[4,8,128]{2,1,0:T(8,128)S(1)} %get-tuple-element.20), channel_id=1, replica_groups=mesh['y'=4,'z'=16,'c'=2,'x'=4] {'x'}, dimensions={0} | all-to-all | bytes 32768 | tf_op jit(solution)/shard_map/all_to_all | solution.py:410
  67.1 0.6 relay.1
  67.7 18.4 %all_to_all.31 = f32[16,8,128]{2,1,0:T(8,128)S(1)} all-to-all(f32[16,8,128]{2,1,0:T(8,128)S(1)} %relay.1), channel_id=1, replica_groups=mesh['y'=4,'z'=16,'c'=2,'x'=4] {'z'}, dimensions={0} | all-to-all | bytes 131072 | tf_op jit(solution)/shard_map/all_to_all | solution.py:410
  86.1 7.9 %all_to_all.32 = f32[4,128,128]{2,1,0:T(8,128)S(1)} all-to-all(f32[4,128,128]{2,1,0:T(8,128)S(1)} %broadcast_in_dim.38), channel_id=1, replica_groups=mesh['y'=4,'z'=16,'c'=2,'x'=4] {'y'}, dimensions={0} | all-to-all | bytes 524288 | tf_op jit(solution)/shard_map/all_to_all | solution.py:410
  94.1 6.1 %second_pairs.1 = (f32[2,8,128]{2,1,0:T(8,128)S(1)}, f32[2,8,128]{2,1,0:T(8,128)S(1)}) custom-call(s32[8,128]{1,0:T(8,128)S(1)} %concatenate.7.codes_ref, s32[1,320]{1,0:T(1,128)S(1)} %get-tuple-element.17.list_ref, s32[1,1]{1,0:T(1,128)} %get-tuple-element.18.count_ref, f32[64,5,4,128]{3,2,1,0:T(4,128)S(1)} %bitcast.32, f32[24,128]{1,0:T(8,128)S(1)} %copy-done, ...), custom_call_target="tpu_custom_call" | custom-call | tf_op jit(solution)/shard_map/second_pairs/pallas_call | solution.py:394
  100.2 6.1 %all-gather.2 = f32[4,8,128]{2,1,0:T(8,128)S(1)} all-gather(f32[2,8,128]{2,1,0:T(8,128)S(1)} %get-tuple-element.22), channel_id=4, replica_groups=mesh['y'=4,'z'=16,'c'=2,'x'=4] {'c'}, dimensions={0}, use_global_device_ids=true | all-gather | bytes 24576 | tf_op jit(solution)/shard_map/all_gather | solution.py:495
  106.3 0.8 finish_last.1
  107.1 28.3 %all_to_all.33.top_ref = f32[256,1,128]{2,1,0:T(1,128)S(1)} all-to-all(f32[256,1,128]{2,1,0:T(1,128)S(1)} %get-tuple-element.24), channel_id=1, replica_groups=mesh['y'=4,'z'=16,'c'=2,'x'=4] {'y','z','x'}, dimensions={0} | all-to-all | bytes 262144 | tf_op jit(solution)/shard_map/all_to_all | solution.py:410
  135.4 1.3 last.1
  (18 shorter events, 0.3 us)
Async XLA Ops:
  2.1 15.9 %copy-start = (f32[24,128]{1,0:T(8,128)S(1)}, f32[24,128]{1,0:T(8,128)}, u32[]{:S(2)}) copy-start(f32[24,128]{1,0:T(8,128)} %get-tuple-element.16.g0) | copy-start | bytes 36868
  2.1 28.1 %all-to-all-start = ((f32[16,5,4,128]{3,2,1,0:T(4,128)}), f32[16,5,4,128]{3,2,1,0:T(4,128)S(1)}, u32[]{:S(2)}, u32[]{:S(2)}) async-start(f32[16,5,4,128]{3,2,1,0:T(4,128)} %get-tuple-element.15), calls=%async_computation | async-start | bytes 327680 | tf_op jit(solution)/shard_map/all_to_all | solution.py:410
  18.0 25.4 %collective-permute-start = (f32[24,128]{1,0:T(8,128)S(1)}, f32[24,128]{1,0:T(8,128)S(1)}, u32[]{:S(2)}, u32[]{:S(2)}) collective-permute-start(f32[24,128]{1,0:T(8,128)S(1)} %copy-done), channel_id=1, source_target_pairs={{0,1},{1,2},{2,3},{3,0},{4,5},{5,6},{6,7},{7,4},{8,9},{9,10},{10,1... | collective-permute-start | bytes 36872 | tf_op jit(solution)/shard_map/ppermute | solution.py:406
  21.1 22.3 %collective-permute-start.1 = (f32[24,128]{1,0:T(8,128)S(1)}, f32[24,128]{1,0:T(8,128)S(1)}, u32[]{:S(2)}, u32[]{:S(2)}) collective-permute-start(f32[24,128]{1,0:T(8,128)S(1)} %copy-done), channel_id=1, source_target_pairs={{0,2},{1,3},{2,0},{3,1},{4,6},{5,7},{6,4},{7,5},{8,10},{9,11},{10,... | collective-permute-start | bytes 36872 | tf_op jit(solution)/shard_map/ppermute | solution.py:406
  25.4 18.0 %collective-permute-start.2 = (f32[24,128]{1,0:T(8,128)S(1)}, f32[24,128]{1,0:T(8,128)S(1)}, u32[]{:S(2)}, u32[]{:S(2)}) collective-permute-start(f32[24,128]{1,0:T(8,128)S(1)} %copy-done), channel_id=1, source_target_pairs={{0,3},{1,0},{2,1},{3,2},{4,7},{5,4},{6,5},{7,6},{8,11},{9,8},{10,9... | collective-permute-start | bytes 36872 | tf_op jit(solution)/shard_map/ppermute | solution.py:406
  31.1 11.8 %all-to-all-start.1 = ((f32[4,80,4,128]{3,2,1,0:T(4,128)}), f32[4,80,4,128]{3,2,1,0:T(4,128)S(1)}, u32[]{:S(2)}, u32[]{:S(2)}) async-start(f32[4,80,4,128]{3,2,1,0:T(4,128)} %broadcast_in_dim.32), calls=%async_computation.1 | async-start | bytes 1310720 | tf_op jit(solution)/shard_map/all_to_all | solution.py:410
  43.4 13.9 %copy-start.1 = (f32[3,3]{1,0:T(4,128)S(1)}, f32[3,3]{1,0:T(4,128)}, u32[]{:S(2)}) copy-start(f32[3,3]{1,0:T(4,128)} %stress_ref.3) | copy-start | bytes 112

commit v6 on v5

--- a/solution.py
+++ b/solution.py
@@ -232,17 +232,17 @@
     return zero, zero, zero
 
 
-def first_kernel(codes_ref, all_ref, g0, g1, g2, g3, chip_ref, force_ref, list_ref, count_ref, *scratch):
+def first_kernel(codes_ref, all_ref, near_ref, force_ref, list_ref, count_ref, *scratch):
     build_list(codes_ref, list_ref, count_ref)
-    group = (g0, g1, g2, g3)
+    core = codes_ref[6, 0]
 
     def get_source(k):
         if isinstance(k, int):
-            return no_source() if k == NDEV + NX else tiles_of(group[k - NDEV])
+            return no_source() if k == NDEV + NX else tiles_of(near_ref.at[core, k - NDEV])
         return tiles_of_rows(all_ref.at[k])
 
     def get_target(side):
-        return tiles_of(chip_ref.at[side])
+        return tiles_of(near_ref.at[side, 0])
 
     pair_body(list_ref, count_ref, get_source, get_target, force_ref, *scratch)
 
@@ -252,59 +252,48 @@
     list_ref,
     count_ref,
     all_ref,
-    g0,
-    g1,
-    g2,
-    g3,
-    chip_ref,
+    near_ref,
     vel_ref,
-    near_ref,
-    chip_vel_ref,
+    near_vel_ref,
     force_ref,
-    chip_x_ref,
+    position_ref,
     *scratch,
 ):
-    x_index = codes_ref[6, 2]
+    core = codes_ref[6, 0]
     top = vel_ref[0]
     for k in range(1, NDEV):
         top = jnp.maximum(top, vel_ref[k])
     top = jnp.max(top[3:4], axis=1, keepdims=True)
     step = STEP_LENGTH / (jnp.sqrt(top) + EPSILON)
-    row = sublane()
-    group = (g0, g1, g2, g3)
+    for side in range(NC):
+        for s in range(NX):
+            position_ref[side, s] = near_ref[side, s, 0:8] + step * near_vel_ref[side, s]
 
     def get_source(k):
         if isinstance(k, int):
             if k == NDEV + NX:
                 return no_source()
-            shift = k - NDEV
-            x_tile, l_tile, b_tile = tiles_of(group[shift])
-            moved = near_ref[lax.bitwise_and(x_index - shift, NX - 1)]
-        else:
-            x_tile, l_tile, b_tile = tiles_of_rows(all_ref.at[k])
-            moved = vel_ref[k]
-        return x_tile + step * moved, l_tile, b_tile
-
-    for side in range(NC):
-        moved = jnp.where(row == 3, 0.0, chip_vel_ref[side])
-        chip_x_ref[side] = chip_ref[side, 0:8] + step * moved
+            tile = near_ref.at[core, k - NDEV]
+            return position_ref[core, k - NDEV], tile[8:16], tile[16:24]
+        x_tile, l_tile, b_tile = tiles_of_rows(all_ref.at[k])
+        return x_tile + step * vel_ref[k], l_tile, b_tile
 
     def get_target(side):
-        return chip_x_ref[side], chip_ref[side, 8:16], chip_ref[side, 16:24]
+        return position_ref[side, 0], near_ref[side, 0, 8:16], near_ref[side, 0, 16:24]
 
     pair_body(list_ref, count_ref, get_source, get_target, force_ref, *scratch)
 
 
-def finish_kernel(last, codes_ref, stress_ref, parts_ref, chip_ref, x_ref, vel_ref, out_ref):
-    core = codes_ref[6, 0]
+def finish_kernel(codes_ref, stress_ref, parts_ref, near_ref, x_ref, vel_ref, out_ref):
+    core, x_index = codes_ref[6, 0], codes_ref[6, 2]
     row = sublane()
     lane = lax.broadcasted_iota(jnp.int32, (8, SEG), 1)
-    tops = []
-    tiles = []
-    for side in range(NC):
-        x_tile = x_ref[side, 0:8]
-        l_tile = chip_ref[side, 8:16]
-        b_tile = chip_ref[side, 16:24]
+    spare = lax.bitwise_and(row, 3) == 3
+    top = jnp.zeros((1, SEG), F32)
+    for side, s in [(side, s) for side in range(NC) for s in range(NX)]:
+        x_tile = x_ref[side, s, 0:8]
+        l_tile = near_ref[side, s, 8:16]
+        b_tile = near_ref[side, s, 16:24]
         rows = []
         for block in range(2):
             b = burgers_rows(l_tile, b_tile, block)
@@ -321,25 +310,17 @@
         left = jnp.where(lane == 0, x_tile, pltpu.roll(x_tile, 1, 1))
         right = jnp.where(lane == SEG - 1, x_tile, pltpu.roll(x_tile, SEG - 1, 1))
         chain = left + right - 2.0 * x_tile
-        pair = parts_ref[0, side] + parts_ref[1, side]
+        at = NC * lax.bitwise_and(x_index - s, NX - 1)
+        pair = parts_ref[at, side] + parts_ref[at + 1, side]
         drag = jnp.where(row < 4, b_tile[4:5], b_tile[5:6])
         velocity = (COUPLE * pair + applied + TENSION * chain) / drag
+        velocity = jnp.where(spare, 0.0, velocity)
+        vel_ref[side, s] = velocity
         speed = velocity * velocity
-        tops.append(
-            jnp.maximum(
-                speed[0:1] + speed[1:2] + speed[2:3], speed[4:5] + speed[5:6] + speed[6:7]
-            )
-        )
-        tiles.append(velocity)
-    top = jnp.maximum(tops[0], tops[1])
-    for side in range(NC):
-        vel_ref[side] = jnp.where(row == 3, top, jnp.where(row == 7, 0.0, tiles[side]))
-    if last:
-        out_ref[...] = jnp.broadcast_to(top[None], out_ref.shape)
-    else:
-        mine = vel_ref[core]
-        for peer in range(NX):
-            out_ref[peer] = mine
+        top = jnp.maximum(top, speed[0:1] + speed[1:2] + speed[2:3])
+        top = jnp.maximum(top, speed[4:5] + speed[5:6] + speed[6:7])
+    send = top if out_ref.shape[1] == 1 else jnp.where(row == 3, top, vel_ref[core, 0])
+    out_ref[...] = jnp.broadcast_to(send[None], out_ref.shape)
 
 
 def pack_kernel(seg_ref, drag_ref, send_ref, part_ref, raw_ref, out_ref):
@@ -360,22 +341,12 @@
             out_ref[peer, at] = rows
 
 
-def relay_kernel(codes_ref, near_ref, out_ref):
-    x_index = codes_ref[6, 2]
-    top = near_ref[0]
-    for x in range(1, NX):
-        top = jnp.maximum(top, near_ref[x])
-    tile = jnp.where(sublane() == 3, top, near_ref[x_index])
-    for peer in range(NZ):
-        out_ref[peer] = tile
-
-
 def last_kernel(codes_ref, top_ref, x_ref, vel_ref, pos_out, vel_out):
     core = codes_ref[6, 0]
     top = jnp.max(jnp.max(top_ref[...], axis=0), axis=1, keepdims=True)
     step = STEP_LENGTH / (jnp.sqrt(top) + EPSILON)
-    velocity = vel_ref[core]
-    moved = x_ref[core] + step * velocity
+    velocity = vel_ref[core, 0]
+    moved = x_ref[core, 0] + step * velocity
     for block in range(2):
         for comp in range(3):
             pos_out[comp, block, :] = moved[4 * block + comp]
@@ -428,8 +399,9 @@
         mib=56,
     )
     along_z = exchange(to_z, "z")
-    chip = lax.all_gather(raw, "c", axis=0)
     group = [raw] + [pass_x(raw, shift) for shift in range(1, NX)]
+    near = lax.all_gather(jnp.stack(group), "c", axis=0)
+    chip = near[:, 0]
 
     lane = lax.broadcasted_iota(jnp.int32, (NC, SEG), 1)
     side = lax.broadcasted_iota(jnp.int32, (NC, SEG), 0)
@@ -457,7 +429,7 @@
     force, items, count = call(
         first_kernel,
         "first_pairs",
-        (codes, everyone, *group, chip),
+        (codes, everyone, near),
         [
             shape(NC, 8, SEG),
             shape(1, LIST, dtype=jnp.int32),
@@ -468,39 +440,34 @@
         scratch=SCRATCH,
         mib=16,
     )
-    chip_vel, to_near = call(
-        functools.partial(finish_kernel, False),
-        "finish",
-        (codes, stress, lax.all_gather(force, "c", axis=0), chip, chip),
-        [shape(NC, 8, SEG), shape(NX, 8, SEG)],
-        smem_in=2,
-    )
-    near = exchange(to_near, "x")
-    (to_z,) = call(relay_kernel, "relay", (codes, near), [shape(NZ, 8, SEG)], smem_in=1)
+    def finish(force, position, peers, name):
+        return call(
+            finish_kernel,
+            name,
+            (codes, stress, exchange(jnp.broadcast_to(force[None], (8, *force.shape)), ("x", "c")), near, position),
+            [shape(NC, NX, 8, SEG), shape(*peers, SEG)],
+            smem_in=2,
+        )
+
+    near_vel, to_z = finish(force, near, (NZ, 8), "finish")
     along_z = exchange(to_z, "z").reshape(1, NZ * 8, SEG)
     vel_all = exchange(jnp.broadcast_to(along_z, (NY, NZ * 8, SEG)), "y").reshape(NDEV, 8, SEG)
 
     force, position = call(
         second_kernel,
         "second_pairs",
-        (codes, items, count, everyone, *group, chip, vel_all, near, chip_vel),
-        [shape(NC, 8, SEG), shape(NC, 8, SEG)],
+        (codes, items, count, everyone, near, vel_all, near_vel),
+        [shape(NC, 8, SEG), shape(NC, NX, 8, SEG)],
         smem_in=3,
         scratch=SCRATCH,
         mib=16,
     )
-    chip_vel, to_all = call(
-        functools.partial(finish_kernel, True),
-        "finish_last",
-        (codes, stress, lax.all_gather(force, "c", axis=0), chip, position),
-        [shape(NC, 8, SEG), shape(NDEV * NX, 1, SEG)],
-        smem_in=2,
-    )
-    tops = exchange(to_all, ("y", "z", "x"))
+    near_vel, to_all = finish(force, position, (NDEV, 1), "finish_last")
+    tops = exchange(to_all, ("y", "z"))
     positions, velocity = call(
         last_kernel,
         "last",
-        (codes, tops, position, chip_vel),
+        (codes, tops, position, near_vel),
         [shape(3, 2, SEG), shape(3, 2, SEG)],
         smem_in=1,
     )

time: 137 us -> 131 us (0.956)
  blocking collectives: 83.2 us -> 77.5 us
    all_gather x3 -> x1, blocking collectives: 19.5 us -> 6.18 us  [local(): near = lax.all_gather(jnp.stack(group), 'c', axis=0)]
    all_to_all x4 -> x5, blocking collectives: 63.7 us -> 71.3 us  [exchange(): return lax.all_to_all(value, axes, 0, 0, tiled=True)]
    pallas_call x7 -> x6, Pallas kernels: 17.6 us -> 17 us  [call(): pl.pallas_call(kernel, name=name, in_specs=[SMEM] * smem_in + [VMEM] * (l...]
where the time goes in v6:
time: 131 us; the launch traced here: 130 us
  blocking collectives  77.5 us (59%)
  starting transfers between devices  29.4 us (22%)
  Pallas kernels  17 us (13%)
  waiting for transfers between devices  4.22 us (3%)
    all_to_all x5, blocking collectives, exchange(): return lax.all_to_all(value, axes, 0, 0, tiled=True)  71.3 us
    all_to_all x2, starting transfers between devices, exchange(): return lax.all_to_all(value, axes, 0, 0, tiled=True)  20.1 us
    pallas_call x6, Pallas kernels, call(): pl.pallas_call(kernel, name=name, in_specs=[SMEM] * smem_in + [VMEM] * (l...  17 us
    ppermute x3, starting transfers between devices, pass_x(): return lax.ppermute(value, 'x', [(i, (i + shift) % NX) for i in range(NX)])  9.33 us
    all_gather x1, blocking collectives, local(): near = lax.all_gather(jnp.stack(group), 'c', axis=0)  6.18 us
    all_to_all x2, waiting for transfers between devices, exchange(): return lax.all_to_all(value, axes, 0, 0, tiled=True)  4.21 us
  transfers between devices with their start and end apart: 5, of which 2 were waited for; matrix products, arithmetic and copies ran while one was open for 1% of the time, Pallas kernels for 0%

profile of v6, /device:TPU:1, one launch (start us, length us, event | category | flops | bytes accessed | tf_op | source)
XLA Modules:
  0.0 130.3 jit_solution(3136703940640108048)
XLA Ops:
  0.6 1.4 %pack.1 = (f32[24,128]{1,0:T(8,128)}, f32[16,5,4,128]{3,2,1,0:T(4,128)}) custom-call(f32[9,2,128]{2,1,0:T(2,128)} %bitcast.51, f32[2,128]{1,0:T(2,128)} %drag_ref.1, s32[1,128]{1,0:T(1,128)} %bitcast.52, s32[1,128]{1,0:T(1,128)} %bitcast.53), custom_call_target="tpu_custom_call" | custom-call | tf_op jit(solution)/shard_map/pack/pallas_call | solution.py:365
  2.0 15.9 %all-to-all-start = ((f32[16,5,4,128]{3,2,1,0:T(4,128)}), f32[16,5,4,128]{3,2,1,0:T(4,128)S(1)}, u32[]{:S(2)}, u32[]{:S(2)}) async-start(f32[16,5,4,128]{3,2,1,0:T(4,128)} %get-tuple-element.15), calls=%async_computation | async-start | bytes 327680 | tf_op jit(solution)/shard_map/all_to_all | solution.py:381
  17.9 4.4 %collective-permute-start.2 = (f32[24,128]{1,0:T(8,128)S(1)}, f32[24,128]{1,0:T(8,128)S(1)}, u32[]{:S(2)}, u32[]{:S(2)}) collective-permute-start(f32[24,128]{1,0:T(8,128)S(1)} %copy-done.1), channel_id=1, source_target_pairs={{0,3},{1,0},{2,1},{3,2},{4,7},{5,4},{6,5},{7,6},{8,11},{9,8},{10,9... | collective-permute-start | bytes 36872 | tf_op jit(solution)/shard_map/ppermute | solution.py:377
  22.3 2.4 %collective-permute-start.1 = (f32[24,128]{1,0:T(8,128)S(1)}, f32[24,128]{1,0:T(8,128)S(1)}, u32[]{:S(2)}, u32[]{:S(2)}) collective-permute-start(f32[24,128]{1,0:T(8,128)S(1)} %copy-done.1), channel_id=1, source_target_pairs={{0,2},{1,3},{2,0},{3,1},{4,6},{5,7},{6,4},{7,5},{8,10},{9,11},{10,... | collective-permute-start | bytes 36872 | tf_op jit(solution)/shard_map/ppermute | solution.py:377
  24.8 2.5 %collective-permute-start = (f32[24,128]{1,0:T(8,128)S(1)}, f32[24,128]{1,0:T(8,128)S(1)}, u32[]{:S(2)}, u32[]{:S(2)}) collective-permute-start(f32[24,128]{1,0:T(8,128)S(1)} %copy-done.1), channel_id=1, source_target_pairs={{0,1},{1,2},{2,3},{3,0},{4,5},{5,6},{6,7},{7,4},{8,9},{9,10},{10,1... | collective-permute-start | bytes 36872 | tf_op jit(solution)/shard_map/ppermute | solution.py:377
  27.3 2.9 %all-to-all-done = f32[16,5,4,128]{3,2,1,0:T(4,128)S(1)} async-done(((f32[16,5,4,128]{3,2,1,0:T(4,128)}), f32[16,5,4,128]{3,2,1,0:T(4,128)S(1)}, u32[]{:S(2)}, u32[]{:S(2)}) %all-to-all-start) | async-done | bytes 163872 | tf_op jit(solution)/shard_map/all_to_all | solution.py:381
  30.2 0.9 broadcast_in_dim.44
  31.1 4.2 %all-to-all-start.1 = ((f32[4,80,4,128]{3,2,1,0:T(4,128)}), f32[4,80,4,128]{3,2,1,0:T(4,128)S(1)}, u32[]{:S(2)}, u32[]{:S(2)}) async-start(f32[4,80,4,128]{3,2,1,0:T(4,128)} %broadcast_in_dim.44), calls=%async_computation.1 | async-start | bytes 1310720 | tf_op jit(solution)/shard_map/all_to_all | solution.py:381
  35.3 6.2 %all-gather = f32[8,24,128]{2,1,0:T(8,128)S(1)} all-gather(f32[4,24,128]{2,1,0:T(8,128)S(1)} %pad_maximum_fusion), channel_id=2, replica_groups=mesh['y'=4,'z'=16,'c'=2,'x'=4] {'c'}, dimensions={0}, use_global_device_ids=true | all-gather | bytes 147456 | tf_op jit(solution)/shard_map/all_gather | solution.py:403
  41.5 1.4 %all-to-all-done.1 = f32[4,80,4,128]{3,2,1,0:T(4,128)S(1)} async-done(((f32[4,80,4,128]{3,2,1,0:T(4,128)}), f32[4,80,4,128]{3,2,1,0:T(4,128)S(1)}, u32[]{:S(2)}, u32[]{:S(2)}) %all-to-all-start.1) | async-done | bytes 655392 | tf_op jit(solution)/shard_map/all_to_all | solution.py:381
  42.9 0.1 slice.25
  43.0 0.2 convolution_convert_fusion
  43.1 0.1 slice.20
  43.2 0.1 compare_select_fusion.2
  43.4 6.6 %first_pairs.1 = (f32[2,8,128]{2,1,0:T(8,128)S(1)}, s32[1,320]{1,0:T(1,128)S(1)}, s32[1,1]{1,0:T(1,128)}) custom-call(s32[8,128]{1,0:T(8,128)S(1)} %concatenate.7.codes_ref, f32[64,5,4,128]{3,2,1,0:T(4,128)S(1)} %bitcast.33, f32[2,4,24,128]{3,2,1,0:T(8,128)S(1)} %bitcast.36), custom_call_target="tpu_custom_call" | custom-call | tf_op jit(solution)/shard_map/first_pairs/pallas_call | solution.py:365
  50.0 14.7 %all_to_all.35.parts_ref = f32[8,2,8,128]{3,2,1,0:T(8,128)S(1)} all-to-all(f32[8,2,8,128]{3,2,1,0:T(8,128)S(1)} %broadcast_in_dim.49), channel_id=1, replica_groups=mesh['y'=4,'z'=16,'c'=2,'x'=4] {'x','c'}, dimensions={0} | all-to-all | bytes 131072 | tf_op jit(solution)/shard_map/all_to_all | solution.py:381
  64.8 0.7 finish.1
  65.5 19.0 %all_to_all.36 = f32[16,8,128]{2,1,0:T(8,128)S(1)} all-to-all(f32[16,8,128]{2,1,0:T(8,128)S(1)} %get-tuple-element.20), channel_id=1, replica_groups=mesh['y'=4,'z'=16,'c'=2,'x'=4] {'z'}, dimensions={0} | all-to-all | bytes 131072 | tf_op jit(solution)/shard_map/all_to_all | solution.py:381
  84.5 7.9 %all_to_all.37 = f32[4,128,128]{2,1,0:T(8,128)S(1)} all-to-all(f32[4,128,128]{2,1,0:T(8,128)S(1)} %broadcast_in_dim.51), channel_id=1, replica_groups=mesh['y'=4,'z'=16,'c'=2,'x'=4] {'y'}, dimensions={0} | all-to-all | bytes 524288 | tf_op jit(solution)/shard_map/all_to_all | solution.py:381
  92.4 6.2 %second_pairs.1 = (f32[2,8,128]{2,1,0:T(8,128)S(1)}, f32[2,4,8,128]{3,2,1,0:T(8,128)S(1)}) custom-call(s32[8,128]{1,0:T(8,128)S(1)} %concatenate.7.codes_ref, s32[1,320]{1,0:T(1,128)S(1)} %get-tuple-element.17.list_ref, s32[1,1]{1,0:T(1,128)} %get-tuple-element.18.count_ref, f32[64,5,4,128]{3,2,1,0:T(4,128)S(1)} %bitcast.34, f32[2,4,24,128]{3,2,1,0:T(8,128)S(1)} %bitcast.39, ...), custom_call_target="tpu_custom_call" | custom-call | tf_op jit(solution)/shard_map/second_pairs/pallas_call | solution.py:365
  98.6 11.1 %all_to_all.38.parts_ref = f32[8,2,8,128]{3,2,1,0:T(8,128)S(1)} all-to-all(f32[8,2,8,128]{3,2,1,0:T(8,128)S(1)} %broadcast_in_dim.52), channel_id=1, replica_groups=mesh['y'=4,'z'=16,'c'=2,'x'=4] {'x','c'}, dimensions={0} | all-to-all | bytes 131072 | tf_op jit(solution)/shard_map/all_to_all | solution.py:381
  109.7 0.8 finish_last.1
  110.5 18.5 %all_to_all.39.top_ref = f32[64,1,128]{2,1,0:T(1,128)S(1)} all-to-all(f32[64,1,128]{2,1,0:T(1,128)S(1)} %get-tuple-element.24), channel_id=1, replica_groups=mesh['y'=4,'z'=16,'c'=2,'x'=4] {'y','z'}, dimensions={0} | all-to-all | bytes 65536 | tf_op jit(solution)/shard_map/all_to_all | solution.py:381
  129.0 1.3 last.1
  (20 shorter events, 0.2 us)
Async XLA Ops:
  2.0 15.9 %copy-start.1 = (f32[24,128]{1,0:T(8,128)S(1)}, f32[24,128]{1,0:T(8,128)}, u32[]{:S(2)}) copy-start(f32[24,128]{1,0:T(8,128)} %get-tuple-element.16) | copy-start | bytes 36868
  2.0 28.1 %all-to-all-start = ((f32[16,5,4,128]{3,2,1,0:T(4,128)}), f32[16,5,4,128]{3,2,1,0:T(4,128)S(1)}, u32[]{:S(2)}, u32[]{:S(2)}) async-start(f32[16,5,4,128]{3,2,1,0:T(4,128)} %get-tuple-element.15), calls=%async_computation | async-start | bytes 327680 | tf_op jit(solution)/shard_map/all_to_all | solution.py:381
  17.9 17.4 %collective-permute-start.2 = (f32[24,128]{1,0:T(8,128)S(1)}, f32[24,128]{1,0:T(8,128)S(1)}, u32[]{:S(2)}, u32[]{:S(2)}) collective-permute-start(f32[24,128]{1,0:T(8,128)S(1)} %copy-done.1), channel_id=1, source_target_pairs={{0,3},{1,0},{2,1},{3,2},{4,7},{5,4},{6,5},{7,6},{8,11},{9,8},{10,9... | collective-permute-start | bytes 36872 | tf_op jit(solution)/shard_map/ppermute | solution.py:377
  22.3 13.0 %collective-permute-start.1 = (f32[24,128]{1,0:T(8,128)S(1)}, f32[24,128]{1,0:T(8,128)S(1)}, u32[]{:S(2)}, u32[]{:S(2)}) collective-permute-start(f32[24,128]{1,0:T(8,128)S(1)} %copy-done.1), channel_id=1, source_target_pairs={{0,2},{1,3},{2,0},{3,1},{4,6},{5,7},{6,4},{7,5},{8,10},{9,11},{10,... | collective-permute-start | bytes 36872 | tf_op jit(solution)/shard_map/ppermute | solution.py:377
  24.8 10.5 %collective-permute-start = (f32[24,128]{1,0:T(8,128)S(1)}, f32[24,128]{1,0:T(8,128)S(1)}, u32[]{:S(2)}, u32[]{:S(2)}) collective-permute-start(f32[24,128]{1,0:T(8,128)S(1)} %copy-done.1), channel_id=1, source_target_pairs={{0,1},{1,2},{2,3},{3,0},{4,5},{5,6},{6,7},{7,4},{8,9},{9,10},{10,1... | collective-permute-start | bytes 36872 | tf_op jit(solution)/shard_map/ppermute | solution.py:377
  31.1 11.8 %all-to-all-start.1 = ((f32[4,80,4,128]{3,2,1,0:T(4,128)}), f32[4,80,4,128]{3,2,1,0:T(4,128)S(1)}, u32[]{:S(2)}, u32[]{:S(2)}) async-start(f32[4,80,4,128]{3,2,1,0:T(4,128)} %broadcast_in_dim.44), calls=%async_computation.1 | async-start | bytes 1310720 | tf_op jit(solution)/shard_map/all_to_all | solution.py:381
  50.0 14.8 %copy-start = (f32[3,3]{1,0:T(4,128)S(1)}, f32[3,3]{1,0:T(4,128)}, u32[]{:S(2)}) copy-start(f32[3,3]{1,0:T(4,128)} %stress_ref.3) | copy-start | bytes 112

commit v7 on v6

--- a/solution.py
+++ b/solution.py
@@ -134,7 +134,9 @@
     count = count + 4 * NX
     for j in range(BATCH):
         list_ref[0, count + j] = DUMMY
-    count_ref[0, 0] = lax.div(count + (BATCH - 1), BATCH)
+    whole = lax.div(count + (BATCH // 2 - 1), BATCH)
+    count_ref[0, 0] = whole
+    count_ref[0, 1] = (count > whole * BATCH).astype(jnp.int32)
 
 
 def pair_body(list_ref, count_ref, get_source, get_target, force_ref, source_s, moment_s, target_s):
@@ -167,10 +169,10 @@
                 target_s[at, 0:SEG] = jnp.where(keep, dist, 0.0).astype(BF16)
                 target_s[at, SEG : 2 * SEG] = jnp.where(mine, weight, 0.0).astype(BF16)
 
-    def items(step, total):
+    def items(start, size, total):
         lows, highs, moments = [], [], []
-        for b in range(BATCH):
-            code = list_ref[0, step * BATCH + b]
+        for b in range(size):
+            code = list_ref[0, start + b]
             n = lax.shift_right_logical(code, 8)
             m = lax.bitwise_and(code, 255)
             at = 2 * n + lax.bitwise_and(m, 1)
@@ -193,7 +195,19 @@
             rhs, lhs, (((1,), (1,)), ((), ())), preferred_element_type=F32
         )
 
-    total = lax.fori_loop(0, count_ref[0, 0], items, jnp.zeros((SEG, 64), F32))
+    whole = count_ref[0, 0]
+    total = lax.fori_loop(
+        0,
+        whole,
+        lambda step, total: items(step * BATCH, BATCH, total),
+        jnp.zeros((SEG, 64), F32),
+    )
+    total = lax.fori_loop(
+        0,
+        count_ref[0, 1],
+        lambda step, total: items(whole * BATCH, BATCH // 2, total),
+        total,
+    )
     total = jnp.concatenate([total, jnp.zeros((SEG, SEG - 64), F32)], axis=1).T
     for side in range(NC):
         x_tile = get_target(side)[0]
@@ -399,7 +413,8 @@
         mib=56,
     )
     along_z = exchange(to_z, "z")
-    group = [raw] + [pass_x(raw, shift) for shift in range(1, NX)]
+    late, along_z = lax.optimization_barrier((raw, along_z))
+    group = [raw, pass_x(raw, 1), pass_x(raw, 2), pass_x(late, 3)]
     near = lax.all_gather(jnp.stack(group), "c", axis=0)
     chip = near[:, 0]
 
@@ -433,7 +448,7 @@
         [
             shape(NC, 8, SEG),
             shape(1, LIST, dtype=jnp.int32),
-            shape(1, 1, dtype=jnp.int32),
+            shape(1, 2, dtype=jnp.int32),
         ],
         smem_in=1,
         smem_out=2,
@@ -449,9 +464,8 @@
             smem_in=2,
         )
 
-    near_vel, to_z = finish(force, near, (NZ, 8), "finish")
-    along_z = exchange(to_z, "z").reshape(1, NZ * 8, SEG)
-    vel_all = exchange(jnp.broadcast_to(along_z, (NY, NZ * 8, SEG)), "y").reshape(NDEV, 8, SEG)
+    near_vel, to_all = finish(force, near, (NDEV, 8), "finish")
+    vel_all = exchange(to_all, ("y", "z"))
 
     force, position = call(
         second_kernel,

time: 131 us -> 132 us (level)
  blocking collectives: 77.5 us -> 70.3 us
  Pallas kernels: 17 us -> 21.4 us
  starting transfers between devices: 29.4 us -> 31.9 us
    all_to_all x5 -> x4, blocking collectives: 71.3 us -> 63.3 us  [exchange(): return lax.all_to_all(value, axes, 0, 0, tiled=True)]
    pallas_call x6, Pallas kernels: 17 us -> 21.4 us  [call(): pl.pallas_call(kernel, name=name, in_specs=[SMEM] * smem_in + [VMEM] * (l...]
    ppermute x3, starting transfers between devices: 9.33 us -> 11.9 us  [pass_x(): return lax.ppermute(value, 'x', [(i, (i + shift) % NX) for i in range(NX)])]
where the time goes in v7:
time: 132 us; the launch traced here: 131 us
  blocking collectives  70.3 us (53%)
  starting transfers between devices  31.9 us (24%)
  Pallas kernels  21.4 us (16%)
  waiting for transfers between devices  5.49 us (4%)
    all_to_all x4, blocking collectives, exchange(): return lax.all_to_all(value, axes, 0, 0, tiled=True)  63.3 us
    pallas_call x6, Pallas kernels, call(): pl.pallas_call(kernel, name=name, in_specs=[SMEM] * smem_in + [VMEM] * (l...  21.4 us
    all_to_all x2, starting transfers between devices, exchange(): return lax.all_to_all(value, axes, 0, 0, tiled=True)  20.1 us
    ppermute x3, starting transfers between devices, pass_x(): return lax.ppermute(value, 'x', [(i, (i + shift) % NX) for i in range(NX)])  11.9 us
    all_gather x1, blocking collectives, local(): near = lax.all_gather(jnp.stack(group), 'c', axis=0)  7.02 us
    all_to_all x2, waiting for transfers between devices, exchange(): return lax.all_to_all(value, axes, 0, 0, tiled=True)  4.72 us
  transfers between devices with their start and end apart: 5, of which 2 were waited for; matrix products, arithmetic and copies ran while one was open for 1% of the time, Pallas kernels for 0%

profile of v7, /device:TPU:1, one launch (start us, length us, event | category | flops | bytes accessed | tf_op | source)
XLA Modules:
  0.0 131.4 jit_solution(13407374049539290840)
XLA Ops:
  0.6 1.4 %pack.1 = (f32[24,128]{1,0:T(8,128)}, f32[16,5,4,128]{3,2,1,0:T(4,128)}) custom-call(f32[9,2,128]{2,1,0:T(2,128)} %bitcast.47, f32[2,128]{1,0:T(2,128)} %drag_ref.1, s32[1,128]{1,0:T(1,128)} %bitcast.48, s32[1,128]{1,0:T(1,128)} %bitcast.49), custom_call_target="tpu_custom_call" | custom-call | tf_op jit(solution)/shard_map/pack/pallas_call | solution.py:379
  2.0 15.9 %all-to-all-start = ((f32[16,5,4,128]{3,2,1,0:T(4,128)}), f32[16,5,4,128]{3,2,1,0:T(4,128)S(1)}, u32[]{:S(2)}, u32[]{:S(2)}) async-start(f32[16,5,4,128]{3,2,1,0:T(4,128)} %get-tuple-element.18), calls=%async_computation | async-start | bytes 327680 | tf_op jit(solution)/shard_map/all_to_all | solution.py:395
  17.9 3.1 %collective-permute-start = (f32[24,128]{1,0:T(8,128)S(1)}, f32[24,128]{1,0:T(8,128)S(1)}, u32[]{:S(2)}, u32[]{:S(2)}) collective-permute-start(f32[24,128]{1,0:T(8,128)S(1)} %copy-done.1), channel_id=1, source_target_pairs={{0,1},{1,2},{2,3},{3,0},{4,5},{5,6},{6,7},{7,4},{8,9},{9,10},{10,1... | collective-permute-start | bytes 36872 | tf_op jit(solution)/shard_map/ppermute | solution.py:391
  21.1 4.4 %collective-permute-start.1 = (f32[24,128]{1,0:T(8,128)S(1)}, f32[24,128]{1,0:T(8,128)S(1)}, u32[]{:S(2)}, u32[]{:S(2)}) collective-permute-start(f32[24,128]{1,0:T(8,128)S(1)} %copy-done.1), channel_id=1, source_target_pairs={{0,2},{1,3},{2,0},{3,1},{4,6},{5,7},{6,4},{7,5},{8,10},{9,11},{10,... | collective-permute-start | bytes 36872 | tf_op jit(solution)/shard_map/ppermute | solution.py:391
  25.4 4.7 %all-to-all-done = f32[16,5,4,128]{3,2,1,0:T(4,128)S(1)} async-done(((f32[16,5,4,128]{3,2,1,0:T(4,128)}), f32[16,5,4,128]{3,2,1,0:T(4,128)S(1)}, u32[]{:S(2)}, u32[]{:S(2)}) %all-to-all-start) | async-done | bytes 163872 | tf_op jit(solution)/shard_map/all_to_all | solution.py:395
  30.2 0.9 broadcast_in_dim.37
  31.1 4.2 %all-to-all-start.1 = ((f32[4,80,4,128]{3,2,1,0:T(4,128)}), f32[4,80,4,128]{3,2,1,0:T(4,128)S(1)}, u32[]{:S(2)}, u32[]{:S(2)}) async-start(f32[4,80,4,128]{3,2,1,0:T(4,128)} %broadcast_in_dim.37), calls=%async_computation.1 | async-start | bytes 1310720 | tf_op jit(solution)/shard_map/all_to_all | solution.py:395
  35.3 4.4 %collective-permute-start.2 = (f32[24,128]{1,0:T(8,128)S(1)}, f32[24,128]{1,0:T(8,128)S(1)}, u32[]{:S(2)}, u32[]{:S(2)}) collective-permute-start(f32[24,128]{1,0:T(8,128)S(1)} %copy-done.1), channel_id=1, source_target_pairs={{0,3},{1,0},{2,1},{3,2},{4,7},{5,4},{6,5},{7,6},{8,11},{9,8},{10,9... | collective-permute-start | bytes 36872 | tf_op jit(solution)/shard_map/ppermute | solution.py:391
  39.7 0.8 collective-permute-done.2
  40.5 7.0 %all-gather = f32[8,24,128]{2,1,0:T(8,128)S(1)} all-gather(f32[4,24,128]{2,1,0:T(8,128)S(1)} %pad_maximum_fusion), channel_id=2, replica_groups=mesh['y'=4,'z'=16,'c'=2,'x'=4] {'c'}, dimensions={0}, use_global_device_ids=true | all-gather | bytes 147456 | tf_op jit(solution)/shard_map/all_gather | solution.py:418
  47.5 0.1 slice.25
  47.6 0.2 convolution_convert_fusion
  47.8 0.1 slice.20
  47.9 0.1 compare_select_fusion.2
  48.0 0.1 concatenate.7.codes_ref
  48.0 9.2 %first_pairs.1 = (f32[2,8,128]{2,1,0:T(8,128)S(1)}, s32[1,320]{1,0:T(1,128)S(1)}, s32[1,2]{1,0:T(1,128)S(1)}) custom-call(s32[8,128]{1,0:T(8,128)S(1)} %concatenate.7.codes_ref, f32[64,5,4,128]{3,2,1,0:T(4,128)S(1)} %bitcast.31, f32[2,4,24,128]{3,2,1,0:T(8,128)S(1)} %bitcast.34), custom_call_target="tpu_custom_call" | custom-call | tf_op jit(solution)/shard_map/first_pairs/pallas_call | solution.py:379
  57.2 8.8 %all_to_all.30.parts_ref = f32[8,2,8,128]{3,2,1,0:T(8,128)S(1)} all-to-all(f32[8,2,8,128]{3,2,1,0:T(8,128)S(1)} %broadcast_in_dim.42), channel_id=1, replica_groups=mesh['y'=4,'z'=16,'c'=2,'x'=4] {'x','c'}, dimensions={0} | all-to-all | bytes 131072 | tf_op jit(solution)/shard_map/all_to_all | solution.py:395
  66.1 0.8 finish.1
  66.8 26.4 %all_to_all.31.vel_ref = f32[64,8,128]{2,1,0:T(8,128)S(1)} all-to-all(f32[64,8,128]{2,1,0:T(8,128)S(1)} %get-tuple-element.24), channel_id=1, replica_groups=mesh['y'=4,'z'=16,'c'=2,'x'=4] {'y','z'}, dimensions={0} | all-to-all | bytes 524288 | tf_op jit(solution)/shard_map/all_to_all | solution.py:395
  93.2 8.1 %second_pairs.1 = (f32[2,8,128]{2,1,0:T(8,128)S(1)}, f32[2,4,8,128]{3,2,1,0:T(8,128)S(1)}) custom-call(s32[8,128]{1,0:T(8,128)S(1)} %concatenate.7.codes_ref, s32[1,320]{1,0:T(1,128)S(1)} %get-tuple-element.21.list_ref, s32[1,2]{1,0:T(1,128)S(1)} %get-tuple-element.22.count_ref, f32[64,5,4,128]{3,2,1,0:T(4,128)S(1)} %bitcast.32, ...), custom_call_target="tpu_custom_call" | custom-call | tf_op jit(solution)/shard_map/second_pairs/pallas_call | solution.py:379
  101.3 10.1 %all_to_all.32.parts_ref = f32[8,2,8,128]{3,2,1,0:T(8,128)S(1)} all-to-all(f32[8,2,8,128]{3,2,1,0:T(8,128)S(1)} %broadcast_in_dim.43), channel_id=1, replica_groups=mesh['y'=4,'z'=16,'c'=2,'x'=4] {'x','c'}, dimensions={0} | all-to-all | bytes 131072 | tf_op jit(solution)/shard_map/all_to_all | solution.py:395
  111.4 0.8 finish_last.1
  112.2 18.0 %all_to_all.33.top_ref = f32[64,1,128]{2,1,0:T(1,128)S(1)} all-to-all(f32[64,1,128]{2,1,0:T(1,128)S(1)} %get-tuple-element.28), channel_id=1, replica_groups=mesh['y'=4,'z'=16,'c'=2,'x'=4] {'y','z'}, dimensions={0} | all-to-all | bytes 65536 | tf_op jit(solution)/shard_map/all_to_all | solution.py:395
  130.2 1.3 last.1
  (18 shorter events, 0.1 us)
Async XLA Ops:
  2.0 15.9 %copy-start.1 = (f32[24,128]{1,0:T(8,128)S(1)}, f32[24,128]{1,0:T(8,128)}, u32[]{:S(2)}) copy-start(f32[24,128]{1,0:T(8,128)} %get-tuple-element.20) | copy-start | bytes 36868
  2.0 28.1 %all-to-all-start = ((f32[16,5,4,128]{3,2,1,0:T(4,128)}), f32[16,5,4,128]{3,2,1,0:T(4,128)S(1)}, u32[]{:S(2)}, u32[]{:S(2)}) async-start(f32[16,5,4,128]{3,2,1,0:T(4,128)} %get-tuple-element.18), calls=%async_computation | async-start | bytes 327680 | tf_op jit(solution)/shard_map/all_to_all | solution.py:395
  17.9 21.8 %collective-permute-start = (f32[24,128]{1,0:T(8,128)S(1)}, f32[24,128]{1,0:T(8,128)S(1)}, u32[]{:S(2)}, u32[]{:S(2)}) collective-permute-start(f32[24,128]{1,0:T(8,128)S(1)} %copy-done.1), channel_id=1, source_target_pairs={{0,1},{1,2},{2,3},{3,0},{4,5},{5,6},{6,7},{7,4},{8,9},{9,10},{10,1... | collective-permute-start | bytes 36872 | tf_op jit(solution)/shard_map/ppermute | solution.py:391
  21.1 18.6 %collective-permute-start.1 = (f32[24,128]{1,0:T(8,128)S(1)}, f32[24,128]{1,0:T(8,128)S(1)}, u32[]{:S(2)}, u32[]{:S(2)}) collective-permute-start(f32[24,128]{1,0:T(8,128)S(1)} %copy-done.1), channel_id=1, source_target_pairs={{0,2},{1,3},{2,0},{3,1},{4,6},{5,7},{6,4},{7,5},{8,10},{9,11},{10,... | collective-permute-start | bytes 36872 | tf_op jit(solution)/shard_map/ppermute | solution.py:391
  31.1 16.5 %all-to-all-start.1 = ((f32[4,80,4,128]{3,2,1,0:T(4,128)}), f32[4,80,4,128]{3,2,1,0:T(4,128)S(1)}, u32[]{:S(2)}, u32[]{:S(2)}) async-start(f32[4,80,4,128]{3,2,1,0:T(4,128)} %broadcast_in_dim.37), calls=%async_computation.1 | async-start | bytes 1310720 | tf_op jit(solution)/shard_map/all_to_all | solution.py:395
  35.3 5.2 %collective-permute-start.2 = (f32[24,128]{1,0:T(8,128)S(1)}, f32[24,128]{1,0:T(8,128)S(1)}, u32[]{:S(2)}, u32[]{:S(2)}) collective-permute-start(f32[24,128]{1,0:T(8,128)S(1)} %copy-done.1), channel_id=1, source_target_pairs={{0,3},{1,0},{2,1},{3,2},{4,7},{5,4},{6,5},{7,6},{8,11},{9,8},{10,9... | collective-permute-start | bytes 36872 | tf_op jit(solution)/shard_map/ppermute | solution.py:391
  57.2 8.8 %copy-start = (f32[3,3]{1,0:T(4,128)S(1)}, f32[3,3]{1,0:T(4,128)}, u32[]{:S(2)}) copy-start(f32[3,3]{1,0:T(4,128)} %stress_ref.3) | copy-start | bytes 112

commit v8 on v7

--- a/solution.py
+++ b/solution.py
@@ -23,7 +23,6 @@
 NX = 4
 BATCH = 32
 LIST = 320
-DUMMY = 2 * (NDEV + NX)
 F32 = jnp.float32
 BF16 = jnp.bfloat16
 
@@ -117,29 +116,66 @@
     return jnp.concatenate(dist + [zero] * 9, axis=0), jnp.concatenate([zero] * 7 + weight, axis=0)
 
 
-def build_list(codes_ref, list_ref, count_ref):
-    core = codes_ref[6, 0]
-
-    def add(k, count):
-        for line in range(2 * NC):
-            code = codes_ref[line, 2 * k + core if line >= NC else 2 * k]
-            list_ref[0, count] = code
-            count = count + (code >= 0).astype(jnp.int32)
-        return count
-
-    count = lax.fori_loop(0, NDEV, add, jnp.int32(0), unroll=8)
+def add_code(list_ref, count, code, keep):
+    list_ref[0, count] = code
+    return count + keep.astype(jnp.int32)
+
+
+def add_group(list_ref, count, core, lines):
     for block in range(2):
         for j in range(2 * NX):
-            list_ref[0, count + 2 * NX * block + j] = 256 * (2 * core + block) + 2 * NDEV + j
+            list_ref[0, count + 2 * NX * block + j] = 256 * (2 * core + block) + 2 * lines + j
     count = count + 4 * NX
     for j in range(BATCH):
-        list_ref[0, count + j] = DUMMY
+        list_ref[0, count + j] = 2 * (lines + NX)
+    return count
+
+
+def batches(count):
     whole = lax.div(count + (BATCH // 2 - 1), BATCH)
-    count_ref[0, 0] = whole
-    count_ref[0, 1] = (count > whole * BATCH).astype(jnp.int32)
-
-
-def pair_body(list_ref, count_ref, get_source, get_target, force_ref, source_s, moment_s, target_s):
+    return whole, (count > whole * BATCH).astype(jnp.int32)
+
+
+def build_list(codes_ref, list_ref):
+    core, y_index = codes_ref[6, 0], codes_ref[6, 1]
+
+    def add_in(k, count):
+        for side in range(NC):
+            code = codes_ref[side, 2 * k]
+            count = add_code(list_ref, count, code, code >= 0)
+        return count
+
+    def add_out(at, count):
+        k = lax.bitwise_and(at + NZ * (y_index + 1), NDEV - 1)
+        for side in range(NC):
+            code = codes_ref[NC + side, 2 * k + core]
+            count = add_code(list_ref, count, code, code >= 0)
+        return count
+
+    count = lax.fori_loop(0, NDEV, add_in, jnp.int32(0), unroll=8)
+    first = lax.fori_loop(0, NDEV - NZ, add_out, count, unroll=8)
+    count = lax.fori_loop(NDEV - NZ, NDEV, add_out, first, unroll=8)
+    return first, add_group(list_ref, count, core, NDEV)
+
+
+def build_near_list(codes_ref, list_ref):
+    core, y_index = codes_ref[6, 0], codes_ref[6, 1]
+
+    def add_out(z, count):
+        for side in range(NC):
+            code = codes_ref[NC + side, 2 * (NZ * y_index + z) + core]
+            count = add_code(list_ref, count, code - 2 * NZ * y_index, code >= 0)
+        return count
+
+    count = lax.fori_loop(0, NZ, add_out, jnp.int32(0), unroll=8)
+    return add_group(list_ref, count, core, NZ)
+
+
+def pair_body(
+    list_ref, whole, tail, limit, lines, get_source, get_target, force_ref, scratch, more=None
+):
+    source_s, moment_s, target_s = scratch
+
     def prepare(k):
         tiles, first, second = source_operands(*get_source(k))
         store_rows(source_s, k, tiles)
@@ -150,8 +186,8 @@
         prepare(k)
         return carry
 
-    lax.fori_loop(0, NDEV, prepare_loop, 0, unroll=4)
-    for k in range(NDEV, NDEV + NX + 1):
+    lax.fori_loop(0, lines, prepare_loop, 0, unroll=4)
+    for k in range(lines, lines + NX + 1):
         prepare(k)
 
     lane = lax.broadcasted_iota(jnp.int32, (SEG, SEG), 1)
@@ -173,6 +209,8 @@
         lows, highs, moments = [], [], []
         for b in range(size):
             code = list_ref[0, start + b]
+            if limit is not None:
+                code = jnp.where(start + b < limit, code, 2 * (lines + NX))
             n = lax.shift_right_logical(code, 8)
             m = lax.bitwise_and(code, 255)
             at = 2 * n + lax.bitwise_and(m, 1)
@@ -189,13 +227,16 @@
             moments.append(
                 jnp.concatenate([jnp.where(n == t, moment, zero) for t in range(4)], axis=0)
             )
-        lhs = jnp.concatenate(moments + moments, axis=1)
-        rhs = jnp.concatenate(highs + lows, axis=1)
-        return total + lax.dot_general(
-            rhs, lhs, (((1,), (1,)), ((), ())), preferred_element_type=F32
+        sums = lax.dot_general(
+            jnp.concatenate(
+                [jnp.concatenate(highs, axis=1), jnp.concatenate(lows, axis=1)], axis=0
+            ),
+            jnp.concatenate(moments, axis=1),
+            (((1,), (1,)), ((), ())),
+            preferred_element_type=F32,
         )
-
-    whole = count_ref[0, 0]
+        return total + sums[0:SEG] + sums[SEG : 2 * SEG]
+
     total = lax.fori_loop(
         0,
         whole,
@@ -203,10 +244,7 @@
         jnp.zeros((SEG, 64), F32),
     )
     total = lax.fori_loop(
-        0,
-        count_ref[0, 1],
-        lambda step, total: items(whole * BATCH, BATCH // 2, total),
-        total,
+        0, tail, lambda step, total: items(whole * BATCH, BATCH // 2, total), total
     )
     total = jnp.concatenate([total, jnp.zeros((SEG, SEG - 64), F32)], axis=1).T
     for side in range(NC):
@@ -219,14 +257,16 @@
                 x_block * total[at + 3 : at + 4] - (total[at : at + 3] + total[at + 8 : at + 11])
             )
             rows.append(jnp.zeros((1, SEG), F32))
-        force_ref[side] = jnp.concatenate(rows, axis=0)
-
-
-SCRATCH = [
-    pltpu.VMEM((NDEV + NX + 1, SEG, SEG), BF16),
-    pltpu.VMEM((2 * (NDEV + NX + 1), 16, SEG), BF16),
-    pltpu.VMEM((8, 2 * SEG, SEG), BF16),
-]
+        force = jnp.concatenate(rows, axis=0)
+        force_ref[side] = force if more is None else force + more[side]
+
+
+def scratch_of(lines):
+    return [
+        pltpu.VMEM((lines + NX + 1, SEG, SEG), BF16),
+        pltpu.VMEM((2 * (lines + NX + 1), 16, SEG), BF16),
+        pltpu.VMEM((8, 2 * SEG, SEG), BF16),
+    ]
 
 
 def tiles_of(tile):
@@ -246,19 +286,44 @@
     return zero, zero, zero
 
 
-def first_kernel(codes_ref, all_ref, near_ref, force_ref, list_ref, count_ref, *scratch):
-    build_list(codes_ref, list_ref, count_ref)
+def near_kernel(codes_ref, line_ref, near_ref, force_ref, list_s, *scratch):
+    count = build_near_list(codes_ref, list_s)
     core = codes_ref[6, 0]
 
     def get_source(k):
         if isinstance(k, int):
-            return no_source() if k == NDEV + NX else tiles_of(near_ref.at[core, k - NDEV])
-        return tiles_of_rows(all_ref.at[k])
+            return no_source() if k == NZ + NX else tiles_of(near_ref.at[core, k - NZ])
+        return tiles_of_rows(line_ref.at[k])
 
     def get_target(side):
         return tiles_of(near_ref.at[side, 0])
 
-    pair_body(list_ref, count_ref, get_source, get_target, force_ref, *scratch)
+    pair_body(list_s, *batches(count), None, NZ, get_source, get_target, force_ref, scratch)
+
+
+def first_kernel(codes_ref, all_ref, near_ref, more_ref, force_ref, list_ref, count_ref, *scratch):
+    first, count = build_list(codes_ref, list_ref)
+    whole, tail = batches(count)
+    count_ref[0, 0] = whole
+    count_ref[0, 1] = tail
+
+    def get_source(k):
+        return no_source() if isinstance(k, int) else tiles_of_rows(all_ref.at[k])
+
+    def get_target(side):
+        return tiles_of(near_ref.at[side, 0])
+
+    pair_body(
+        list_ref,
+        *batches(first),
+        first,
+        NDEV,
+        get_source,
+        get_target,
+        force_ref,
+        scratch,
+        more_ref,
+    )
 
 
 def second_kernel(
@@ -295,7 +360,17 @@
     def get_target(side):
         return position_ref[side, 0], near_ref[side, 0, 8:16], near_ref[side, 0, 16:24]
 
-    pair_body(list_ref, count_ref, get_source, get_target, force_ref, *scratch)
+    pair_body(
+        list_ref,
+        count_ref[0, 0],
+        count_ref[0, 1],
+        None,
+        NDEV,
+        get_source,
+        get_target,
+        force_ref,
+        scratch,
+    )
 
 
 def finish_kernel(codes_ref, stress_ref, parts_ref, near_ref, x_ref, vel_ref, out_ref):
@@ -375,7 +450,7 @@
     return jax.ShapeDtypeStruct(dims, dtype)
 
 
-def call(kernel, name, operands, outs, smem_in=0, smem_out=0, scratch=(), mib=4):
+def call(kernel, name, operands, outs, smem_in=0, smem_out=0, scratch=(), mib=4, cost=None):
     return pl.pallas_call(
         kernel,
         name=name,
@@ -384,6 +459,7 @@
         out_shape=outs,
         scratch_shapes=scratch,
         compiler_params=pltpu.CompilerParams(vmem_limit_bytes=mib << 20),
+        cost_estimate=cost,
     )(*operands)
 
 
@@ -413,8 +489,7 @@
         mib=56,
     )
     along_z = exchange(to_z, "z")
-    late, along_z = lax.optimization_barrier((raw, along_z))
-    group = [raw, pass_x(raw, 1), pass_x(raw, 2), pass_x(late, 3)]
+    group = [raw] + [pass_x(raw, shift) for shift in range(1, NX)]
     near = lax.all_gather(jnp.stack(group), "c", axis=0)
     chip = near[:, 0]
 
@@ -428,11 +503,23 @@
     where = jnp.where(first == 0, core, jnp.where(first == 1, y_index, x_index))
     zero = jnp.zeros((1, SEG), jnp.int32)
     known = jnp.concatenate([out, zero, zero, where, zero], axis=0)
+    nothing = jnp.zeros((NC, SEG), jnp.int32)
     pick = (lane == 2 * chip_index + side).astype(F32)
 
     everyone = exchange(
         jnp.broadcast_to(along_z.reshape(1, NZ * 5, 4, SEG), (NY, NZ * 5, 4, SEG)), "y"
     ).reshape(NDEV, 5, 4, SEG)
+    (near_force,) = call(
+        near_kernel,
+        "near_pairs",
+        (jnp.concatenate([nothing, known], axis=0), along_z, near),
+        [shape(NC, 8, SEG)],
+        smem_in=1,
+        scratch=[pltpu.SMEM((1, 128), jnp.int32)] + scratch_of(NZ),
+        mib=8,
+        cost=pl.CostEstimate(flops=1 << 30, bytes_accessed=1 << 24, transcendentals=1 << 20),
+    )
+    everyone, near_force = lax.optimization_barrier((everyone, near_force))
     lists = everyone[:, 0:2, 3].reshape(2 * NDEV, SEG)
     incoming = lax.dot_general(
         pick, lists, (((1,), (1,)), ((), ())), precision=lax.Precision.HIGHEST
@@ -444,7 +531,7 @@
     force, items, count = call(
         first_kernel,
         "first_pairs",
-        (codes, everyone, near),
+        (codes, everyone, near, near_force),
         [
             shape(NC, 8, SEG),
             shape(1, LIST, dtype=jnp.int32),
@@ -452,7 +539,7 @@
         ],
         smem_in=1,
         smem_out=2,
-        scratch=SCRATCH,
+        scratch=scratch_of(NDEV),
         mib=16,
     )
     def finish(force, position, peers, name):
@@ -464,8 +551,9 @@
             smem_in=2,
         )
 
-    near_vel, to_all = finish(force, near, (NDEV, 8), "finish")
-    vel_all = exchange(to_all, ("y", "z"))
+    near_vel, to_z = finish(force, near, (NZ, 8), "finish")
+    along_z = exchange(to_z, "z").reshape(1, NZ * 8, SEG)
+    vel_all = exchange(jnp.broadcast_to(along_z, (NY, NZ * 8, SEG)), "y").reshape(NDEV, 8, SEG)
 
     force, position = call(
         second_kernel,
@@ -473,7 +561,7 @@
         (codes, items, count, everyone, near, vel_all, near_vel),
         [shape(NC, 8, SEG), shape(NC, NX, 8, SEG)],
         smem_in=3,
-        scratch=SCRATCH,
+        scratch=scratch_of(NDEV),
         mib=16,
     )
     near_vel, to_all = finish(force, position, (NDEV, 1), "finish_last")

time: 132 us -> 129 us (0.977)
  blocking collectives: 70.3 us -> 75.6 us
  waiting for transfers between devices: 5.49 us -> 2.82 us
  starting transfers between devices: 31.9 us -> 29.4 us
  Pallas kernels: 21.4 us -> 19.1 us
    all_to_all x4 -> x5, blocking collectives: 63.3 us -> 69.5 us  [exchange(): return lax.all_to_all(value, axes, 0, 0, tiled=True)]
    ppermute x3, starting transfers between devices: 11.9 us -> 9.33 us  [pass_x(): return lax.ppermute(value, 'x', [(i, (i + shift) % NX) for i in range(NX)])]
    pallas_call x6 -> x7, Pallas kernels: 21.4 us -> 19.1 us  [call(): pl.pallas_call(kernel, name=name, in_specs=[SMEM] * smem_in + [VMEM] * (l...]
    all_to_all x2, waiting for transfers between devices: 4.72 us -> 2.81 us  [exchange(): return lax.all_to_all(value, axes, 0, 0, tiled=True)]
  transfers between devices with their start and end apart: 5 -> 5, of which waited for: 2 -> 1; matrix products, arithmetic and copies ran while one was open for 1% -> 1% of each run, Pallas kernels for 0% -> 2%
where the time goes in v8:
time: 129 us
  blocking collectives  75.6 us (59%)
  starting transfers between devices  29.4 us (23%)
  Pallas kernels  19.1 us (15%)
  waiting for transfers between devices  2.82 us (2%)
    all_to_all x5, blocking collectives, exchange(): return lax.all_to_all(value, axes, 0, 0, tiled=True)  69.5 us
    all_to_all x2, starting transfers between devices, exchange(): return lax.all_to_all(value, axes, 0, 0, tiled=True)  20.1 us
    pallas_call x7, Pallas kernels, call(): pl.pallas_call(kernel, name=name, in_specs=[SMEM] * smem_in + [VMEM] * (l...  19.1 us
    ppermute x3, starting transfers between devices, pass_x(): return lax.ppermute(value, 'x', [(i, (i + shift) % NX) for i in range(NX)])  9.33 us
    all_gather x1, blocking collectives, local(): near = lax.all_gather(jnp.stack(group), 'c', axis=0)  6.18 us
    all_to_all x2, waiting for transfers between devices, exchange(): return lax.all_to_all(value, axes, 0, 0, tiled=True)  2.81 us
  transfers between devices with their start and end apart: 5, of which 1 were waited for; matrix products, arithmetic and copies ran while one was open for 1% of the time, Pallas kernels for 2%

profile of v8, /device:TPU:1, one launch (start us, length us, event | category | flops | bytes accessed | tf_op | source)
XLA Modules:
  0.0 129.3 jit_solution(6585894732666108819)
XLA Ops:
  0.6 1.4 %pack.1 = (f32[24,128]{1,0:T(8,128)}, f32[16,5,4,128]{3,2,1,0:T(4,128)}) custom-call(f32[9,2,128]{2,1,0:T(2,128)} %bitcast.52, f32[2,128]{1,0:T(2,128)} %drag_ref.1, s32[1,128]{1,0:T(1,128)} %bitcast.53, s32[1,128]{1,0:T(1,128)} %bitcast.54), custom_call_target="tpu_custom_call" | custom-call | tf_op jit(solution)/shard_map/pack/pallas_call | solution.py:454
  2.1 15.9 %all-to-all-start = ((f32[16,5,4,128]{3,2,1,0:T(4,128)}), f32[16,5,4,128]{3,2,1,0:T(4,128)S(1)}, u32[]{:S(2)}, u32[]{:S(2)}) async-start(f32[16,5,4,128]{3,2,1,0:T(4,128)} %get-tuple-element.17), calls=%async_computation | async-start | bytes 327680 | tf_op jit(solution)/shard_map/all_to_all | solution.py:471
  17.9 4.4 %collective-permute-start.2 = (f32[24,128]{1,0:T(8,128)S(1)}, f32[24,128]{1,0:T(8,128)S(1)}, u32[]{:S(2)}, u32[]{:S(2)}) collective-permute-start(f32[24,128]{1,0:T(8,128)S(1)} %copy-done.1), channel_id=1, source_target_pairs={{0,3},{1,0},{2,1},{3,2},{4,7},{5,4},{6,5},{7,6},{8,11},{9,8},{10,9... | collective-permute-start | bytes 36872 | tf_op jit(solution)/shard_map/ppermute | solution.py:467
  22.3 2.4 %collective-permute-start.1 = (f32[24,128]{1,0:T(8,128)S(1)}, f32[24,128]{1,0:T(8,128)S(1)}, u32[]{:S(2)}, u32[]{:S(2)}) collective-permute-start(f32[24,128]{1,0:T(8,128)S(1)} %copy-done.1), channel_id=1, source_target_pairs={{0,2},{1,3},{2,0},{3,1},{4,6},{5,7},{6,4},{7,5},{8,10},{9,11},{10,... | collective-permute-start | bytes 36872 | tf_op jit(solution)/shard_map/ppermute | solution.py:467
  24.8 2.5 %collective-permute-start = (f32[24,128]{1,0:T(8,128)S(1)}, f32[24,128]{1,0:T(8,128)S(1)}, u32[]{:S(2)}, u32[]{:S(2)}) collective-permute-start(f32[24,128]{1,0:T(8,128)S(1)} %copy-done.1), channel_id=1, source_target_pairs={{0,1},{1,2},{2,3},{3,0},{4,5},{5,6},{6,7},{7,4},{8,9},{9,10},{10,1... | collective-permute-start | bytes 36872 | tf_op jit(solution)/shard_map/ppermute | solution.py:467
  27.3 2.8 %all-to-all-done.line_ref = f32[16,5,4,128]{3,2,1,0:T(4,128)S(1)} async-done(((f32[16,5,4,128]{3,2,1,0:T(4,128)}), f32[16,5,4,128]{3,2,1,0:T(4,128)S(1)}, u32[]{:S(2)}, u32[]{:S(2)}) %all-to-all-start) | async-done | bytes 163872 | tf_op jit(solution)/shard_map/all_to_all | solution.py:471
  30.2 0.9 broadcast_in_dim.44
  31.1 4.2 %all-to-all-start.1 = ((f32[4,80,4,128]{3,2,1,0:T(4,128)}), f32[4,80,4,128]{3,2,1,0:T(4,128)S(1)}, u32[]{:S(2)}, u32[]{:S(2)}) async-start(f32[4,80,4,128]{3,2,1,0:T(4,128)} %broadcast_in_dim.44), calls=%async_computation.1 | async-start | bytes 1310720 | tf_op jit(solution)/shard_map/all_to_all | solution.py:471
  35.3 6.2 %all-gather = f32[8,24,128]{2,1,0:T(8,128)S(1)} all-gather(f32[4,24,128]{2,1,0:T(8,128)S(1)} %pad_maximum_fusion), channel_id=2, replica_groups=mesh['y'=4,'z'=16,'c'=2,'x'=4] {'c'}, dimensions={0}, use_global_device_ids=true | all-gather | bytes 147456 | tf_op jit(solution)/shard_map/all_gather | solution.py:493
  41.6 2.5 %near_pairs.1.more_ref = f32[2,8,128]{2,1,0:T(8,128)S(1)} custom-call(s32[8,128]{1,0:T(8,128)S(1)} %concatenate.12.codes_ref, f32[16,5,4,128]{3,2,1,0:T(4,128)S(1)} %all-to-all-done.line_ref, f32[2,4,24,128]{3,2,1,0:T(8,128)S(1)} %bitcast.36), custom_call_target="tpu_custom_call" | custom-call | flops 1073741824 | bytes 16777216 | tf_op jit(solution)/shard_map/near_pairs/pallas_call | solution.py:454
  44.2 0.2 convolution_convert_fusion
  44.3 0.1 slice.23
  44.4 0.1 compare_select_fusion
  44.5 0.1 concatenate.14.codes_ref
  44.6 6.2 %first_pairs.1 = (f32[2,8,128]{2,1,0:T(8,128)S(1)}, s32[1,320]{1,0:T(1,128)S(1)}, s32[1,2]{1,0:T(1,128)S(1)}) custom-call(s32[8,128]{1,0:T(8,128)S(1)} %concatenate.14.codes_ref, f32[64,5,4,128]{3,2,1,0:T(4,128)S(1)} %bitcast.33, f32[2,4,24,128]{3,2,1,0:T(8,128)S(1)} %bitcast.37, f32[2,8,128]{2,1,0:T(8,128)S(1)} %near_pairs.1.more_ref), custom_call_target="tpu_custom_call" | custom-call | tf_op jit(solution)/shard_map/first_pairs/pallas_call | solution.py:454
  50.8 13.3 %all_to_all.35.parts_ref = f32[8,2,8,128]{3,2,1,0:T(8,128)S(1)} all-to-all(f32[8,2,8,128]{3,2,1,0:T(8,128)S(1)} %broadcast_in_dim.49), channel_id=1, replica_groups=mesh['y'=4,'z'=16,'c'=2,'x'=4] {'x','c'}, dimensions={0} | all-to-all | bytes 131072 | tf_op jit(solution)/shard_map/all_to_all | solution.py:471
  64.1 0.7 finish.1
  64.8 18.6 %all_to_all.36 = f32[16,8,128]{2,1,0:T(8,128)S(1)} all-to-all(f32[16,8,128]{2,1,0:T(8,128)S(1)} %get-tuple-element.24), channel_id=1, replica_groups=mesh['y'=4,'z'=16,'c'=2,'x'=4] {'z'}, dimensions={0} | all-to-all | bytes 131072 | tf_op jit(solution)/shard_map/all_to_all | solution.py:471
  83.4 8.3 %all_to_all.37 = f32[4,128,128]{2,1,0:T(8,128)S(1)} all-to-all(f32[4,128,128]{2,1,0:T(8,128)S(1)} %broadcast_in_dim.51), channel_id=1, replica_groups=mesh['y'=4,'z'=16,'c'=2,'x'=4] {'y'}, dimensions={0} | all-to-all | bytes 524288 | tf_op jit(solution)/shard_map/all_to_all | solution.py:471
  91.7 6.3 %second_pairs.1 = (f32[2,8,128]{2,1,0:T(8,128)S(1)}, f32[2,4,8,128]{3,2,1,0:T(8,128)S(1)}) custom-call(s32[8,128]{1,0:T(8,128)S(1)} %concatenate.14.codes_ref, s32[1,320]{1,0:T(1,128)S(1)} %get-tuple-element.21.list_ref, s32[1,2]{1,0:T(1,128)S(1)} %get-tuple-element.22.count_ref, f32[64,5,4,128]{3,2,1,0:T(4,128)S(1)} %bitcast.34, ...), custom_call_target="tpu_custom_call" | custom-call | tf_op jit(solution)/shard_map/second_pairs/pallas_call | solution.py:454
  98.0 11.4 %all_to_all.38.parts_ref = f32[8,2,8,128]{3,2,1,0:T(8,128)S(1)} all-to-all(f32[8,2,8,128]{3,2,1,0:T(8,128)S(1)} %broadcast_in_dim.52), channel_id=1, replica_groups=mesh['y'=4,'z'=16,'c'=2,'x'=4] {'x','c'}, dimensions={0} | all-to-all | bytes 131072 | tf_op jit(solution)/shard_map/all_to_all | solution.py:471
  109.4 0.8 finish_last.1
  110.1 17.9 %all_to_all.39.top_ref = f32[64,1,128]{2,1,0:T(1,128)S(1)} all-to-all(f32[64,1,128]{2,1,0:T(1,128)S(1)} %get-tuple-element.28), channel_id=1, replica_groups=mesh['y'=4,'z'=16,'c'=2,'x'=4] {'y','z'}, dimensions={0} | all-to-all | bytes 65536 | tf_op jit(solution)/shard_map/all_to_all | solution.py:471
  128.0 1.3 %last.1 = (f32[3,2,128]{2,1,0:T(2,128)}, f32[3,2,128]{2,1,0:T(2,128)}) custom-call(s32[8,128]{1,0:T(8,128)S(1)} %concatenate.14.codes_ref, f32[64,1,128]{2,1,0:T(1,128)S(1)} %all_to_all.39.top_ref, f32[2,4,8,128]{3,2,1,0:T(8,128)S(1)} %get-tuple-element.27.x_ref, f32[2,4,8,128]{3,2,1,0:T(8,128)S(1)} %get-tuple-element.29.vel_ref), custom_call_target="tpu_custom_call" | custom-call | tf_op jit(solution)/shard_map/last/pallas_call | solution.py:454
  (23 shorter events, 0.3 us)
Async XLA Ops:
  2.0 15.9 %copy-start.1 = (f32[24,128]{1,0:T(8,128)S(1)}, f32[24,128]{1,0:T(8,128)}, u32[]{:S(2)}) copy-start(f32[24,128]{1,0:T(8,128)} %get-tuple-element.18) | copy-start | bytes 36868
  2.1 28.1 %all-to-all-start = ((f32[16,5,4,128]{3,2,1,0:T(4,128)}), f32[16,5,4,128]{3,2,1,0:T(4,128)S(1)}, u32[]{:S(2)}, u32[]{:S(2)}) async-start(f32[16,5,4,128]{3,2,1,0:T(4,128)} %get-tuple-element.17), calls=%async_computation | async-start | bytes 327680 | tf_op jit(solution)/shard_map/all_to_all | solution.py:471
  17.9 17.3 %collective-permute-start.2 = (f32[24,128]{1,0:T(8,128)S(1)}, f32[24,128]{1,0:T(8,128)S(1)}, u32[]{:S(2)}, u32[]{:S(2)}) collective-permute-start(f32[24,128]{1,0:T(8,128)S(1)} %copy-done.1), channel_id=1, source_target_pairs={{0,3},{1,0},{2,1},{3,2},{4,7},{5,4},{6,5},{7,6},{8,11},{9,8},{10,9... | collective-permute-start | bytes 36872 | tf_op jit(solution)/shard_map/ppermute | solution.py:467
  22.3 12.9 %collective-permute-start.1 = (f32[24,128]{1,0:T(8,128)S(1)}, f32[24,128]{1,0:T(8,128)S(1)}, u32[]{:S(2)}, u32[]{:S(2)}) collective-permute-start(f32[24,128]{1,0:T(8,128)S(1)} %copy-done.1), channel_id=1, source_target_pairs={{0,2},{1,3},{2,0},{3,1},{4,6},{5,7},{6,4},{7,5},{8,10},{9,11},{10,... | collective-permute-start | bytes 36872 | tf_op jit(solution)/shard_map/ppermute | solution.py:467
  24.8 10.5 %collective-permute-start = (f32[24,128]{1,0:T(8,128)S(1)}, f32[24,128]{1,0:T(8,128)S(1)}, u32[]{:S(2)}, u32[]{:S(2)}) collective-permute-start(f32[24,128]{1,0:T(8,128)S(1)} %copy-done.1), channel_id=1, source_target_pairs={{0,1},{1,2},{2,3},{3,0},{4,5},{5,6},{6,7},{7,4},{8,9},{9,10},{10,1... | collective-permute-start | bytes 36872 | tf_op jit(solution)/shard_map/ppermute | solution.py:467
  31.1 13.0 %all-to-all-start.1 = ((f32[4,80,4,128]{3,2,1,0:T(4,128)}), f32[4,80,4,128]{3,2,1,0:T(4,128)S(1)}, u32[]{:S(2)}, u32[]{:S(2)}) async-start(f32[4,80,4,128]{3,2,1,0:T(4,128)} %broadcast_in_dim.44), calls=%async_computation.1 | async-start | bytes 1310720 | tf_op jit(solution)/shard_map/all_to_all | solution.py:471
  50.8 13.3 %copy-start = (f32[3,3]{1,0:T(4,128)S(1)}, f32[3,3]{1,0:T(4,128)}, u32[]{:S(2)}) copy-start(f32[3,3]{1,0:T(4,128)} %stress_ref.3) | copy-start | bytes 112

commit v9 on v8

--- a/solution.py
+++ b/solution.py
@@ -139,7 +139,8 @@
 def build_list(codes_ref, list_ref):
     core, y_index = codes_ref[6, 0], codes_ref[6, 1]
 
-    def add_in(k, count):
+    def add_in(at, count):
+        k = lax.bitwise_and(at + NZ * (y_index + 1), NDEV - 1)
         for side in range(NC):
             code = codes_ref[side, 2 * k]
             count = add_code(list_ref, count, code, code >= 0)
@@ -152,22 +153,26 @@
             count = add_code(list_ref, count, code, code >= 0)
         return count
 
-    count = lax.fori_loop(0, NDEV, add_in, jnp.int32(0), unroll=8)
-    first = lax.fori_loop(0, NDEV - NZ, add_out, count, unroll=8)
-    count = lax.fori_loop(NDEV - NZ, NDEV, add_out, first, unroll=8)
+    far = NDEV - NZ
+    count = lax.fori_loop(0, far, add_in, jnp.int32(0), unroll=8)
+    first = lax.fori_loop(0, far, add_out, count, unroll=8)
+    count = lax.fori_loop(far, NDEV, add_in, first, unroll=8)
+    count = lax.fori_loop(far, NDEV, add_out, count, unroll=8)
     return first, add_group(list_ref, count, core, NDEV)
 
 
-def build_near_list(codes_ref, list_ref):
-    core, y_index = codes_ref[6, 0], codes_ref[6, 1]
-
-    def add_out(z, count):
+def build_near_list(codes_ref, into_ref, list_ref):
+    core, y_index, chip = codes_ref[6, 0], codes_ref[6, 1], codes_ref[6, 3]
+
+    def add_both(z, count):
         for side in range(NC):
+            code = into_ref[z, 2 * chip + side]
+            count = add_code(list_ref, count, code, code >= 0)
             code = codes_ref[NC + side, 2 * (NZ * y_index + z) + core]
             count = add_code(list_ref, count, code - 2 * NZ * y_index, code >= 0)
         return count
 
-    count = lax.fori_loop(0, NZ, add_out, jnp.int32(0), unroll=8)
+    count = lax.fori_loop(0, NZ, add_both, jnp.int32(0), unroll=8)
     return add_group(list_ref, count, core, NZ)
 
 
@@ -286,8 +291,8 @@
     return zero, zero, zero
 
 
-def near_kernel(codes_ref, line_ref, near_ref, force_ref, list_s, *scratch):
-    count = build_near_list(codes_ref, list_s)
+def near_kernel(codes_ref, into_ref, line_ref, near_ref, force_ref, list_s, *scratch):
+    count = build_near_list(codes_ref, into_ref, list_s)
     core = codes_ref[6, 0]
 
     def get_source(k):
@@ -501,20 +506,29 @@
     out = jnp.where(sent >= 0, even + other + 256 * (2 * side + sent), -1)
     first = lane[0:1]
     where = jnp.where(first == 0, core, jnp.where(first == 1, y_index, x_index))
+    where = jnp.where(first == 3, chip_index, where)
     zero = jnp.zeros((1, SEG), jnp.int32)
     known = jnp.concatenate([out, zero, zero, where, zero], axis=0)
     nothing = jnp.zeros((NC, SEG), jnp.int32)
     pick = (lane == 2 * chip_index + side).astype(F32)
 
+    near_sent = along_z[:, 0, 3].astype(jnp.int32)
+    near_part = along_z[:, 1, 3].astype(jnp.int32)
+    z_row = lax.broadcasted_iota(jnp.int32, (NZ, SEG), 0)
+    target = lax.bitwise_and(lax.broadcasted_iota(jnp.int32, (NZ, SEG), 1), 1)
+    near_into = jnp.where(
+        near_sent >= 0, 2 * z_row + near_sent + 256 * (2 * target + near_part), -1
+    )
+    along_z, near_into = lax.optimization_barrier((along_z, near_into))
     everyone = exchange(
         jnp.broadcast_to(along_z.reshape(1, NZ * 5, 4, SEG), (NY, NZ * 5, 4, SEG)), "y"
     ).reshape(NDEV, 5, 4, SEG)
     (near_force,) = call(
         near_kernel,
         "near_pairs",
-        (jnp.concatenate([nothing, known], axis=0), along_z, near),
+        (jnp.concatenate([nothing, known], axis=0), near_into, along_z, near),
         [shape(NC, 8, SEG)],
-        smem_in=1,
+        smem_in=2,
         scratch=[pltpu.SMEM((1, 128), jnp.int32)] + scratch_of(NZ),
         mib=8,
         cost=pl.CostEstimate(flops=1 << 30, bytes_accessed=1 << 24, transcendentals=1 << 20),

time: 129 us -> 128 us (level)
  blocking collectives: 75.6 us -> 72.3 us
  Pallas kernels: 19.1 us -> 20.7 us
    all_to_all x5, blocking collectives: 69.5 us -> 66.2 us  [exchange(): return lax.all_to_all(value, axes, 0, 0, tiled=True)]
    pallas_call x7, Pallas kernels: 19.1 us -> 20.7 us  [call(): pl.pallas_call(kernel, name=name, in_specs=[SMEM] * smem_in + [VMEM] * (l...]
  transfers between devices with their start and end apart: 5 -> 5, of which waited for: 1 -> 1; matrix products, arithmetic and copies ran while one was open for 1% -> 1% of each run, Pallas kernels for 2% -> 3%
where the time goes in v9:
time: 128 us
  blocking collectives  72.3 us (56%)
  starting transfers between devices  29.4 us (23%)
  Pallas kernels  20.7 us (16%)
  waiting for transfers between devices  2.8 us (2%)
    all_to_all x5, blocking collectives, exchange(): return lax.all_to_all(value, axes, 0, 0, tiled=True)  66.2 us
    pallas_call x7, Pallas kernels, call(): pl.pallas_call(kernel, name=name, in_specs=[SMEM] * smem_in + [VMEM] * (l...  20.7 us
    all_to_all x2, starting transfers between devices, exchange(): return lax.all_to_all(value, axes, 0, 0, tiled=True)  20.1 us
    ppermute x3, starting transfers between devices, pass_x(): return lax.ppermute(value, 'x', [(i, (i + shift) % NX) for i in range(NX)])  9.33 us
    all_gather x1, blocking collectives, local(): near = lax.all_gather(jnp.stack(group), 'c', axis=0)  6.18 us
    all_to_all x2, waiting for transfers between devices, exchange(): return lax.all_to_all(value, axes, 0, 0, tiled=True)  2.79 us
  transfers between devices with their start and end apart: 5, of which 1 were waited for; matrix products, arithmetic and copies ran while one was open for 1% of the time, Pallas kernels for 3%

profile of v9, /device:TPU:1, one launch (start us, length us, event | category | flops | bytes accessed | tf_op | source)
XLA Modules:
  0.0 127.7 jit_solution(6354965348616781106)
XLA Ops:
  0.6 1.4 %pack.1 = (f32[24,128]{1,0:T(8,128)}, f32[16,5,4,128]{3,2,1,0:T(4,128)}) custom-call(f32[9,2,128]{2,1,0:T(2,128)} %bitcast.65, f32[2,128]{1,0:T(2,128)} %drag_ref.1, s32[1,128]{1,0:T(1,128)} %bitcast.66, s32[1,128]{1,0:T(1,128)} %bitcast.67), custom_call_target="tpu_custom_call" | custom-call | tf_op jit(solution)/shard_map/pack/pallas_call | solution.py:459
  2.0 15.9 %all-to-all-start = ((f32[16,5,4,128]{3,2,1,0:T(4,128)}), f32[16,5,4,128]{3,2,1,0:T(4,128)S(1)}, u32[]{:S(2)}, u32[]{:S(2)}) async-start(f32[16,5,4,128]{3,2,1,0:T(4,128)} %get-tuple-element.19), calls=%async_computation | async-start | bytes 327680 | tf_op jit(solution)/shard_map/all_to_all | solution.py:476
  17.9 4.4 %collective-permute-start.2 = (f32[24,128]{1,0:T(8,128)S(1)}, f32[24,128]{1,0:T(8,128)S(1)}, u32[]{:S(2)}, u32[]{:S(2)}) collective-permute-start(f32[24,128]{1,0:T(8,128)S(1)} %copy-done.1), channel_id=1, source_target_pairs={{0,3},{1,0},{2,1},{3,2},{4,7},{5,4},{6,5},{7,6},{8,11},{9,8},{10,9... | collective-permute-start | bytes 36872 | tf_op jit(solution)/shard_map/ppermute | solution.py:472
  22.3 2.4 %collective-permute-start.1 = (f32[24,128]{1,0:T(8,128)S(1)}, f32[24,128]{1,0:T(8,128)S(1)}, u32[]{:S(2)}, u32[]{:S(2)}) collective-permute-start(f32[24,128]{1,0:T(8,128)S(1)} %copy-done.1), channel_id=1, source_target_pairs={{0,2},{1,3},{2,0},{3,1},{4,6},{5,7},{6,4},{7,5},{8,10},{9,11},{10,... | collective-permute-start | bytes 36872 | tf_op jit(solution)/shard_map/ppermute | solution.py:472
  24.8 2.5 %collective-permute-start = (f32[24,128]{1,0:T(8,128)S(1)}, f32[24,128]{1,0:T(8,128)S(1)}, u32[]{:S(2)}, u32[]{:S(2)}) collective-permute-start(f32[24,128]{1,0:T(8,128)S(1)} %copy-done.1), channel_id=1, source_target_pairs={{0,1},{1,2},{2,3},{3,0},{4,5},{5,6},{6,7},{7,4},{8,9},{9,10},{10,1... | collective-permute-start | bytes 36872 | tf_op jit(solution)/shard_map/ppermute | solution.py:472
  27.4 2.8 %all-to-all-done.line_ref = f32[16,5,4,128]{3,2,1,0:T(4,128)S(1)} async-done(((f32[16,5,4,128]{3,2,1,0:T(4,128)}), f32[16,5,4,128]{3,2,1,0:T(4,128)S(1)}, u32[]{:S(2)}, u32[]{:S(2)}) %all-to-all-start) | async-done | bytes 163872 | tf_op jit(solution)/shard_map/all_to_all | solution.py:476
  30.2 0.1 fusion.1.into_ref
  30.3 0.9 broadcast_in_dim.52
  31.2 4.2 %all-to-all-start.1 = ((f32[4,80,4,128]{3,2,1,0:T(4,128)}), f32[4,80,4,128]{3,2,1,0:T(4,128)S(1)}, u32[]{:S(2)}, u32[]{:S(2)}) async-start(f32[4,80,4,128]{3,2,1,0:T(4,128)} %broadcast_in_dim.52), calls=%async_computation.1 | async-start | bytes 1310720 | tf_op jit(solution)/shard_map/all_to_all | solution.py:476
  35.4 6.2 %all-gather = f32[8,24,128]{2,1,0:T(8,128)S(1)} all-gather(f32[4,24,128]{2,1,0:T(8,128)S(1)} %pad_maximum_fusion), channel_id=2, replica_groups=mesh['y'=4,'z'=16,'c'=2,'x'=4] {'c'}, dimensions={0}, use_global_device_ids=true | all-gather | bytes 147456 | tf_op jit(solution)/shard_map/all_gather | solution.py:498
  41.7 3.4 %near_pairs.1.more_ref = f32[2,8,128]{2,1,0:T(8,128)S(1)} custom-call(s32[8,128]{1,0:T(8,128)S(1)} %concatenate.12.codes_ref, s32[16,128]{1,0:T(8,128)S(1)} %fusion.1.into_ref, f32[16,5,4,128]{3,2,1,0:T(4,128)S(1)} %all-to-all-done.line_ref, f32[2,4,24,128]{3,2,1,0:T(8,128)S(1)} %bitcast.47), custom_call_target="tpu_custom_call" | custom-call | flops 1073741824 | bytes 16777216 | tf_op jit(solution)/shard_map/near_pairs/pallas_call | solution.py:459
  45.2 0.2 convolution_convert_fusion
  45.5 0.1 compare_select_fusion
  45.5 0.1 concatenate.14.codes_ref
  45.6 6.2 %first_pairs.1 = (f32[2,8,128]{2,1,0:T(8,128)S(1)}, s32[1,320]{1,0:T(1,128)S(1)}, s32[1,2]{1,0:T(1,128)S(1)}) custom-call(s32[8,128]{1,0:T(8,128)S(1)} %concatenate.14.codes_ref, f32[64,5,4,128]{3,2,1,0:T(4,128)S(1)} %bitcast.44, f32[2,4,24,128]{3,2,1,0:T(8,128)S(1)} %bitcast.48, f32[2,8,128]{2,1,0:T(8,128)S(1)} %near_pairs.1.more_ref), custom_call_target="tpu_custom_call" | custom-call | tf_op jit(solution)/shard_map/first_pairs/pallas_call | solution.py:459
  51.9 12.6 %all_to_all.35.parts_ref = f32[8,2,8,128]{3,2,1,0:T(8,128)S(1)} all-to-all(f32[8,2,8,128]{3,2,1,0:T(8,128)S(1)} %broadcast_in_dim.58), channel_id=1, replica_groups=mesh['y'=4,'z'=16,'c'=2,'x'=4] {'x','c'}, dimensions={0} | all-to-all | bytes 131072 | tf_op jit(solution)/shard_map/all_to_all | solution.py:476
  64.5 0.7 finish.1
  65.2 17.8 %all_to_all.36 = f32[16,8,128]{2,1,0:T(8,128)S(1)} all-to-all(f32[16,8,128]{2,1,0:T(8,128)S(1)} %get-tuple-element.28), channel_id=1, replica_groups=mesh['y'=4,'z'=16,'c'=2,'x'=4] {'z'}, dimensions={0} | all-to-all | bytes 131072 | tf_op jit(solution)/shard_map/all_to_all | solution.py:476
  83.0 7.9 %all_to_all.37 = f32[4,128,128]{2,1,0:T(8,128)S(1)} all-to-all(f32[4,128,128]{2,1,0:T(8,128)S(1)} %broadcast_in_dim.60), channel_id=1, replica_groups=mesh['y'=4,'z'=16,'c'=2,'x'=4] {'y'}, dimensions={0} | all-to-all | bytes 524288 | tf_op jit(solution)/shard_map/all_to_all | solution.py:476
  91.0 6.8 %second_pairs.1 = (f32[2,8,128]{2,1,0:T(8,128)S(1)}, f32[2,4,8,128]{3,2,1,0:T(8,128)S(1)}) custom-call(s32[8,128]{1,0:T(8,128)S(1)} %concatenate.14.codes_ref, s32[1,320]{1,0:T(1,128)S(1)} %get-tuple-element.25.list_ref, s32[1,2]{1,0:T(1,128)S(1)} %get-tuple-element.26.count_ref, f32[64,5,4,128]{3,2,1,0:T(4,128)S(1)} %bitcast.45, ...), custom_call_target="tpu_custom_call" | custom-call | tf_op jit(solution)/shard_map/second_pairs/pallas_call | solution.py:459
  97.8 10.6 %all_to_all.38.parts_ref = f32[8,2,8,128]{3,2,1,0:T(8,128)S(1)} all-to-all(f32[8,2,8,128]{3,2,1,0:T(8,128)S(1)} %broadcast_in_dim.61), channel_id=1, replica_groups=mesh['y'=4,'z'=16,'c'=2,'x'=4] {'x','c'}, dimensions={0} | all-to-all | bytes 131072 | tf_op jit(solution)/shard_map/all_to_all | solution.py:476
  108.4 0.8 finish_last.1
  109.1 17.3 %all_to_all.39.top_ref = f32[64,1,128]{2,1,0:T(1,128)S(1)} all-to-all(f32[64,1,128]{2,1,0:T(1,128)S(1)} %get-tuple-element.32), channel_id=1, replica_groups=mesh['y'=4,'z'=16,'c'=2,'x'=4] {'y','z'}, dimensions={0} | all-to-all | bytes 65536 | tf_op jit(solution)/shard_map/all_to_all | solution.py:476
  126.4 1.3 %last.1 = (f32[3,2,128]{2,1,0:T(2,128)}, f32[3,2,128]{2,1,0:T(2,128)}) custom-call(s32[8,128]{1,0:T(8,128)S(1)} %concatenate.14.codes_ref, f32[64,1,128]{2,1,0:T(1,128)S(1)} %all_to_all.39.top_ref, f32[2,4,8,128]{3,2,1,0:T(8,128)S(1)} %get-tuple-element.31.x_ref, f32[2,4,8,128]{3,2,1,0:T(8,128)S(1)} %get-tuple-element.33.vel_ref), custom_call_target="tpu_custom_call" | custom-call | tf_op jit(solution)/shard_map/last/pallas_call | solution.py:459
  (27 shorter events, 0.4 us)
Async XLA Ops:
  2.0 15.9 %copy-start.1 = (f32[24,128]{1,0:T(8,128)S(1)}, f32[24,128]{1,0:T(8,128)}, u32[]{:S(2)}) copy-start(f32[24,128]{1,0:T(8,128)} %get-tuple-element.21) | copy-start | bytes 36868
  2.0 28.1 %all-to-all-start = ((f32[16,5,4,128]{3,2,1,0:T(4,128)}), f32[16,5,4,128]{3,2,1,0:T(4,128)S(1)}, u32[]{:S(2)}, u32[]{:S(2)}) async-start(f32[16,5,4,128]{3,2,1,0:T(4,128)} %get-tuple-element.19), calls=%async_computation | async-start | bytes 327680 | tf_op jit(solution)/shard_map/all_to_all | solution.py:476
  17.9 17.4 %collective-permute-start.2 = (f32[24,128]{1,0:T(8,128)S(1)}, f32[24,128]{1,0:T(8,128)S(1)}, u32[]{:S(2)}, u32[]{:S(2)}) collective-permute-start(f32[24,128]{1,0:T(8,128)S(1)} %copy-done.1), channel_id=1, source_target_pairs={{0,3},{1,0},{2,1},{3,2},{4,7},{5,4},{6,5},{7,6},{8,11},{9,8},{10,9... | collective-permute-start | bytes 36872 | tf_op jit(solution)/shard_map/ppermute | solution.py:472
  22.3 13.0 %collective-permute-start.1 = (f32[24,128]{1,0:T(8,128)S(1)}, f32[24,128]{1,0:T(8,128)S(1)}, u32[]{:S(2)}, u32[]{:S(2)}) collective-permute-start(f32[24,128]{1,0:T(8,128)S(1)} %copy-done.1), channel_id=1, source_target_pairs={{0,2},{1,3},{2,0},{3,1},{4,6},{5,7},{6,4},{7,5},{8,10},{9,11},{10,... | collective-permute-start | bytes 36872 | tf_op jit(solution)/shard_map/ppermute | solution.py:472
  24.8 10.6 %collective-permute-start = (f32[24,128]{1,0:T(8,128)S(1)}, f32[24,128]{1,0:T(8,128)S(1)}, u32[]{:S(2)}, u32[]{:S(2)}) collective-permute-start(f32[24,128]{1,0:T(8,128)S(1)} %copy-done.1), channel_id=1, source_target_pairs={{0,1},{1,2},{2,3},{3,0},{4,5},{5,6},{6,7},{7,4},{8,9},{9,10},{10,1... | collective-permute-start | bytes 36872 | tf_op jit(solution)/shard_map/ppermute | solution.py:472
  31.2 14.0 %all-to-all-start.1 = ((f32[4,80,4,128]{3,2,1,0:T(4,128)}), f32[4,80,4,128]{3,2,1,0:T(4,128)S(1)}, u32[]{:S(2)}, u32[]{:S(2)}) async-start(f32[4,80,4,128]{3,2,1,0:T(4,128)} %broadcast_in_dim.52), calls=%async_computation.1 | async-start | bytes 1310720 | tf_op jit(solution)/shard_map/all_to_all | solution.py:476
  51.9 12.6 %copy-start = (f32[3,3]{1,0:T(4,128)S(1)}, f32[3,3]{1,0:T(4,128)}, u32[]{:S(2)}) copy-start(f32[3,3]{1,0:T(4,128)} %stress_ref.3) | copy-start | bytes 112

commit v10 on v9

--- a/solution.py
+++ b/solution.py
@@ -177,7 +177,7 @@
 
 
 def pair_body(
-    list_ref, whole, tail, limit, lines, get_source, get_target, force_ref, scratch, more=None
+    list_ref, whole, tail, limit, lines, get_source, get_target, force_ref, scratch, more=None, far=None
 ):
     source_s, moment_s, target_s = scratch
 
@@ -187,11 +187,11 @@
         moment_s[2 * k] = jnp.concatenate(first, axis=0).astype(BF16)
         moment_s[2 * k + 1] = jnp.concatenate(second, axis=0).astype(BF16)
 
-    def prepare_loop(k, carry):
-        prepare(k)
+    def prepare_loop(at, carry):
+        prepare(at if far is None else lax.bitwise_and(at + far, NDEV - 1))
         return carry
 
-    lax.fori_loop(0, lines, prepare_loop, 0, unroll=4)
+    lax.fori_loop(0, lines if far is None else NDEV - NZ, prepare_loop, 0, unroll=4)
     for k in range(lines, lines + NX + 1):
         prepare(k)
 
@@ -328,6 +328,7 @@
         force_ref,
         scratch,
         more_ref,
+        NZ * (codes_ref[6, 1] + 1),
     )
 
 
@@ -435,6 +436,16 @@
             out_ref[peer, at] = rows
 
 
+def fan_kernel(in_ref, out_ref, sems):
+    copies = [
+        pltpu.make_async_copy(in_ref, out_ref.at[peer], sems.at[peer]) for peer in range(NY)
+    ]
+    for copy in copies:
+        copy.start()
+    for copy in copies:
+        copy.wait()
+
+
 def last_kernel(codes_ref, top_ref, x_ref, vel_ref, pos_out, vel_out):
     core = codes_ref[6, 0]
     top = jnp.max(jnp.max(top_ref[...], axis=0), axis=1, keepdims=True)
@@ -520,9 +531,16 @@
         near_sent >= 0, 2 * z_row + near_sent + 256 * (2 * target + near_part), -1
     )
     along_z, near_into = lax.optimization_barrier((along_z, near_into))
-    everyone = exchange(
-        jnp.broadcast_to(along_z.reshape(1, NZ * 5, 4, SEG), (NY, NZ * 5, 4, SEG)), "y"
-    ).reshape(NDEV, 5, 4, SEG)
+    to_y = pl.pallas_call(
+        fan_kernel,
+        name="fan",
+        in_specs=[VMEM],
+        out_specs=pl.BlockSpec(memory_space=pl.ANY),
+        out_shape=shape(NY, NZ * 5, 4, SEG),
+        scratch_shapes=[pltpu.SemaphoreType.DMA((NY,))],
+        compiler_params=pltpu.CompilerParams(vmem_limit_bytes=4 << 20),
+    )(along_z.reshape(NZ * 5, 4, SEG))
+    everyone = exchange(to_y, "y").reshape(NDEV, 5, 4, SEG)
     (near_force,) = call(
         near_kernel,
         "near_pairs",

time: 128 us -> 129 us (level)
  blocking collectives: 72.3 us -> 73.8 us
    all_to_all x5, blocking collectives: 66.2 us -> 67.6 us  [exchange(): return lax.all_to_all(value, axes, 0, 0, tiled=True)]
  transfers between devices with their start and end apart: 5 -> 5, of which waited for: 1 -> 1; matrix products, arithmetic and copies ran while one was open for 1% -> 0% of each run, Pallas kernels for 3% -> 3%
where the time goes in v10:
time: 129 us; the launch traced here: 128 us
  blocking collectives  73.8 us (57%)
  starting transfers between devices  29.4 us (23%)
  Pallas kernels  20.8 us (16%)
  waiting for transfers between devices  2.8 us (2%)
    all_to_all x5, blocking collectives, exchange(): return lax.all_to_all(value, axes, 0, 0, tiled=True)  67.6 us
    all_to_all x2, starting transfers between devices, exchange(): return lax.all_to_all(value, axes, 0, 0, tiled=True)  20.1 us
    pallas_call x7, Pallas kernels, call(): pl.pallas_call(kernel, name=name, in_specs=[SMEM] * smem_in + [VMEM] * (l...  20 us
    ppermute x3, starting transfers between devices, pass_x(): return lax.ppermute(value, 'x', [(i, (i + shift) % NX) for i in range(NX)])  9.33 us
    all_gather x1, blocking collectives, local(): near = lax.all_gather(jnp.stack(group), 'c', axis=0)  6.18 us
    all_to_all x2, waiting for transfers between devices, exchange(): return lax.all_to_all(value, axes, 0, 0, tiled=True)  2.79 us
  transfers between devices with their start and end apart: 5, of which 1 were waited for; matrix products, arithmetic and copies ran while one was open for 0% of the time, Pallas kernels for 3%

profile of v10, /device:TPU:1, one launch (start us, length us, event | category | flops | bytes accessed | tf_op | source)
XLA Modules:
  0.0 128.5 jit_solution(9959123967008827903)
XLA Ops:
  0.6 1.4 %pack.1 = (f32[24,128]{1,0:T(8,128)}, f32[16,5,4,128]{3,2,1,0:T(4,128)}) custom-call(f32[9,2,128]{2,1,0:T(2,128)} %bitcast.65, f32[2,128]{1,0:T(2,128)} %drag_ref.1, s32[1,128]{1,0:T(1,128)} %bitcast.66, s32[1,128]{1,0:T(1,128)} %bitcast.67), custom_call_target="tpu_custom_call" | custom-call | tf_op jit(solution)/shard_map/pack/pallas_call | solution.py:470
  2.0 15.9 %all-to-all-start = ((f32[16,5,4,128]{3,2,1,0:T(4,128)}), f32[16,5,4,128]{3,2,1,0:T(4,128)S(1)}, u32[]{:S(2)}, u32[]{:S(2)}) async-start(f32[16,5,4,128]{3,2,1,0:T(4,128)} %get-tuple-element.19), calls=%async_computation | async-start | bytes 327680 | tf_op jit(solution)/shard_map/all_to_all | solution.py:487
  17.9 4.4 %collective-permute-start.2 = (f32[24,128]{1,0:T(8,128)S(1)}, f32[24,128]{1,0:T(8,128)S(1)}, u32[]{:S(2)}, u32[]{:S(2)}) collective-permute-start(f32[24,128]{1,0:T(8,128)S(1)} %copy-done.1), channel_id=1, source_target_pairs={{0,3},{1,0},{2,1},{3,2},{4,7},{5,4},{6,5},{7,6},{8,11},{9,8},{10,9... | collective-permute-start | bytes 36872 | tf_op jit(solution)/shard_map/ppermute | solution.py:483
  22.3 2.4 %collective-permute-start.1 = (f32[24,128]{1,0:T(8,128)S(1)}, f32[24,128]{1,0:T(8,128)S(1)}, u32[]{:S(2)}, u32[]{:S(2)}) collective-permute-start(f32[24,128]{1,0:T(8,128)S(1)} %copy-done.1), channel_id=1, source_target_pairs={{0,2},{1,3},{2,0},{3,1},{4,6},{5,7},{6,4},{7,5},{8,10},{9,11},{10,... | collective-permute-start | bytes 36872 | tf_op jit(solution)/shard_map/ppermute | solution.py:483
  24.8 2.5 %collective-permute-start = (f32[24,128]{1,0:T(8,128)S(1)}, f32[24,128]{1,0:T(8,128)S(1)}, u32[]{:S(2)}, u32[]{:S(2)}) collective-permute-start(f32[24,128]{1,0:T(8,128)S(1)} %copy-done.1), channel_id=1, source_target_pairs={{0,1},{1,2},{2,3},{3,0},{4,5},{5,6},{6,7},{7,4},{8,9},{9,10},{10,1... | collective-permute-start | bytes 36872 | tf_op jit(solution)/shard_map/ppermute | solution.py:483
  27.4 2.8 %all-to-all-done.line_ref = f32[16,5,4,128]{3,2,1,0:T(4,128)S(1)} async-done(((f32[16,5,4,128]{3,2,1,0:T(4,128)}), f32[16,5,4,128]{3,2,1,0:T(4,128)S(1)}, u32[]{:S(2)}, u32[]{:S(2)}) %all-to-all-start) | async-done | bytes 163872 | tf_op jit(solution)/shard_map/all_to_all | solution.py:487
  30.2 0.1 fusion.1.into_ref
  30.3 0.9 fan.1
  31.1 4.2 %all-to-all-start.1 = ((f32[4,80,4,128]{3,2,1,0:T(4,128)}), f32[4,80,4,128]{3,2,1,0:T(4,128)S(1)}, u32[]{:S(2)}, u32[]{:S(2)}) async-start(f32[4,80,4,128]{3,2,1,0:T(4,128)} %fan.1), calls=%async_computation.1 | async-start | bytes 1310720 | tf_op jit(solution)/shard_map/all_to_all | solution.py:487
  35.4 6.2 %all-gather = f32[8,24,128]{2,1,0:T(8,128)S(1)} all-gather(f32[4,24,128]{2,1,0:T(8,128)S(1)} %pad_maximum_fusion), channel_id=2, replica_groups=mesh['y'=4,'z'=16,'c'=2,'x'=4] {'c'}, dimensions={0}, use_global_device_ids=true | all-gather | bytes 147456 | tf_op jit(solution)/shard_map/all_gather | solution.py:509
  41.7 3.4 %near_pairs.1.more_ref = f32[2,8,128]{2,1,0:T(8,128)S(1)} custom-call(s32[8,128]{1,0:T(8,128)S(1)} %concatenate.12.codes_ref, s32[16,128]{1,0:T(8,128)S(1)} %fusion.1.into_ref, f32[16,5,4,128]{3,2,1,0:T(4,128)S(1)} %all-to-all-done.line_ref, f32[2,4,24,128]{3,2,1,0:T(8,128)S(1)} %bitcast.47), custom_call_target="tpu_custom_call" | custom-call | flops 1073741824 | bytes 16777216 | tf_op jit(solution)/shard_map/near_pairs/pallas_call | solution.py:470
  45.2 0.2 convolution_convert_fusion
  45.4 0.1 compare_select_fusion
  45.5 0.1 concatenate.14.codes_ref
  45.6 6.1 %first_pairs.1 = (f32[2,8,128]{2,1,0:T(8,128)S(1)}, s32[1,320]{1,0:T(1,128)S(1)}, s32[1,2]{1,0:T(1,128)S(1)}) custom-call(s32[8,128]{1,0:T(8,128)S(1)} %concatenate.14.codes_ref, f32[64,5,4,128]{3,2,1,0:T(4,128)S(1)} %bitcast.44, f32[2,4,24,128]{3,2,1,0:T(8,128)S(1)} %bitcast.48, f32[2,8,128]{2,1,0:T(8,128)S(1)} %near_pairs.1.more_ref), custom_call_target="tpu_custom_call" | custom-call | tf_op jit(solution)/shard_map/first_pairs/pallas_call | solution.py:470
  51.7 11.9 %all_to_all.35.parts_ref = f32[8,2,8,128]{3,2,1,0:T(8,128)S(1)} all-to-all(f32[8,2,8,128]{3,2,1,0:T(8,128)S(1)} %broadcast_in_dim.49), channel_id=1, replica_groups=mesh['y'=4,'z'=16,'c'=2,'x'=4] {'x','c'}, dimensions={0} | all-to-all | bytes 131072 | tf_op jit(solution)/shard_map/all_to_all | solution.py:487
  63.6 0.7 finish.1
  64.3 18.5 %all_to_all.36 = f32[16,8,128]{2,1,0:T(8,128)S(1)} all-to-all(f32[16,8,128]{2,1,0:T(8,128)S(1)} %get-tuple-element.28), channel_id=1, replica_groups=mesh['y'=4,'z'=16,'c'=2,'x'=4] {'z'}, dimensions={0} | all-to-all | bytes 131072 | tf_op jit(solution)/shard_map/all_to_all | solution.py:487
  82.9 7.9 %all_to_all.37 = f32[4,128,128]{2,1,0:T(8,128)S(1)} all-to-all(f32[4,128,128]{2,1,0:T(8,128)S(1)} %broadcast_in_dim.51), channel_id=1, replica_groups=mesh['y'=4,'z'=16,'c'=2,'x'=4] {'y'}, dimensions={0} | all-to-all | bytes 524288 | tf_op jit(solution)/shard_map/all_to_all | solution.py:487
  90.8 6.3 %second_pairs.1 = (f32[2,8,128]{2,1,0:T(8,128)S(1)}, f32[2,4,8,128]{3,2,1,0:T(8,128)S(1)}) custom-call(s32[8,128]{1,0:T(8,128)S(1)} %concatenate.14.codes_ref, s32[1,320]{1,0:T(1,128)S(1)} %get-tuple-element.25.list_ref, s32[1,2]{1,0:T(1,128)S(1)} %get-tuple-element.26.count_ref, f32[64,5,4,128]{3,2,1,0:T(4,128)S(1)} %bitcast.45, ...), custom_call_target="tpu_custom_call" | custom-call | tf_op jit(solution)/shard_map/second_pairs/pallas_call | solution.py:470
  97.1 11.3 %all_to_all.38.parts_ref = f32[8,2,8,128]{3,2,1,0:T(8,128)S(1)} all-to-all(f32[8,2,8,128]{3,2,1,0:T(8,128)S(1)} %broadcast_in_dim.52), channel_id=1, replica_groups=mesh['y'=4,'z'=16,'c'=2,'x'=4] {'x','c'}, dimensions={0} | all-to-all | bytes 131072 | tf_op jit(solution)/shard_map/all_to_all | solution.py:487
  108.3 0.8 finish_last.1
  109.1 18.1 %all_to_all.39.top_ref = f32[64,1,128]{2,1,0:T(1,128)S(1)} all-to-all(f32[64,1,128]{2,1,0:T(1,128)S(1)} %get-tuple-element.32), channel_id=1, replica_groups=mesh['y'=4,'z'=16,'c'=2,'x'=4] {'y','z'}, dimensions={0} | all-to-all | bytes 65536 | tf_op jit(solution)/shard_map/all_to_all | solution.py:487
  127.2 1.3 %last.1 = (f32[3,2,128]{2,1,0:T(2,128)}, f32[3,2,128]{2,1,0:T(2,128)}) custom-call(s32[8,128]{1,0:T(8,128)S(1)} %concatenate.14.codes_ref, f32[64,1,128]{2,1,0:T(1,128)S(1)} %all_to_all.39.top_ref, f32[2,4,8,128]{3,2,1,0:T(8,128)S(1)} %get-tuple-element.31.x_ref, f32[2,4,8,128]{3,2,1,0:T(8,128)S(1)} %get-tuple-element.33.vel_ref), custom_call_target="tpu_custom_call" | custom-call | tf_op jit(solution)/shard_map/last/pallas_call | solution.py:470
  (27 shorter events, 0.4 us)
Async XLA Ops:
  2.0 15.9 %copy-start.1 = (f32[24,128]{1,0:T(8,128)S(1)}, f32[24,128]{1,0:T(8,128)}, u32[]{:S(2)}) copy-start(f32[24,128]{1,0:T(8,128)} %get-tuple-element.21) | copy-start | bytes 36868
  2.0 28.1 %all-to-all-start = ((f32[16,5,4,128]{3,2,1,0:T(4,128)}), f32[16,5,4,128]{3,2,1,0:T(4,128)S(1)}, u32[]{:S(2)}, u32[]{:S(2)}) async-start(f32[16,5,4,128]{3,2,1,0:T(4,128)} %get-tuple-element.19), calls=%async_computation | async-start | bytes 327680 | tf_op jit(solution)/shard_map/all_to_all | solution.py:487
  17.9 17.4 %collective-permute-start.2 = (f32[24,128]{1,0:T(8,128)S(1)}, f32[24,128]{1,0:T(8,128)S(1)}, u32[]{:S(2)}, u32[]{:S(2)}) collective-permute-start(f32[24,128]{1,0:T(8,128)S(1)} %copy-done.1), channel_id=1, source_target_pairs={{0,3},{1,0},{2,1},{3,2},{4,7},{5,4},{6,5},{7,6},{8,11},{9,8},{10,9... | collective-permute-start | bytes 36872 | tf_op jit(solution)/shard_map/ppermute | solution.py:483
  22.3 13.0 %collective-permute-start.1 = (f32[24,128]{1,0:T(8,128)S(1)}, f32[24,128]{1,0:T(8,128)S(1)}, u32[]{:S(2)}, u32[]{:S(2)}) collective-permute-start(f32[24,128]{1,0:T(8,128)S(1)} %copy-done.1), channel_id=1, source_target_pairs={{0,2},{1,3},{2,0},{3,1},{4,6},{5,7},{6,4},{7,5},{8,10},{9,11},{10,... | collective-permute-start | bytes 36872 | tf_op jit(solution)/shard_map/ppermute | solution.py:483
  24.8 10.6 %collective-permute-start = (f32[24,128]{1,0:T(8,128)S(1)}, f32[24,128]{1,0:T(8,128)S(1)}, u32[]{:S(2)}, u32[]{:S(2)}) collective-permute-start(f32[24,128]{1,0:T(8,128)S(1)} %copy-done.1), channel_id=1, source_target_pairs={{0,1},{1,2},{2,3},{3,0},{4,5},{5,6},{6,7},{7,4},{8,9},{9,10},{10,1... | collective-permute-start | bytes 36872 | tf_op jit(solution)/shard_map/ppermute | solution.py:483
  31.1 14.0 %all-to-all-start.1 = ((f32[4,80,4,128]{3,2,1,0:T(4,128)}), f32[4,80,4,128]{3,2,1,0:T(4,128)S(1)}, u32[]{:S(2)}, u32[]{:S(2)}) async-start(f32[4,80,4,128]{3,2,1,0:T(4,128)} %fan.1), calls=%async_computation.1 | async-start | bytes 1310720 | tf_op jit(solution)/shard_map/all_to_all | solution.py:487
  51.7 11.9 %copy-start = (f32[3,3]{1,0:T(4,128)S(1)}, f32[3,3]{1,0:T(4,128)}, u32[]{:S(2)}) copy-start(f32[3,3]{1,0:T(4,128)} %stress_ref.3) | copy-start | bytes 112
